TPU v7x, 32 devices: a whole 2x2x4 slice. The times are simulated.
32 devices in a mesh: expert: 8 (over z, x), hidden: 4 (over y, core).
Axes of the slice: x: 2, y: 2, z: 4, core: 2. Of those that a mesh axis runs over, the one named last changes fastest.
Arguments:
- tokens: bfloat16 [16384, 768], P(('expert', 'hidden')), may hold values from -6 to 6
- doc_lengths: int32 [8, 3], P('expert'), may hold values from 1 to 1024, 2048 in all within a row
- expert_ids: int32 [16384, 2], P(('expert', 'hidden')), may hold values from 0 to 7, all different within a row; in each aligned block of 512 rows (0 to 511, 512 to 1023, ...) at most 160 rows name the same one
- gain_one: float32 [768], replicated, may hold values from 0.5 to 1.5
- shift_one: float32 [768], replicated, may hold values from -1.25 to 1.25
- w_query: bfloat16 [768, 768], replicated, may hold values from -0.21875 to 0.21875
- w_key: bfloat16 [768, 768], replicated, may hold values from -0.21875 to 0.21875
- w_value: bfloat16 [768, 768], replicated, may hold values from -0.21875 to 0.21875
- w_out: bfloat16 [768, 768], replicated, may hold values from -3.5 to 3.5
- gain_two: float32 [768], replicated, may hold values from 0.5 to 1.5
- shift_two: float32 [768], replicated, may hold values from -1.25 to 1.25
- w_router: bfloat16 [768, 8], replicated, may hold values from -0.21875 to 0.21875
- w_up: bfloat16 [8, 768, 3072], P('expert', None, 'hidden'), may hold values from -0.21875 to 0.21875
- w_down: bfloat16 [8, 3072, 768], P('expert', 'hidden'), may hold values from -0.109375 to 0.109375
- out_grad: bfloat16 [16384, 768], P(('expert', 'hidden')), may hold values from -6 to 6
Outputs:
- output: bfloat16 [16384, 768], P(('expert', 'hidden'))
- input_grad: bfloat16 [16384, 768], P(('expert', 'hidden'))
- gain_one_grad: float32 [768], replicated
- shift_one_grad: float32 [768], replicated
- w_query_grad: float32 [768, 768], replicated
- w_key_grad: float32 [768, 768], replicated
- w_value_grad: float32 [768, 768], replicated
- w_out_grad: float32 [768, 768], replicated
- gain_two_grad: float32 [768], replicated
- shift_two_grad: float32 [768], replicated
- w_router_grad: float32 [768, 8], replicated
- w_up_grad: float32 [8, 768, 3072], P('expert', None, 'hidden')
- w_down_grad: float32 [8, 3072, 768], P('expert', 'hidden')
- load: float32 [8], replicated
Inputs may be any that keep to these rules, and one draw needn't show every extreme that they name: `doc_lengths`: the lengths of a group's documents, in order; they sum to 2048 and the longest in every group is 1024. `expert_ids`: each token names 2 different experts; among the 512 tokens of one device no expert is named more than 160 times, and in every draw some expert is named exactly 160 times by one device.
All inputs are finite; a program needn't handle non-finite values.
Results may differ from a plain program's by a relative error of at most 0.019.
Values may be sent and summed in bfloat16 or wider, within the bound.
A program may use at most 192 MiB of HBM per device.

v0:
```python
from functools import partial

import jax
import jax.numpy as jnp
from jax import lax
from jax.sharding import PartitionSpec as P

HEADS = 12
HEAD_DIM = 64


EPSILON = 1e-05
SCALE = 0.125
MASKED = -1e30
EXACT = lax.Precision.HIGHEST


def product(left, right):
    return jnp.dot(left, right, preferred_element_type=jnp.float32)


def contract(left, right, left_axis, right_axis):
    return lax.dot_general(
        left, right, (((left_axis,), (right_axis,)), ((), ())), preferred_element_type=jnp.float32
    )


def norm_parts(values):
    row_mean = jnp.mean(values, axis=-1, keepdims=True)
    centred = values - row_mean
    inverse = lax.rsqrt(jnp.mean(centred * centred, axis=-1, keepdims=True) + EPSILON)
    return (centred * inverse, inverse)


def norm_back(grad_out, normed, inverse, gain):
    grad_normed = grad_out * gain
    first_mean = jnp.mean(grad_normed, axis=-1, keepdims=True)
    second_mean = jnp.mean(grad_normed * normed, axis=-1, keepdims=True)
    return inverse * (grad_normed - first_mean - normed * second_mean)


def gelu_back(pre_act, grad_hidden):
    unused, pull = jax.vjp(partial(jax.nn.gelu, approximate=True), pre_act)
    return pull(grad_hidden)[0]


def split_heads(array):
    return array.reshape(array.shape[0], HEADS, HEAD_DIM).transpose(1, 0, 2)


def join_heads(array):
    return array.transpose(1, 0, 2).reshape(array.shape[1], HEADS * HEAD_DIM)


def shards(
    tokens,
    doc_lengths,
    expert_ids,
    gain_one,
    shift_one,
    w_query,
    w_key,
    w_value,
    w_out,
    gain_two,
    shift_two,
    w_router,
    w_up,
    w_down,
    out_grad,
):
    row_count = tokens.shape[0]
    model_width = tokens.shape[1]
    top_count = expert_ids.shape[1]
    experts = lax.axis_size("expert") * w_up.shape[0]
    capacity = max(2, row_count * top_count * 5 // (4 * experts))
    input_float = tokens.astype(jnp.float32)
    normed_one, inverse_one = norm_parts(input_float)
    h_one = (normed_one * gain_one + shift_one).astype(jnp.bfloat16)
    queries = product(h_one, w_query).astype(jnp.bfloat16)
    key_proj = product(h_one, w_key).astype(jnp.bfloat16)
    value_proj = product(h_one, w_value).astype(jnp.bfloat16)
    all_keys, all_values = (
        lax.all_gather(key_proj, "hidden", axis=0, tiled=True),
        lax.all_gather(value_proj, "hidden", axis=0, tiled=True),
    )
    key_count = all_keys.shape[0]
    doc_ends = jnp.cumsum(doc_lengths[0])
    query_pos = lax.axis_index("hidden") * row_count + jnp.arange(row_count, dtype=jnp.int32)
    key_pos = jnp.arange(key_count, dtype=jnp.int32)
    query_doc = jnp.sum((query_pos[:, None] >= doc_ends[None, :]).astype(jnp.int32), axis=1)
    key_doc = jnp.sum((key_pos[:, None] >= doc_ends[None, :]).astype(jnp.int32), axis=1)
    allowed = (query_doc[:, None] == key_doc[None, :]) & (key_pos[None, :] <= query_pos[:, None])

    def head_forward(pieces):
        q_head, k_head, v_head = pieces
        scores = jnp.where(allowed, contract(q_head, k_head, 1, 1) * SCALE, MASKED)
        top_score = jnp.max(scores, axis=1, keepdims=True)
        expd = jnp.exp(scores - top_score)
        row_total = jnp.sum(expd, axis=1, keepdims=True)
        weights = (expd / row_total).astype(jnp.bfloat16)
        return (product(weights, v_head), (top_score + jnp.log(row_total))[:, 0])

    mixture, log_total = lax.map(
        head_forward, (split_heads(queries), split_heads(all_keys), split_heads(all_values))
    )
    attended = join_heads(mixture).astype(jnp.bfloat16)
    residual = input_float + product(attended, w_out)
    normed_two, inverse_two = norm_parts(residual)
    h_two = (normed_two * gain_two + shift_two).astype(jnp.bfloat16)
    h_two_float = h_two.astype(jnp.float32)
    router_float = w_router.astype(jnp.float32)
    logits = jnp.dot(h_two_float, router_float, precision=EXACT)
    choose_table = (
        expert_ids[:, :, None] == jnp.arange(experts, dtype=jnp.int32)[None, None, :]
    ).astype(jnp.float32)
    chosen = jnp.sum(choose_table * logits[:, None, :], axis=2)
    gate_weights = jax.nn.softmax(chosen, axis=1)
    flat_ids = expert_ids.reshape(-1)
    onehot = choose_table.reshape(-1, experts).astype(jnp.int32)
    before = jnp.cumsum(onehot, axis=0) - onehot
    slot_index = jnp.sum(before * onehot, axis=1)
    counts = jnp.sum(choose_table, axis=(0, 1))
    outgoing = (
        jnp.zeros((experts, capacity, model_width), jnp.bfloat16)
        .at[flat_ids, slot_index]
        .set(jnp.repeat(h_two, top_count, axis=0))
    )
    slot_rows = lax.all_to_all(outgoing, "expert", split_axis=0, concat_axis=0, tiled=True).reshape(
        -1, model_width
    )
    rows_all = lax.all_gather(slot_rows, "hidden", axis=0, tiled=True)
    pre_act = product(rows_all, w_up[0])
    hidden_act = jax.nn.gelu(pre_act, approximate=True).astype(jnp.bfloat16)
    partial_sum = product(hidden_act, w_down[0])
    produced = lax.psum_scatter(
        partial_sum.astype(jnp.bfloat16), "hidden", scatter_dimension=0, tiled=True
    )
    returned = lax.all_to_all(
        produced.reshape(-1, capacity, model_width),
        "expert",
        split_axis=0,
        concat_axis=0,
        tiled=True,
    )
    returned_rows = (
        returned[flat_ids, slot_index]
        .reshape(row_count, top_count, model_width)
        .astype(jnp.float32)
    )
    expert_mix = jnp.sum(gate_weights[:, :, None] * returned_rows, axis=1)
    output = (residual + expert_mix).astype(jnp.bfloat16)
    grad_output = out_grad.astype(jnp.float32)
    grad_returned = (gate_weights[:, :, None] * grad_output[:, None, :]).astype(jnp.bfloat16)
    grad_gates = jnp.sum(returned_rows * grad_output[:, None, :], axis=2)
    grad_chosen = gate_weights * (
        grad_gates - jnp.sum(gate_weights * grad_gates, axis=1, keepdims=True)
    )
    grad_logits = jnp.sum(grad_chosen[:, :, None] * choose_table, axis=1)
    router_grad = jnp.dot(h_two_float.T, grad_logits, precision=EXACT)
    grad_h_two = jnp.dot(grad_logits, router_float.T, precision=EXACT)
    grad_outgoing = (
        jnp.zeros((experts, capacity, model_width), jnp.bfloat16)
        .at[flat_ids, slot_index]
        .set(grad_returned.reshape(-1, model_width))
    )
    grad_slots = lax.all_to_all(
        grad_outgoing, "expert", split_axis=0, concat_axis=0, tiled=True
    ).reshape(-1, model_width)
    trainable = (lax.axis_index("expert") >= experts // 2).astype(jnp.float32)
    grad_all = lax.all_gather(grad_slots, "hidden", axis=0, tiled=True)
    grad_hidden = contract(grad_all, w_down[0], 1, 1)
    down_grad = contract(hidden_act, grad_all, 0, 0)
    grad_pre = gelu_back(pre_act, grad_hidden).astype(jnp.bfloat16)
    up_grad = contract(rows_all, grad_pre, 0, 0)
    partial_in = contract(grad_pre, w_up[0], 1, 1)
    grad_in = lax.psum_scatter(
        partial_in.astype(jnp.bfloat16), "hidden", scatter_dimension=0, tiled=True
    )
    up_grad = up_grad[None] * trainable
    down_grad = down_grad[None] * trainable
    grad_back = lax.all_to_all(
        grad_in.reshape(-1, capacity, model_width),
        "expert",
        split_axis=0,
        concat_axis=0,
        tiled=True,
    )
    grad_h_two = grad_h_two + jnp.sum(
        grad_back[flat_ids, slot_index]
        .reshape(row_count, top_count, model_width)
        .astype(jnp.float32),
        axis=1,
    )
    gain_two_grad = jnp.sum(grad_h_two * normed_two, axis=0)
    shift_two_grad = jnp.sum(grad_h_two, axis=0)
    grad_residual = grad_output + norm_back(grad_h_two, normed_two, inverse_two, gain_two)
    grad_branch = grad_residual.astype(jnp.bfloat16)
    out_proj_grad = contract(attended, grad_branch, 0, 0)
    grad_attended = contract(grad_branch, w_out, 1, 1).astype(jnp.bfloat16)
    back_keys, back_values = (all_keys, all_values)

    def head_backward(pieces):
        q_head, k_head, v_head, g_head, head_total = pieces
        scores = jnp.where(allowed, contract(q_head, k_head, 1, 1) * SCALE, MASKED)
        weights = jnp.exp(scores - head_total[:, None])
        grad_weights = contract(g_head, v_head, 1, 1)
        grad_scores = (
            weights * (grad_weights - jnp.sum(weights * grad_weights, axis=1, keepdims=True))
        ).astype(jnp.bfloat16)
        grad_query = product(grad_scores, k_head) * SCALE
        grad_key = contract(grad_scores, q_head, 0, 0) * SCALE
        grad_value = contract(weights.astype(jnp.bfloat16), g_head, 0, 0)
        return (grad_query, grad_key, grad_value)

    grad_query, grad_key, grad_value = lax.map(
        head_backward,
        (
            split_heads(queries),
            split_heads(back_keys),
            split_heads(back_values),
            split_heads(grad_attended),
            log_total,
        ),
    )
    grad_key, grad_value = (
        lax.psum_scatter(
            join_heads(grad_key).astype(jnp.bfloat16), "hidden", scatter_dimension=0, tiled=True
        ).astype(jnp.float32),
        lax.psum_scatter(
            join_heads(grad_value).astype(jnp.bfloat16), "hidden", scatter_dimension=0, tiled=True
        ).astype(jnp.float32),
    )
    grad_query = join_heads(grad_query).astype(jnp.bfloat16)
    grad_key = grad_key.astype(jnp.bfloat16)
    grad_value = grad_value.astype(jnp.bfloat16)
    query_grad = contract(h_one, grad_query, 0, 0)
    key_grad = contract(h_one, grad_key, 0, 0)
    value_grad = contract(h_one, grad_value, 0, 0)
    grad_h_one = (
        contract(grad_query, w_query, 1, 1)
        + contract(grad_key, w_key, 1, 1)
        + contract(grad_value, w_value, 1, 1)
    )
    gain_one_grad = jnp.sum(grad_h_one * normed_one, axis=0)
    shift_one_grad = jnp.sum(grad_h_one, axis=0)
    input_grad = (grad_residual + norm_back(grad_h_one, normed_one, inverse_one, gain_one)).astype(
        jnp.bfloat16
    )
    totals = lax.psum(
        (
            gain_one_grad,
            shift_one_grad,
            query_grad,
            key_grad,
            value_grad,
            out_proj_grad,
            gain_two_grad,
            shift_two_grad,
            router_grad,
            counts,
        ),
        ("expert", "hidden"),
    )
    total_tokens = row_count * lax.axis_size("expert") * lax.axis_size("hidden")
    load = totals[9] * experts / (total_tokens * top_count)
    return (
        output,
        input_grad,
        totals[0],
        totals[1],
        totals[2],
        totals[3],
        totals[4],
        totals[5],
        totals[6],
        totals[7],
        totals[8],
        up_grad,
        down_grad,
        load,
    )


def solution(mesh):
    in_specs = (
        P(("expert", "hidden"), None),
        P("expert", None),
        P(("expert", "hidden"), None),
        P(),
        P(),
        P(),
        P(),
        P(),
        P(),
        P(),
        P(),
        P(),
        P("expert", None, "hidden"),
        P("expert", "hidden", None),
        P(("expert", "hidden"), None),
    )
    out_specs = (
        P(("expert", "hidden"), None),
        P(("expert", "hidden"), None),
        P(),
        P(),
        P(),
        P(),
        P(),
        P(),
        P(),
        P(),
        P(),
        P("expert", None, "hidden"),
        P("expert", "hidden", None),
        P(),
    )
    return jax.shard_map(shards, mesh=mesh, in_specs=in_specs, out_specs=out_specs, check_vma=False)
```

profile of v0, /device:TPU:17, one launch (start us, length us, event | category | flops | bytes accessed | tf_op | source)
XLA Modules:
  0.0 1051.0 jit_solution(8360045255467511472)
XLA Ops:
  10.2 3.5 convolution_convert_fusion.4
  31.9 12.0 %all-gather.5.cloned.1.call-done = bf16[2048,768]{1,0:T(8,128)(2,1)} async-done(((bf16[512,768]{1,0:T(8,128)(2,1)}), bf16[2048,768]{1,0:T(8,128)(2,1)}) %all-gather.5.cloned.1.call-update) | async-done | bytes 3145744 | tf_op jit(solution)/shard_map/all_gather | solution.py:84
  43.9 4.8 copy.68
  48.7 6.7 copy.71
  55.4 19.3 %all-gather.7.cloned.1.call-done = bf16[2048,768]{1,0:T(8,128)(2,1)} async-done(((bf16[512,768]{1,0:T(8,128)(2,1)}), bf16[2048,768]{1,0:T(8,128)(2,1)}) %all-gather.7.cloned.1.call-update) | async-done | bytes 3145744 | tf_op jit(solution)/shard_map/all_gather | solution.py:85
  74.6 4.7 copy.69
  79.3 6.5 copy.72
  86.8 85.5 %while.28 = (s32[]{:T(128)}, bf16[12,512,64]{1,2,0:T(8,128)(2,1)}, f32[12,512]{1,0:T(8,128)}, bf16[12,512,64]{2,1,0:T(8,128)(2,1)S(1)}, bf16[12,2048,64]{2,1,0:T...) while((s32[]{:T(128)}, bf16[12,512,64]{1,2,0:T(8,128)(2,1)}, ...), condition=%wide.region_8.9_spmd.clone, body=%wide.region_5.8_spmd.clone.sunk | while | flops 279969280 | bytes 13928569 | solution.py:104
  89.8 2.7 fusion.149
  97.0 2.7 fusion.149
  104.1 2.7 fusion.149
  111.2 2.7 fusion.149
  118.3 2.7 fusion.149
  125.5 2.7 fusion.149
  139.7 2.7 fusion.149
  154.0 2.7 fusion.149
  168.2 2.7 fusion.149
  172.3 3.0 fusion.95
  179.7 7.4 scatter_custom_fusion
  187.1 49.4 %all_to_all.20 = bf16[8,160,768]{2,1,0:T(8,128)(2,1)} all-to-all(bf16[8,160,768]{2,1,0:T(8,128)(2,1)} %bitcast.191), channel_id=1, replica_groups=mesh['expert'=8,'hidden'=4] {'expert'}, dimensions={0} | all-to-all | bytes 3932160 | tf_op jit(solution)/shard_map/all_to_all | solution.py:129
  240.1 5.4 mul.265
  246.3 7.2 scatter_custom_fusion.1
  253.5 48.3 %all_to_all.21 = bf16[8,160,768]{2,1,0:T(8,128)(2,1)} all-to-all(bf16[8,160,768]{2,1,0:T(8,128)(2,1)S(1)} %bitcast.190), channel_id=1, replica_groups=mesh['expert'=8,'hidden'=4] {'expert'}, dimensions={0} | all-to-all | bytes 3932160 | tf_op jit(solution)/shard_map/all_to_all | solution.py:167
  302.3 13.1 %fusion.72 = f32[5120,768]{1,0:T(8,128)} fusion(bf16[5120,768]{1,0:T(8,128)(2,1)} %all-gather.9.cloned.1.call-done, bf16[1,768,768]{2,1,0:T(8,128)(2,1)S(1)} %copy-done), kind=kOutput, calls=%fused_computation.115 | convolution fusion | flops 6039797760 | bytes 24772608 | tf_op jit(solution)/shard_map/dot_general | solution.py:19
  315.5 42.4 %all-gather.11.cloned.1.call-done = bf16[5120,768]{1,0:T(8,128)(2,1)} async-done(((bf16[1280,768]{1,0:T(8,128)(2,1)}), bf16[5120,768]{1,0:T(8,128)(2,1)}) %all-gather.11.cloned.1.call-update) | async-done | bytes 7864336 | tf_op jit(solution)/shard_map/all_gather | solution.py:171
  357.9 19.0 %fusion.50 = bf16[5120,768]{1,0:T(8,128)(2,1)S(1)} fusion(f32[5120,768]{1,0:T(8,128)} %fusion.72, bf16[5120,768]{1,0:T(8,128)(2,1)} %all-gather.11.cloned.1.call-done, bf16[1,768,768]{2,1,0:T(8,128)(2,1)S(1)} %copy-done.40), kind=kOutput, calls=%fused_computation.67 | convolution fusion | flops 6118440960 | bytes 32636928 | tf_op jit(solution)/shard_map/dot_general | solution.py:23
  376.9 3.1 copy-done.48
  380.0 8.7 convolution_convert_fusion
  388.8 14.8 %convolution_convert_fusion.1 = bf16[5120,768]{1,0:T(8,128)(2,1)} fusion(bf16[1,768,768]{2,1,0:T(8,128)(2,1)S(1)} %copy-done.40, f32[5120,768]{1,0:T(8,128)} %fusion.72), kind=kOutput, calls=%fused_computation.70 | convolution fusion | flops 6079119360 | bytes 24772608 | tf_op jit(solution)/shard_map/dot_general | solution.py:19
  403.6 53.8 %reduce-scatter.7.cloned.1.call-done = bf16[1280,768]{1,0:T(8,128)(2,1)} async-done(((bf16[5120,768]{1,0:T(8,128)(2,1)}), bf16[1280,768]{1,0:T(8,128)(2,1)}) %reduce-scatter.7.cloned.1.call-update) | async-done | bytes 1966096 | tf_op jit(solution)/shard_map/reduce_scatter | solution.py:177
  457.5 5.5 all-to-all-start.3
  462.9 66.1 %reduce-scatter.5.cloned.1.call-done = bf16[1280,768]{1,0:T(8,128)(2,1)} async-done(((bf16[5120,768]{1,0:T(8,128)(2,1)}), bf16[1280,768]{1,0:T(8,128)(2,1)}) %reduce-scatter.5.cloned.1.call-update) | async-done | bytes 1966096 | tf_op jit(solution)/shard_map/reduce_scatter | solution.py:136
  529.0 5.6 all-to-all-start.1
  535.9 14.1 %gather_fusion.1 = bf16[1024,768]{1,0:T(8,128)(2,1)} fusion(bf16[8,160,768]{2,1,0:T(8,128)(2,1)S(1)} %all-to-all-done.3, s32[1024]{0:T(1024)S(1)} %bitcast.184), kind=kCustom, calls=%fused_computation.1 | custom fusion | bytes 3153920 | tf_op jit(solution)/shard_map/gather | solution.py:190
  550.0 4.9 reshape.365
  554.9 21.3 %all-to-all-done.1 = bf16[8,160,768]{2,1,0:T(8,128)(2,1)} async-done(((bf16[8,160,768]{2,1,0:T(8,128)(2,1)}), bf16[8,160,768]{2,1,0:T(8,128)(2,1)}, u32[]{:S(2)}, u32[]{:S(2)}) %all-to-all-start.1) | async-done | bytes 1966112 | tf_op jit(solution)/shard_map/all_to_all | solution.py:139
  576.1 19.8 %gather_fusion = bf16[1024,768]{1,0:T(8,128)(2,1)} fusion(bf16[8,160,768]{2,1,0:T(8,128)(2,1)} %all-to-all-done.1, s32[1024]{0:T(1024)S(1)} %bitcast.185), kind=kCustom, calls=%fused_computation | custom fusion | bytes 3153920 | tf_op jit(solution)/shard_map/gather | solution.py:147
  595.9 3.5 reshape.364
  599.4 9.7 multiply_reduce_fusion.1
  610.4 5.7 reduce_sum.241
  620.8 132.8 %while.29 = (s32[]{:T(128)}, bf16[12,512,64]{1,2,0:T(8,128)(2,1)S(1)}, bf16[12,2048,64]{1,2,0:T(8,128)(2,1)}, bf16[12,2048,64]{1,2,0:T(8,128)(2,1)}, bf16[12,512...) while((s32[]{:T(128)}, ...), condition=%wide.region_30.31_spmd.clone, body=%wide.region_28.30_spmd.clone.sunk | while | flops 683834880 | bytes 34630792 | solution.py:216
  623.3 2.9 multiply_reduce_fusion.11
  634.4 2.9 multiply_reduce_fusion.11
  645.4 3.0 multiply_reduce_fusion.11
  656.5 3.0 multiply_reduce_fusion.11
  667.6 3.0 multiply_reduce_fusion.11
  678.6 3.0 multiply_reduce_fusion.11
  689.7 2.9 multiply_reduce_fusion.11
  700.8 3.0 multiply_reduce_fusion.11
  711.9 2.9 multiply_reduce_fusion.11
  722.9 2.9 multiply_reduce_fusion.11
  734.0 2.9 multiply_reduce_fusion.11
  745.0 3.0 multiply_reduce_fusion.11
  755.0 3.7 fusion.89
  760.9 32.9 %reduce-scatter.9.cloned.1.call-done = bf16[512,768]{0,1:T(8,128)(2,1)} async-done(((bf16[2048,768]{0,1:T(8,128)(2,1)}), bf16[512,768]{0,1:T(8,128)(2,1)}) %reduce-scatter.9.cloned.1.call-update) | async-done | bytes 786448 | tf_op jit(solution)/shard_map/reduce_scatter | solution.py:227
  793.8 3.6 fusion.87
  797.4 37.1 %reduce-scatter.11.cloned.1.call-done = bf16[512,768]{0,1:T(8,128)(2,1)} async-done(((bf16[2048,768]{0,1:T(8,128)(2,1)}), bf16[512,768]{0,1:T(8,128)(2,1)}) %reduce-scatter.11.cloned.1.call-update) | async-done | bytes 786448 | tf_op jit(solution)/shard_map/reduce_scatter | solution.py:230
  834.5 3.6 fusion.85
  838.1 12.2 %multiply_bitcast_fusion.1 = f32[1,768,768]{2,1,0:T(8,128)} fusion(bf16[5120,768]{1,0:T(8,128)(2,1)} %all-gather.9.cloned.1.call-done, bf16[5120,768]{1,0:T(8,128)(2,1)} %copy-done.48, f32[]{:T(128)S(6)} %convert_element_type.180), kind=kOutput, calls=%fused_computation.78 | convolution fusion | flops 6040387584 | bytes 18087940 | tf_op jit(solution)/shard_map/dot_general | solution.py:23
  850.3 14.4 %multiply_bitcast_fusion = f32[1,768,768]{2,1,0:T(8,128)} fusion(bf16[5120,768]{1,0:T(8,128)(2,1)} %all-gather.11.cloned.1.call-done, f32[]{:T(128)S(6)} %convert_element_type.180, f32[5120,768]{1,0:T(8,128)} %fusion.72), kind=kOutput, calls=%fused_computation.77 | convolution fusion | flops 6075777024 | bytes 25952260 | tf_op jit(solution)/shard_map/dot_general | solution.py:23
  870.7 41.1 %all-reduce = (f32[768]{0:T(1024)}, f32[768]{0:T(1024)}, f32[768]{0:T(1024)}, f32[768]{0:T(1024)}, f32[768,8]{0,1:T(8,128)}, /*index=5*/f32[8]{0:T(128)S(1)}) all-reduce(f32[768]{0:T(1024)S(1)} %get-tuple-element.230, f32[768]{0:T(1024)S(1)} %get-tuple-element.235, ...), channel_id=1, replica_groups=mesh['expert'=8,'hidden'=4] {'expert','hidden'}, use_global_device_ids=true, to_apply=%region_36.37 | all-reduce | flops 9224 | bytes 73792 | tf_op jit(solution)/shard_map/psum | solution.py:250
  912.3 2.8 fusion.63
  915.2 119.3 %all-reduce.4.cloned.1.call-done = (f32[768,768]{1,0:T(8,128)}, f32[768,768]{1,0:T(8,128)}, f32[768,768]{1,0:T(8,128)}, f32[768,768]{1,0:T(8,128)}) async-done(((f32[768,768]{1,0:T(8,128)}, f32[768,768]{1,0:T(8,128)}, f32[768,768]{1,0:T(8,128)}, f32[768,768]{1,0:T(8,128)}), (f32[768,768]{1,0:T(8,128)}, f32[768,768]{1,0:T(8,128)}, f32[768,768]{1,0:T(8,128)}, ...) | async-done | bytes 9437200 | tf_op jit(solution)/shard_map/psum | solution.py:250
  1034.5 3.4 copy.121
  (306 shorter events, 212.7 us)
Async XLA Ops:
  7.2 295.1 %copy-start = (bf16[1,768,768]{2,1,0:T(8,128)(2,1)S(1)}, bf16[1,768,768]{2,1,0:T(8,128)(2,1)}, u32[]{:S(2)}) copy-start(bf16[1,768,768]{2,1,0:T(8,128)(2,1)} %param.31) | copy-start | bytes 3538948
  7.2 36.7 %all-gather.5.cloned.1.call-start = ((), (), s32[]{:S(2)}) async-start(), calls=%async_computation.8 | async-start | bytes 3932160 | tf_op jit(solution)/shard_map/all_gather | solution.py:84
  8.6 12.3 %copy-start.26 = (f32[512]{0:T(512)}, f32[512]{0:T(512)S(1)}, u32[]{:S(2)}) copy-start(f32[512]{0:T(512)S(1)} %broadcast_multiply_fusion.5) | copy-start | bytes 6148
  10.2 10.8 %copy-start.30 = (f32[512]{0:T(512)}, f32[512]{0:T(512)S(1)}, u32[]{:S(2)}) copy-start(f32[512]{0:T(512)S(1)} %add_rsqrt_fusion.1) | copy-start | bytes 6148
  10.2 3.6 copy-start.4
  10.2 3.6 copy-start.17
  10.2 3.6 copy-start.32
  10.2 3.6 copy-start.45
  13.7 2.2 copy-start.25
  13.7 3.5 copy-start.47
  13.7 60.9 %all-gather.7.cloned.1.call-start = ((), (), s32[]{:S(2)}) async-start(), calls=%async_computation.9 | async-start | bytes 3932160 | tf_op jit(solution)/shard_map/all_gather | solution.py:85
  15.7 286.7 %all-gather.9.cloned.1.call-start = ((), (), s32[]{:S(2)}) async-start(), calls=%async_computation.10 | async-start | bytes 9830400 | tf_op jit(solution)/shard_map/all_gather | solution.py:132
  20.1 0.6 copy-start.22
  23.2 3.1 copy-start.39
  26.2 5.1 copy-start.34
  79.3 7.5 copy-start.35
  172.3 3.0 copy-start.12
  172.3 4.7 copy-start.24
  172.3 4.7 copy-start.38
  175.3 1.1 copy-start.2
  176.5 0.6 copy-start.28
  177.4 68.2 %copy-start.6 = (bf16[512,768]{1,0:T(8,128)(2,1)}, bf16[512,768]{1,0:T(8,128)(2,1)S(1)}, u32[]{:S(2)}) copy-start(bf16[512,768]{1,0:T(8,128)(2,1)S(1)} %add_convert_fusion.1) | copy-start | bytes 2359300
  236.5 1.1 copy-start.8
  236.5 121.3 %all-gather.11.cloned.1.call-start = ((), (), s32[]{:S(2)}) async-start(), calls=%async_computation.12 | async-start | bytes 9830400 | tf_op jit(solution)/shard_map/all_gather | solution.py:171
  240.1 5.4 copy-start.23
  301.8 56.0 %copy-start.40 = (bf16[1,768,768]{2,1,0:T(8,128)(2,1)S(1)}, bf16[1,768,768]{2,1,0:T(8,128)(2,1)}, u32[]{:S(2)}) copy-start(bf16[1,768,768]{2,1,0:T(8,128)(2,1)} %param.32) | copy-start | bytes 3538948
  301.8 155.6 %reduce-scatter.7.cloned.1.call-start = ((), (), s32[]{:S(2)}) async-start(), calls=%async_computation.13 | async-start | bytes 9830400 | tf_op jit(solution)/shard_map/reduce_scatter | solution.py:177
  376.9 3.2 copy-start.48
  388.7 140.3 %reduce-scatter.5.cloned.1.call-start = ((), (), s32[]{:S(2)}) async-start(), calls=%async_computation.11 | async-start | bytes 9830400 | tf_op jit(solution)/shard_map/reduce_scatter | solution.py:136
  457.5 71.6 %all-to-all-start.3 = ((bf16[8,160,768]{2,1,0:T(8,128)(2,1)}), bf16[8,160,768]{2,1,0:T(8,128)(2,1)S(1)}, u32[]{:S(2)}, u32[]{:S(2)}) async-start(bf16[8,160,768]{2,1,0:T(8,128)(2,1)} %bitcast.199), calls=%async_computation.5 | async-start | bytes 3932160 | tf_op jit(solution)/shard_map/all_to_all | solution.py:182
  529.0 5.6 copy-start.9
  529.0 47.1 %all-to-all-start.1 = ((bf16[8,160,768]{2,1,0:T(8,128)(2,1)}), bf16[8,160,768]{2,1,0:T(8,128)(2,1)}, u32[]{:S(2)}, u32[]{:S(2)}) async-start(bf16[8,160,768]{2,1,0:T(8,128)(2,1)} %bitcast.198), calls=%async_computation.2 | async-start | bytes 3932160 | tf_op jit(solution)/shard_map/all_to_all | solution.py:139
  534.6 259.2 %reduce-scatter.9.cloned.1.call-start = ((), (), s32[]{:S(2)}) async-start(), calls=%async_computation.14 | async-start | bytes 3932160 | tf_op jit(solution)/shard_map/reduce_scatter | solution.py:227
  610.4 5.7 copy-start.3
  610.4 5.8 copy-start.29
  616.2 1.4 copy-start.10
  616.2 1.6 copy-start.11
  617.8 1.4 copy-start.41
  620.1 0.7 copy-start.36
  620.1 0.7 copy-start.37
  753.6 0.9 copy-start.20
  753.6 1.4 copy-start.5
  753.6 1.4 copy-start.27
  753.6 1.4 copy-start.31
  753.6 1.4 copy-start.33
  753.6 1.4 copy-start.46
  753.6 80.9 %reduce-scatter.11.cloned.1.call-start = ((), (), s32[]{:S(2)}) async-start(), calls=%async_computation.15 | async-start | bytes 3932160 | tf_op jit(solution)/shard_map/reduce_scatter | solution.py:230
  754.5 280.0 %all-reduce.4.cloned.1.call-start = ((), (), s32[]{:S(2)}) async-start(), calls=%async_computation.16 | async-start | bytes 18874368 | tf_op jit(solution)/shard_map/psum | solution.py:250
  755.0 3.7 copy-start.13
  850.3 14.4 %copy-start.7 = (bf16[512,768]{1,0:T(8,128)(2,1)S(1)}, bf16[512,768]{1,0:T(8,128)(2,1)}, u32[]{:S(2)}) copy-start(bf16[512,768]{1,0:T(8,128)(2,1)} %copy-done.6) | copy-start | bytes 2359300
  850.3 14.8 %copy-start.21 = (bf16[12,512,64]{1,2,0:T(8,128)(2,1)S(1)}, bf16[12,512,64]{1,2,0:T(8,128)(2,1)}, u32[]{:S(2)}) copy-start(bf16[12,512,64]{1,2,0:T(8,128)(2,1)} %copy-done.20) | copy-start | bytes 2359300
  850.3 14.8 %copy-start.42 = (bf16[768,768]{1,0:T(8,128)(2,1)S(1)}, bf16[768,768]{1,0:T(8,128)(2,1)}, u32[]{:S(2)}) copy-start(bf16[768,768]{1,0:T(8,128)(2,1)} %param.24) | copy-start | bytes 3538948
  865.1 1.3 copy-start.43
  865.1 1.5 copy-start.44
  866.6 1.3 copy-start.18
  866.6 1.5 copy-start.19
  1034.4 3.4 copy-start.16
  1037.8 2.5 copy-start.15
  1040.3 2.5 copy-start.14
  1040.3 3.9 copy-start.1
Sparse Core Ops, SparseCore 0:
  13.8 30.0 all-gather.4
  46.0 28.5 all-gather.6
  236.7 55.4 all-gather.8
  302.0 55.8 all-gather.10
  388.8 68.5 reduce-scatter.6
  460.0 68.9 reduce-scatter.4
  753.7 40.0 reduce-scatter.8
  796.5 37.9 reduce-scatter.10
  841.3 193.0 all-reduce.3
where the time goes:
time: 1060 us; the launch traced here: 1050 us
  waiting for transfers between devices  405 us (38%)
  matrix products  292 us (28%)
  blocking collectives  139 us (13%)
  local copies, waits for them, and re-layouts  133 us (13%)
  other arithmetic  55 us (5%)
  between operations  14.6 us (1%)
  starting transfers between devices  11.9 us (1%)
    dot_general x72, matrix products, contract(): lax.dot_general(left, right, (((left_axis,), (right_axis,)), ((), ())), p...  197 us
    psum x1, waiting for transfers between devices, shards(): lax.psum((gain_one_grad, shift_one_grad, query_grad, key_grad, value_grad...  119 us
    dot_general x30, matrix products, product(): return jnp.dot(left, right, preferred_element_type=jnp.float32)  93.2 us
    reduce_scatter x1, waiting for transfers between devices, shards(): lax.psum_scatter(partial_sum.astype(jnp.bfloat16), 'hidden', scatter_dime...  66.1 us
    reduce_scatter x1, waiting for transfers between devices, shards(): lax.psum_scatter(partial_in.astype(jnp.bfloat16), 'hidden', scatter_dimen...  53.8 us
    all_to_all x1, blocking collectives, shards(): lax.all_to_all(outgoing, 'expert', split_axis=0, concat_axis=0, tiled=True)  49.4 us
    all_to_all x1, blocking collectives, shards(): lax.all_to_all(grad_outgoing, 'expert', split_axis=0, concat_axis=0, tile...  48.3 us
    all_gather x1, waiting for transfers between devices, shards(): grad_all = lax.all_gather(grad_slots, 'hidden', axis=0, tiled=True)  42.4 us
  transfers between devices with their start and end apart: 11, of which 9 were waited for; matrix products, arithmetic and copies ran while one was open for 13% of the time, Pallas kernels for 0%

commit v1 on v0

v1 whole, which is shorter than its diff:
```python
from functools import partial

import jax
import jax.numpy as jnp
from jax import lax
from jax.experimental import pallas as pl
from jax.experimental.pallas import tpu as pltpu
from jax.sharding import PartitionSpec as P

HEAD_DIM = 64
HEADS = 12
EPSILON = 1e-05
SCALE = 0.125
MASKED = -1e30
BLOCK = 256
LANES = 128
BF = jnp.bfloat16
F32 = jnp.float32
I32 = jnp.int32
MESH = pl.DeviceIdType.MESH
ANY = pl.BlockSpec(memory_space=pl.ANY)
SMEM = pl.BlockSpec(memory_space=pltpu.SMEM)
VMEM = pl.BlockSpec(memory_space=pltpu.VMEM)
DMA = pltpu.SemaphoreType.DMA
GELU_A = 0.7978845608028654
GELU_B = 0.044715


def mm(left, right):
    return jnp.dot(left, right, preferred_element_type=F32)


def mm_nt(left, right):
    return lax.dot_general(left, right, (((1,), (1,)), ((), ())), preferred_element_type=F32)


def mm_tn(left, right):
    return lax.dot_general(left, right, (((0,), (0,)), ((), ())), preferred_element_type=F32)


def iota(shape, axis):
    return lax.broadcasted_iota(I32, shape, axis)


def norm_parts(values):
    centred = values - jnp.mean(values, axis=-1, keepdims=True)
    inverse = lax.rsqrt(jnp.mean(centred * centred, axis=-1, keepdims=True) + EPSILON)
    return centred * inverse, inverse


def norm_back(grad_out, normed, inverse, gain):
    grad_normed = grad_out * gain
    first = jnp.mean(grad_normed, axis=-1, keepdims=True)
    second = jnp.mean(grad_normed * normed, axis=-1, keepdims=True)
    return inverse * (grad_normed - first - normed * second)


def split_two(value):
    high = value.astype(BF)
    return high, (value - high.astype(F32)).astype(BF)


def shape_of(shape, dtype):
    return jax.ShapeDtypeStruct(shape, dtype)


def local_call(body, name, outs, *args, specs=None, scratch=(), flops=0, vmem=60):
    nbytes = sum(a.size * a.dtype.itemsize for a in args)
    return pl.pallas_call(
        body,
        name=name,
        out_shape=outs,
        in_specs=specs or [VMEM] * len(args),
        out_specs=jax.tree.map(lambda _: VMEM, outs),
        scratch_shapes=list(scratch),
        compiler_params=pltpu.CompilerParams(vmem_limit_bytes=vmem << 20),
        cost_estimate=pl.CostEstimate(flops=flops, bytes_accessed=nbytes, transcendentals=0),
    )(*args)


def greet(peers):
    barrier = pltpu.get_barrier_semaphore()
    for peer in peers:
        pl.semaphore_signal(barrier, inc=1, device_id=peer, device_id_type=MESH)
    pl.semaphore_wait(barrier, len(peers))


def remote(src, dst, send, recv, peer):
    return pltpu.make_async_remote_copy(
        src_ref=src, dst_ref=dst, send_sem=send, recv_sem=recv, device_id=peer, device_id_type=MESH
    )


def exchange_body(axis, size, count, *refs):
    ins, outs = refs[:count], refs[count : 2 * count]
    local_sem, send_sem, recv_sem = refs[2 * count :]
    me = lax.axis_index(axis)
    peers = [lax.rem(me + step, size) for step in range(1, size)]
    greet([{axis: peer} for peer in peers])
    copies = []
    for at, peer in enumerate(peers):
        for which in range(count):
            copy = remote(
                ins[which].at[peer],
                outs[which].at[me],
                send_sem.at[which, at],
                recv_sem.at[which, at],
                {axis: peer},
            )
            copy.start()
            copies.append(copy)
    own = [
        pltpu.make_async_copy(ins[which].at[me], outs[which].at[me], local_sem.at[which])
        for which in range(count)
    ]
    for copy in own:
        copy.start()
    for copy in own:
        copy.wait()
    for copy in copies:
        copy.wait()


def exchange(axis, arrays, name, cid):
    size = lax.axis_size(axis)
    count = len(arrays)
    return pl.pallas_call(
        partial(exchange_body, axis, size, count),
        name=name,
        out_shape=[shape_of(a.shape, a.dtype) for a in arrays],
        in_specs=[ANY] * count,
        out_specs=[ANY] * count,
        scratch_shapes=[DMA((count,)), DMA((count, size - 1)), DMA((count, size - 1))],
        compiler_params=pltpu.CompilerParams(collective_id=cid, has_side_effects=True),
    )(*arrays)


def gather_body(size, chunks, x, o, local_sem, s1, r1, s2, r2, s3, r3):
    me = lax.axis_index("hidden")
    core = lax.rem(me, 2)
    far = size // 2
    pair = me // 2
    mate = pair * 2 + 1 - core
    others = [lax.rem(pair + step, far) * 2 + core for step in range(1, far)]
    greet([{"hidden": p} for p in others] + [{"hidden": mate}])
    own = pltpu.make_async_copy(x, o.at[me], local_sem)
    own.start()
    rows = x.shape[0] // chunks
    across, beside, onward = [], [], []
    for k in range(chunks):
        part = pl.ds(k * rows, rows)
        for n, peer in enumerate(others):
            copy = remote(x.at[part], o.at[me, part], s1.at[n, k], r1.at[n, k], {"hidden": peer})
            copy.start()
            across.append((n, k, copy))
        copy = remote(x.at[part], o.at[me, part], s2.at[k], r2.at[k], {"hidden": mate})
        copy.start()
        beside.append(copy)
    for n, k, copy in across:
        part = pl.ds(k * rows, rows)
        source = lax.rem(pair + far - (n + 1), far) * 2 + core
        copy.wait_recv()
        slot = o.at[source, part]
        onto = remote(slot, slot, s3.at[n, k], r3.at[n, k], {"hidden": mate})
        onto.start()
        onward.append(onto)
    own.wait()
    for _, _, copy in across:
        copy.wait_send()
    for copy in beside + onward:
        copy.wait()


def gather_hidden(x, name, cid, chunks=8):
    size = lax.axis_size("hidden")
    far = size // 2
    return pl.pallas_call(
        partial(gather_body, size, chunks),
        name=name,
        out_shape=shape_of((size, *x.shape), x.dtype),
        in_specs=[ANY],
        out_specs=ANY,
        scratch_shapes=[DMA]
        + [DMA((far - 1, chunks))] * 2
        + [DMA((chunks,))] * 2
        + [DMA((far - 1, chunks))] * 2,
        compiler_params=pltpu.CompilerParams(collective_id=cid, has_side_effects=True),
    )(x)


def total_body(sizes, x, o, first, second, s1, r1, s2, r2):
    along = ("hidden", "expert")
    me = [lax.axis_index(axis) for axis in along]
    peers = [
        [{axis: lax.rem(me[n] + step, sizes[n])} for step in range(1, sizes[n])]
        for n, axis in enumerate(along)
    ]
    greet(peers[0] + peers[1])
    held = x
    for n, (box, send, recv) in enumerate(((first, s1, r1), (second, s2, r2))):
        copies = []
        for at, peer in enumerate(peers[n]):
            copy = remote(held, box.at[at], send.at[at], recv.at[at], peer)
            copy.start()
            copies.append(copy)
        for copy in copies:
            copy.wait()
        summed = held[...]
        for at in range(sizes[n] - 1):
            summed = summed + box[at]
        o[...] = summed
        held = o


def total_all(x, name, cid):
    sizes = (lax.axis_size("hidden"), lax.axis_size("expert"))
    return pl.pallas_call(
        partial(total_body, sizes),
        name=name,
        out_shape=shape_of(x.shape, x.dtype),
        in_specs=[VMEM],
        out_specs=VMEM,
        scratch_shapes=[
            pltpu.VMEM((sizes[0] - 1, *x.shape), x.dtype),
            pltpu.VMEM((sizes[1] - 1, *x.shape), x.dtype),
            DMA((sizes[0] - 1,)),
            DMA((sizes[0] - 1,)),
            DMA((sizes[1] - 1,)),
            DMA((sizes[1] - 1,)),
        ],
        compiler_params=pltpu.CompilerParams(collective_id=cid, has_side_effects=True),
    )(x)


def sum_scatter_body(axis, size, x, o, box, send, recv):
    me = lax.axis_index(axis)
    peers = [lax.rem(me + step, size) for step in range(1, size)]
    greet([{axis: peer} for peer in peers])
    copies = []
    for at, peer in enumerate(peers):
        copy = remote(x.at[peer], box.at[at], send.at[at], recv.at[at], {axis: peer})
        copy.start()
        copies.append(copy)
    total = x[me].astype(F32)
    for at, copy in enumerate(copies):
        copy.wait_recv()
        total = total + box[at].astype(F32)
    o[...] = total.astype(o.dtype)
    for copy in copies:
        copy.wait_send()


def sum_scatter(axis, x, name, cid, dtype):
    size = lax.axis_size(axis)
    return pl.pallas_call(
        partial(sum_scatter_body, axis, size),
        name=name,
        out_shape=shape_of(x.shape[1:], dtype),
        in_specs=[VMEM],
        out_specs=VMEM,
        scratch_shapes=[
            pltpu.VMEM((size - 1, *x.shape[1:]), x.dtype),
            DMA((size - 1,)),
            DMA((size - 1,)),
        ],
        compiler_params=pltpu.CompilerParams(
            collective_id=cid, has_side_effects=True, vmem_limit_bytes=40 << 20
        ),
    )(x)


def route_body(experts, capacity, ids, ids_t, grad, pos, pos_t, slot, count, out):
    rows = ids.shape[0]
    col = [ids[:, j : j + 1] for j in range(2)]
    row = [ids_t[j : j + 1, :] for j in range(2)]
    lane = iota((rows, LANES), 1)
    hot = [(lane == c).astype(BF) for c in col]
    either = hot[0] + hot[1]
    below = (iota((rows, rows), 0) > iota((rows, rows), 1)).astype(BF)
    before = mm(below, either)
    wide = max(experts, 16)
    deep = iota((wide, rows), 0)
    hot_t = [(deep == r).astype(BF) for r in row]
    either_t = hot_t[0] + hot_t[1]
    above = (iota((rows, rows), 0) < iota((rows, rows), 1)).astype(BF)
    before_t = mm(either_t, above)
    count[...] = jnp.sum(either.astype(F32), axis=0, keepdims=True)
    slots_t = []
    for j in range(2):
        at = jnp.sum(hot[j].astype(F32) * before, axis=1, keepdims=True).astype(I32)
        pos[:, j : j + 1] = col[j] * capacity + at
        slot[:, j : j + 1] = at
        at_t = jnp.sum(hot_t[j].astype(F32) * before_t, axis=0, keepdims=True).astype(I32)
        at_t = row[j] * capacity + at_t
        pos_t[j : j + 1, :] = at_t
        slots_t.append(at_t)
    total = experts * capacity
    half = total // 2
    for n in range(2):
        place = iota((half, rows), 0) + n * half
        pick = ((place == slots_t[0]) | (place == slots_t[1])).astype(BF)
        out[pl.ds(n * half, half), :] = mm(pick, grad[...]).astype(BF)


def doc_bounds(docs, count):
    ends, at = [], 0
    for n in range(count - 1):
        at = at + docs[0, n]
        ends.append(at)
    return ends


def start_of(place, ends):
    begin = jnp.zeros_like(place)
    for end in ends:
        begin = jnp.where(place >= end, end, begin)
    return begin


def end_of(place, ends, last):
    finish = last
    for end in reversed(ends):
        finish = jnp.where(place < end, end, finish)
    return finish


def forward_body(heads, docs, tokens, gain, shift, w_t, h_one, qkv_t, out_t, lse, keys):
    count = tokens.shape[0]
    width = heads * HEAD_DIM
    blocks = count // BLOCK
    ends = doc_bounds(docs, docs.shape[1])

    def project(i, _):
        rows = pl.ds(pl.multiple_of(i * BLOCK, BLOCK), BLOCK)
        normed, _unused = norm_parts(tokens[rows, :].astype(F32))
        hidden = (normed * gain[...] + shift[...]).astype(BF)
        h_one[rows, :] = hidden
        block = mm_nt(w_t[...], hidden)
        qkv_t[0:width, rows] = block[0:width].astype(BF)
        qkv_t[width:, rows] = block[width:].astype(BF)
        for n in range(heads):
            part = block[width + n * HEAD_DIM : width + (n + 1) * HEAD_DIM]
            keys[n, rows, :] = part.T.astype(BF)
        return 0

    lax.fori_loop(0, blocks, project, 0)
    lse[...] = jnp.zeros_like(lse)

    def attend(i, _):
        base = i * BLOCK
        rows = pl.ds(pl.multiple_of(base, BLOCK), BLOCK)
        q_pos = base + iota((1, BLOCK), 1)
        begin = start_of(q_pos, ends)
        first = start_of(base, ends) // BLOCK
        queries = [
            qkv_t[n * HEAD_DIM : (n + 1) * HEAD_DIM, rows] * jnp.asarray(SCALE, BF)
            for n in range(heads)
        ]

        def step(j, carry):
            at = pl.multiple_of(j * BLOCK, BLOCK)
            part = pl.ds(at, BLOCK)
            k_pos = at + iota((BLOCK, BLOCK), 0)
            allowed = (k_pos <= q_pos) & (k_pos >= begin)
            result = []
            for n in range(heads):
                top, total, acc = carry[n]
                score = mm(keys[n, part, :], queries[n])
                score = jnp.where(allowed, score, MASKED)
                new_top = jnp.maximum(top, jnp.max(score, axis=0, keepdims=True))
                fade = jnp.exp(top - new_top)
                weight = jnp.exp(score - new_top)
                total = total * fade + jnp.sum(weight, axis=0, keepdims=True)
                lo = 2 * width + n * HEAD_DIM
                value = qkv_t[lo : lo + HEAD_DIM, part]
                acc = acc * fade + mm(value, weight.astype(BF))
                result.append((new_top, total, acc))
            return tuple(result)

        empty = (
            jnp.full((1, BLOCK), MASKED, F32),
            jnp.zeros((1, BLOCK), F32),
            jnp.zeros((HEAD_DIM, BLOCK), F32),
        )
        final = lax.fori_loop(first, i + 1, step, (empty,) * heads)
        for n in range(heads):
            top, total, acc = final[n]
            out_t[n * HEAD_DIM : (n + 1) * HEAD_DIM, rows] = (acc / total).astype(BF)
            lse[n : n + 1, rows] = top + jnp.log(total)
        return 0

    lax.fori_loop(0, blocks, attend, 0)


def middle_body(
    experts,
    capacity,
    padded,
    tokens,
    att_t,
    w_out,
    gain,
    shift,
    w_router,
    ids,
    slot,
    pos_t,
    residual,
    gates,
    slots,
    gate_rows,
):
    rows = tokens.shape[0]
    res = tokens[...].astype(F32) + mm_tn(att_t[...], w_out[...])
    residual[...] = res
    normed, _unused = norm_parts(res)
    hidden = (normed * gain[...] + shift[...]).astype(BF)
    logits = mm(hidden, w_router[...])
    lane = iota((rows, experts), 1)
    chosen = [
        jnp.sum(jnp.where(lane == ids[:, j : j + 1], logits, 0.0), axis=1, keepdims=True)
        for j in range(2)
    ]
    top = jnp.maximum(chosen[0], chosen[1])
    raised = [jnp.exp(c - top) for c in chosen]
    both = raised[0] + raised[1]
    gate = [r / both for r in raised]
    for j in range(2):
        gates[:, j : j + 1] = gate[j]
    total = experts * capacity
    half = total // 2
    for n in range(2):
        place = iota((half, rows), 0) + n * half
        pick = ((place == pos_t[0:1, :]) | (place == pos_t[1:2, :])).astype(BF)
        slots[pl.ds(n * half, half), :] = mm(pick, hidden).astype(BF)
    column = iota((rows, padded), 1)
    for e in range(experts):
        mix = jnp.zeros((rows, padded), F32)
        for j in range(2):
            here = (ids[:, j : j + 1] == e) & (slot[:, j : j + 1] == column)
            mix = jnp.where(here, gate[j], mix)
        line = jnp.sum(mix, axis=0, keepdims=True)
        gate_rows[e] = jnp.broadcast_to(line, (8, padded))


def experts_body(
    sources, capacity, padded, xs, gs, gate_rows, ups, downs, y, dx, dg, xg, dy, act, dz
):
    rows = xs.shape[0]
    shards = ups.shape[0]
    width = ups.shape[2]
    x, g = xs[...], gs[...]
    y_acc = jnp.zeros((rows, x.shape[1]), F32)
    dx_acc = jnp.zeros((rows, x.shape[1]), F32)
    for c in range(shards):
        z = mm(x, ups[c])
        du = mm_nt(g, downs[c])
        square = z * z
        t = jnp.tanh(z * (GELU_A + GELU_A * GELU_B * square))
        plus = 0.5 + 0.5 * t
        hidden = (z * plus).astype(BF)
        slope = plus + 0.5 * z * (1.0 - t * t) * (GELU_A + 3.0 * GELU_A * GELU_B * square)
        back = (slope * du).astype(BF)
        act[:, c * width : (c + 1) * width] = hidden
        dz[:, c * width : (c + 1) * width] = back
        y_acc = y_acc + mm(hidden, downs[c])
        dx_acc = dx_acc + mm_nt(back, ups[c])
    y_low = y_acc.astype(BF)
    y[...] = y_low
    dx[...] = dx_acc.astype(BF)
    dots = jnp.sum(y_low.astype(F32) * g.astype(F32), axis=1, keepdims=True)
    for s in range(sources):
        part = slice(s * capacity, (s + 1) * capacity)
        gate = gate_rows[s].T[0:capacity, 0:1]
        xg[part, :] = (x[part].astype(F32) * gate).astype(BF)
        dy[part, :] = (g[part].astype(F32) * gate).astype(BF)
        tall = jnp.broadcast_to(dots[part], (capacity, LANES))
        if padded > capacity:
            tall = jnp.concatenate([tall, jnp.zeros((padded - capacity, LANES), F32)], axis=0)
        dg[s] = tall.T[0:8]


def second_body(
    experts,
    capacity,
    padded,
    residual,
    grad,
    dx,
    dg_rows,
    gates,
    ids,
    slot,
    pos,
    att_t,
    w_out,
    gain,
    shift,
    w_router,
    d_res,
    d_att_t,
    w_out_grad,
    sums,
    router_grad,
):
    rows = residual.shape[0]
    normed, inverse = norm_parts(residual[...])
    hidden = (normed * gain[...] + shift[...]).astype(BF)
    gate = [gates[:, j : j + 1] for j in range(2)]
    column = iota((rows, padded), 1)
    dots = []
    for j in range(2):
        mix = jnp.zeros((rows, padded), F32)
        for e in range(experts):
            here = (ids[:, j : j + 1] == e) & (slot[:, j : j + 1] == column)
            mix = jnp.where(here, dg_rows[e, 0:1, :], mix)
        dots.append(jnp.sum(mix, axis=1, keepdims=True))
    mean = gate[0] * dots[0] + gate[1] * dots[1]
    lane = iota((rows, experts), 1)
    d_logits = jnp.zeros((rows, experts), F32)
    for j in range(2):
        d_logits = jnp.where(lane == ids[:, j : j + 1], gate[j] * (dots[j] - mean), d_logits)
    high, low = split_two(d_logits)
    d_hidden = mm_nt(high, w_router[...]) + mm_nt(low, w_router[...])
    router_grad[...] = mm_tn(high, hidden) + mm_tn(low, hidden)
    total = experts * capacity
    place = iota((rows, total), 1)
    for j in range(2):
        pick = (place == pos[:, j : j + 1]).astype(BF)
        d_hidden = d_hidden + gate[j] * mm(pick, dx[...])
    sums[0:1, :] = jnp.sum(d_hidden * normed, axis=0, keepdims=True)
    sums[1:2, :] = jnp.sum(d_hidden, axis=0, keepdims=True)
    d_resid = grad[...].astype(F32) + norm_back(d_hidden, normed, inverse, gain[...])
    d_res[...] = d_resid
    branch = d_resid.astype(BF)
    d_att_t[...] = mm_nt(w_out[...], branch).astype(BF)
    w_out_grad[...] = mm(att_t[...], branch).astype(BF)


def output_body(residual, gates, pos, y, out):
    rows, total = residual.shape[0], y.shape[0]
    place = iota((rows, total), 1)
    result = residual[...]
    for j in range(2):
        pick = (place == pos[:, j : j + 1]).astype(BF)
        result = result + gates[:, j : j + 1] * mm(pick, y[...])
    out[...] = result.astype(BF)


def backward_body(
    heads,
    docs,
    tokens,
    gain,
    h_one,
    qkv_t,
    out_t,
    lse,
    d_att_t,
    w_t,
    d_hidden,
    w_grad,
    sums,
    keys,
    values,
    dots,
    dq_acc,
    dk_acc,
    dv_acc,
    d_qkv,
    w_acc,
):
    count = tokens.shape[0]
    width = heads * HEAD_DIM
    blocks = count // BLOCK
    ends = doc_bounds(docs, docs.shape[1])
    dq_acc[...] = jnp.zeros_like(dq_acc)

    def prepare(i, _):
        rows = pl.ds(pl.multiple_of(i * BLOCK, BLOCK), BLOCK)
        for n in range(heads):
            lo = n * HEAD_DIM
            here = slice(lo, lo + HEAD_DIM)
            keys[n, rows, :] = (
                qkv_t[width + lo : width + lo + HEAD_DIM, rows].astype(F32).T.astype(BF)
            )
            values[n, rows, :] = (
                qkv_t[2 * width + lo : 2 * width + lo + HEAD_DIM, rows].astype(F32).T.astype(BF)
            )
            product = out_t[here, rows].astype(F32) * d_att_t[here, rows].astype(F32)
            dots[n : n + 1, rows] = jnp.sum(product, axis=0, keepdims=True)
        return 0

    lax.fori_loop(0, blocks, prepare, 0)

    def over_keys(j, _):
        at = pl.multiple_of(j * BLOCK, BLOCK)
        part = pl.ds(at, BLOCK)
        k_pos = at + iota((BLOCK, BLOCK), 0)
        last = (end_of(at + BLOCK - 1, ends, count) - 1) // BLOCK
        dk_acc[...] = jnp.zeros_like(dk_acc)
        dv_acc[...] = jnp.zeros_like(dv_acc)

        def over_queries(i, _):
            base = pl.multiple_of(i * BLOCK, BLOCK)
            rows = pl.ds(base, BLOCK)
            q_pos = base + iota((1, BLOCK), 1)
            begin = start_of(q_pos, ends)
            allowed = (k_pos <= q_pos) & (k_pos >= begin)
            for n in range(heads):
                here = slice(n * HEAD_DIM, (n + 1) * HEAD_DIM)
                query = qkv_t[here, rows] * jnp.asarray(SCALE, BF)
                d_att = d_att_t[here, rows]
                score = mm(keys[n, part, :], query) - lse[n : n + 1, rows]
                weight = jnp.exp(jnp.where(allowed, score, MASKED))
                d_weight = mm(values[n, part, :], d_att)
                d_score = (weight * (d_weight - dots[n : n + 1, rows])).astype(BF)
                dv_acc[here, :] += mm_nt(d_att, weight.astype(BF))
                dk_acc[here, :] += mm_nt(query, d_score)
                lo = width + n * HEAD_DIM
                dq_acc[here, rows] += mm(qkv_t[lo : lo + HEAD_DIM, part], d_score)
            return 0

        lax.fori_loop(j, last + 1, over_queries, 0)
        d_qkv[width : 2 * width, part] = dk_acc[...].astype(BF)
        d_qkv[2 * width :, part] = dv_acc[...].astype(BF)
        return 0

    lax.fori_loop(0, blocks, over_keys, 0)
    w_acc[...] = jnp.zeros_like(w_acc)
    sums[...] = jnp.zeros_like(sums)

    def finish(i, _):
        rows = pl.ds(pl.multiple_of(i * BLOCK, BLOCK), BLOCK)
        d_qkv[0:width, rows] = (dq_acc[:, rows] * SCALE).astype(BF)
        block = d_qkv[:, rows]
        grad = mm_tn(block, w_t[...])
        normed, _unused = norm_parts(tokens[rows, :].astype(F32))
        d_hidden[rows, :] = grad.astype(BF)
        sums[0:1, :] += jnp.sum(grad * normed, axis=0, keepdims=True)
        sums[1:2, :] += jnp.sum(grad, axis=0, keepdims=True)
        w_acc[...] += mm(block, h_one[rows, :])
        return 0

    lax.fori_loop(0, blocks, finish, 0)
    w_grad[...] = w_acc[...].astype(BF)


def input_body(tokens, gain, d_res, d_hidden, out):
    normed, inverse = norm_parts(tokens[...].astype(F32))
    grad = d_hidden[...].astype(F32)
    out[...] = (d_res[...] + norm_back(grad, normed, inverse, gain[...])).astype(BF)


def shards(
    tokens,
    doc_lengths,
    expert_ids,
    gain_one,
    shift_one,
    w_query,
    w_key,
    w_value,
    w_out,
    gain_two,
    shift_two,
    w_router,
    w_up,
    w_down,
    out_grad,
):
    rows, model = tokens.shape
    n_expert, n_hidden = lax.axis_size("expert"), lax.axis_size("hidden")
    experts = n_expert * w_up.shape[0]
    capacity = max(2, rows * 2 * 5 // (4 * experts))
    padded = -(-capacity // LANES) * LANES
    total = experts * capacity
    group = rows * n_hidden
    heads = HEADS // n_hidden
    width = heads * HEAD_DIM
    mine = lax.axis_index("hidden") * width
    g1, s1 = gain_one.reshape(1, model), shift_one.reshape(1, model)
    g2, s2 = gain_two.reshape(1, model), shift_two.reshape(1, model)

    pos, pos_t, slot, count, g_slots = local_call(
        partial(route_body, experts, capacity),
        "route",
        [
            shape_of((rows, 2), I32),
            shape_of((2, rows), I32),
            shape_of((rows, 2), I32),
            shape_of((1, LANES), F32),
            shape_of((total, model), BF),
        ],
        expert_ids,
        expert_ids.T,
        out_grad,
    )
    g_in = lax.all_to_all(
        g_slots.reshape(experts, capacity, model), "expert", split_axis=0, concat_axis=0, tiled=True
    ).reshape(total, model)

    all_tokens = gather_hidden(tokens, "gather_tokens", 1).reshape(group, model)
    up_src, down_src, all_tokens = lax.optimization_barrier((w_up, w_down, all_tokens))
    ups = lax.all_gather(up_src, "hidden", axis=0, tiled=True)
    downs = lax.all_gather(down_src, "hidden", axis=0, tiled=True)

    w_t = jnp.concatenate(
        [lax.dynamic_slice(w, (0, mine), (model, width)).T for w in (w_query, w_key, w_value)],
        axis=0,
    )
    h_one, qkv_t, att_own, lse = local_call(
        partial(forward_body, heads),
        "attend",
        [
            shape_of((group, model), BF),
            shape_of((3 * width, group), BF),
            shape_of((width, group), BF),
            shape_of((8, group), F32),
        ],
        doc_lengths,
        all_tokens,
        g1,
        s1,
        w_t,
        specs=[SMEM, VMEM, VMEM, VMEM, VMEM],
        scratch=[pltpu.VMEM((heads, group, HEAD_DIM), BF)],
    )
    att_split = att_own.reshape(width, n_hidden, rows).transpose(1, 0, 2)
    (att_t,) = exchange("hidden", [att_split], "swap_att", 2)
    att_t = att_t.reshape(model, rows)

    residual, gates, x_slots, gate_rows = local_call(
        partial(middle_body, experts, capacity, padded),
        "middle",
        [
            shape_of((rows, model), F32),
            shape_of((rows, 2), F32),
            shape_of((total, model), BF),
            shape_of((experts, 8, padded), F32),
        ],
        tokens,
        att_t,
        w_out,
        g2,
        s2,
        w_router,
        expert_ids,
        slot,
        pos_t,
    )
    x_in, gate_in = exchange(
        "expert", [x_slots.reshape(experts, capacity, model), gate_rows], "dispatch", 3
    )
    x_in = x_in.reshape(total, model)

    per = max(1, 320 // capacity)
    steps = experts // per
    tall = per * capacity
    hidden_units = n_hidden * w_up.shape[2]

    def by_rows(width_of):
        return pl.BlockSpec((tall, width_of), lambda i: (i, 0))

    whole_w = pl.BlockSpec((n_hidden, *w_up.shape[1:]), lambda i: (0, 0, 0))
    by_source = pl.BlockSpec((per, 8, padded), lambda i: (i, 0, 0))
    y_out, dx_out, dg_rows, xg, dy, act, dz = pl.pallas_call(
        partial(experts_body, per, capacity, padded),
        name="experts",
        grid=(steps,),
        out_shape=[
            shape_of((total, model), BF),
            shape_of((total, model), BF),
            shape_of((experts, 8, padded), F32),
            shape_of((total, model), BF),
            shape_of((total, model), BF),
            shape_of((total, hidden_units), BF),
            shape_of((total, hidden_units), BF),
        ],
        in_specs=[by_rows(model), by_rows(model), by_source, whole_w, whole_w],
        out_specs=[
            by_rows(model),
            by_rows(model),
            by_source,
            by_rows(model),
            by_rows(model),
            by_rows(hidden_units),
            by_rows(hidden_units),
        ],
        compiler_params=pltpu.CompilerParams(
            dimension_semantics=("arbitrary",), vmem_limit_bytes=60 << 20
        ),
        cost_estimate=pl.CostEstimate(
            flops=8 * total * model * hidden_units, bytes_accessed=40 << 20, transcendentals=0
        ),
    )(x_in, g_in, gate_in, ups, downs)

    dx_back, dg_back = exchange(
        "expert", [dx_out.reshape(experts, capacity, model), dg_rows], "collect", 4
    )
    dx_back, y_out, act, dz = lax.optimization_barrier((dx_back, y_out, act, dz))
    y_back = lax.all_to_all(
        y_out.reshape(experts, capacity, model), "expert", split_axis=0, concat_axis=0, tiled=True
    ).reshape(total, model)

    trainable = (lax.axis_index("expert") >= experts // 2).astype(F32)
    up_part = lax.dot_general(xg, dz, (((0,), (0,)), ((), ())), preferred_element_type=F32)
    down_part = lax.dot_general(act, dy, (((0,), (0,)), ((), ())), preferred_element_type=F32)
    up_part = up_part.astype(BF).reshape(model, n_hidden, -1).transpose(1, 0, 2)
    down_part = down_part.astype(BF).reshape(n_hidden, -1, model)
    up_grad = lax.psum_scatter(up_part, "hidden", scatter_dimension=0, tiled=True)
    down_grad = lax.psum_scatter(down_part, "hidden", scatter_dimension=0, tiled=True)
    up_grad = up_grad.astype(F32) * trainable
    down_grad = down_grad.astype(F32) * trainable

    d_res, d_att_t, w_out_part, sums_two, router_part = local_call(
        partial(second_body, experts, capacity, padded),
        "second",
        [
            shape_of((rows, model), F32),
            shape_of((model, rows), BF),
            shape_of((model, model), BF),
            shape_of((2, model), F32),
            shape_of((experts, model), F32),
        ],
        residual,
        out_grad,
        dx_back.reshape(total, model),
        dg_back,
        gates,
        expert_ids,
        slot,
        pos,
        att_t,
        w_out,
        g2,
        s2,
        w_router,
    )
    (d_att_in,) = exchange("hidden", [d_att_t.reshape(n_hidden, width, rows)], "swap_datt", 5)
    d_att_own = d_att_in.transpose(1, 0, 2).reshape(width, group)

    d_hidden, w_part, sums_one = local_call(
        partial(backward_body, heads),
        "attend_back",
        [
            shape_of((group, model), BF),
            shape_of((3 * width, model), BF),
            shape_of((2, model), F32),
        ],
        doc_lengths,
        all_tokens,
        g1,
        h_one,
        qkv_t,
        att_own,
        lse,
        d_att_own,
        w_t,
        specs=[SMEM] + [VMEM] * 8,
        scratch=[
            pltpu.VMEM((heads, group, HEAD_DIM), BF),
            pltpu.VMEM((heads, group, HEAD_DIM), BF),
            pltpu.VMEM((8, group), F32),
            pltpu.VMEM((width, group), F32),
            pltpu.VMEM((width, BLOCK), F32),
            pltpu.VMEM((width, BLOCK), F32),
            pltpu.VMEM((3 * width, group), BF),
            pltpu.VMEM((3 * width, model), F32),
        ],
    )
    output = local_call(
        output_body, "output", shape_of((rows, model), BF), residual, gates, pos, y_back
    )
    d_hidden_own = sum_scatter(
        "hidden", d_hidden.reshape(n_hidden, rows, model), "sum_dh", 6, F32
    )
    input_grad = local_call(
        input_body, "input_grad", shape_of((rows, model), BF), tokens, g1, d_res, d_hidden_own
    )

    w_out_own = sum_scatter(
        "hidden", w_out_part.reshape(n_hidden, width, model), "sum_wout", 7, BF
    )
    w_all = jnp.concatenate([w_part, w_out_own], axis=0)
    piece = sum_scatter(
        "expert", w_all.reshape(n_expert, 4 * width // n_expert, model), "sum_w", 8, BF
    )
    pieces = exchange_all(piece, "spread_expert", 9).reshape(4 * width, model)
    full = gather_hidden(pieces, "spread_hidden", 10).reshape(n_hidden, 4, width, model)
    w_grads = [full[:, n].reshape(model, model).T.astype(F32) for n in range(3)]
    w_out_grad = full[:, 3].reshape(model, model).astype(F32)
    counts = jnp.zeros((1, model), F32).at[:, :experts].set(count[:, :experts])
    small = jnp.concatenate([sums_one, sums_two, counts, router_part], axis=0)
    short = small.shape[0]
    small = jnp.pad(small, ((0, -short % 8), (0, 0)))
    small = total_all(small, "total", 11)
    load = small[4, :experts] * experts / (rows * n_expert * n_hidden * 2)
    return (
        output,
        input_grad,
        small[0],
        small[1],
        *w_grads,
        w_out_grad,
        small[2],
        small[3],
        small[5 : 5 + experts].T,
        up_grad,
        down_grad,
        load,
    )


def spread_body(axis, size, x, o, local_sem, send_sem, recv_sem):
    me = lax.axis_index(axis)
    peers = [lax.rem(me + step, size) for step in range(1, size)]
    greet([{axis: peer} for peer in peers])
    copies = []
    for at, peer in enumerate(peers):
        copy = remote(x, o.at[me], send_sem.at[at], recv_sem.at[at], {axis: peer})
        copy.start()
        copies.append(copy)
    own = pltpu.make_async_copy(x, o.at[me], local_sem)
    own.start()
    own.wait()
    for copy in copies:
        copy.wait()


def exchange_all(x, name, cid):
    size = lax.axis_size("expert")
    return pl.pallas_call(
        partial(spread_body, "expert", size),
        name=name,
        out_shape=shape_of((size, *x.shape), x.dtype),
        in_specs=[ANY],
        out_specs=ANY,
        scratch_shapes=[DMA, DMA((size - 1,)), DMA((size - 1,))],
        compiler_params=pltpu.CompilerParams(collective_id=cid, has_side_effects=True),
    )(x)


def solution(mesh):
    in_specs = (
        P(("expert", "hidden"), None),
        P("expert", None),
        P(("expert", "hidden"), None),
        P(),
        P(),
        P(),
        P(),
        P(),
        P(),
        P(),
        P(),
        P(),
        P("expert", None, "hidden"),
        P("expert", "hidden", None),
        P(("expert", "hidden"), None),
    )
    out_specs = (
        P(("expert", "hidden"), None),
        P(("expert", "hidden"), None),
        P(),
        P(),
        P(),
        P(),
        P(),
        P(),
        P(),
        P(),
        P(),
        P("expert", None, "hidden"),
        P("expert", "hidden", None),
        P(),
    )
    return jax.shard_map(shards, mesh=mesh, in_specs=in_specs, out_specs=out_specs, check_vma=False)
```

time: 1060 us -> 581 us (0.55)
  Pallas kernels: 0 us -> 477 us
  waiting for transfers between devices: 405 us -> 0.79 us
  matrix products: 292 us -> 21.4 us
  blocking collectives: 139 us -> 0 us
  local copies, waits for them, and re-layouts: 133 us -> 31.3 us
  other arithmetic: 55 us -> 13.4 us
    pallas_call x0 -> x19, Pallas kernels: none -> 477 us  [the longest x4 141 us: exchange(): pl.pallas_call(partial(exchange_body, axis, size, count), name=name, out_...]
    dot_general x105 -> x2, matrix products: 292 us -> 21.4 us  [the longest x1 11.6 us: shards(): lax.dot_general(act, dy, (((0,), (0,)), ((), ())), preferred_element_type...]
    reduce_scatter x4 -> x2, waiting for transfers between devices: 190 us -> 0.01 us  [the longest x1 0.01 us: shards(): lax.psum_scatter(down_part, 'hidden', scatter_dimension=0, tiled=True)]
    psum x1 -> x0, waiting for transfers between devices: 119 us -> none  [shards(): lax.psum((gain_one_grad, shift_one_grad, query_grad, key_grad, value_grad...]
    all_to_all x2 -> x0, blocking collectives: 97.7 us -> none  [the longest x1 49.4 us: shards(): lax.all_to_all(outgoing, 'expert', split_axis=0, concat_axis=0, tiled=True)]
    all_gather x4 -> x2, waiting for transfers between devices: 73.6 us -> 0.04 us  [the longest x1 0.02 us: shards(): ups = lax.all_gather(up_src, 'hidden', axis=0, tiled=True)]
    psum x1 -> x0, blocking collectives: 41.1 us -> none  [shards(): lax.psum((gain_one_grad, shift_one_grad, query_grad, key_grad, value_grad...]
    gather x2 -> x0, local copies, waits for them, and re-layouts: 33.9 us -> none  [the longest x1 19.8 us: shards(): returned[flat_ids, slot_index].reshape(row_count, top_count, model_width)]
  transfers between devices with their start and end apart: 11 -> 6, of which waited for: 9 -> 0; matrix products, arithmetic and copies ran while one was open for 13% -> 8% of each run, Pallas kernels for 0% -> 64%
where the time goes in v1:
time: 581 us; the launch traced here: 572 us
  Pallas kernels  477 us (82%)
  local copies, waits for them, and re-layouts  31.3 us (5%)
  matrix products  21.4 us (4%)
  between operations  14.6 us (3%)
  other arithmetic  13.4 us (2%)
  starting transfers between devices  13.2 us (2%)
    pallas_call x4, Pallas kernels, exchange(): pl.pallas_call(partial(exchange_body, axis, size, count), name=name, out_...  141 us
    pallas_call x3, Pallas kernels, sum_scatter(): pl.pallas_call(partial(sum_scatter_body, axis, size), name=name, out_shap...  95.2 us
    pallas_call x7, Pallas kernels, local_call(): pl.pallas_call(body, name=name, out_shape=outs, in_specs=specs or [VMEM]...  94.4 us
    pallas_call x2, Pallas kernels, gather_hidden(): pl.pallas_call(partial(gather_body, size, chunks), name=name, out_shape=s...  65.2 us
    pallas_call x1, Pallas kernels, shards(): pl.pallas_call(partial(experts_body, per, capacity, padded), name='expert...  35.4 us
    pallas_call x1, Pallas kernels, exchange_all(): pl.pallas_call(partial(spread_body, 'expert', size), name=name, out_shape...  29.9 us
    pallas_call x1, Pallas kernels, total_all(): pl.pallas_call(partial(total_body, sizes), name=name, out_shape=shape_of(...  15.9 us
    unnamed x50, local copies, waits for them, and re-layouts  14.5 us
  transfers between devices with their start and end apart: 6, of which 0 were waited for; matrix products, arithmetic and copies ran while one was open for 8% of the time, Pallas kernels for 64%

profile of v1, /device:TPU:17, one launch (start us, length us, event | category | flops | bytes accessed | tf_op | source)
XLA Modules:
  0.0 571.7 jit_solution(6675298268527766841)
XLA Ops:
  7.2 0.0 all-gather.3.cloned.1.call-start
  7.2 26.7 %gather_tokens.1 = bf16[4,512,768]{2,1,0:T(8,128)(2,1)} custom-call(bf16[512,768]{1,0:T(8,128)(2,1)} %tokens.3), custom_call_target="tpu_custom_call" | custom-call | tf_op jit(solution)/shard_map/gather_tokens/pallas_call | solution.py:177
  34.0 0.0 all-gather.5.cloned.1.call-start
  34.0 0.7 all-gather.5.cloned.1.call-update
  34.8 0.9 copy.65.ids
  35.6 4.2 route.1
  39.9 5.7 %all-to-all-start = ((bf16[8,160,768]{2,1,0:T(8,128)(2,1)}), bf16[8,160,768]{2,1,0:T(8,128)(2,1)S(1)}, u32[]{:S(2)}, u32[]{:S(2)}) async-start(bf16[8,160,768]{2,1,0:T(8,128)(2,1)} %bitcast.87), calls=%async_computation | async-start | bytes 3932160 | tf_op jit(solution)/shard_map/all_to_all | solution.py:699
  45.6 0.6 reshape.139.gain
  46.2 0.6 reshape.143.gain
  46.8 0.6 reshape.144.shift
  47.4 0.6 reshape.140.shift
  47.9 0.8 copy.64.w_router
  48.7 0.2 constant_dynamic-slice_fusion.2
  48.9 0.2 copy.76
  49.1 1.6 constant_dynamic-slice_fusion
  50.7 0.2 copy.78
  50.8 0.2 copy.77
  51.0 1.0 pad_maximum_fusion.1.w_t
  52.0 27.9 %attend.1 = (bf16[2048,768]{1,0:T(8,128)(2,1)}, bf16[576,2048]{1,0:T(8,128)(2,1)}, bf16[192,2048]{1,0:T(8,128)(2,1)}, f32[8,2048]{1,0:T(8,128)}) custom-call(s32[1,3]{1,0:T(1,128)} %docs.3, bf16[2048,768]{1,0:T(8,128)(2,1)} %bitcast.73, f32[1,768]{1,0:T(1,128)} %reshape.139.gain, f32[1,768]{1,0:T(1,128)} %reshape.140.shift, ...), custom_call_target="tpu_custom_call" | custom-call | bytes 4036620 | tf_op jit(solution)/shard_map/attend/pallas_call | solution.py:69
  79.9 2.2 copy.88
  82.0 21.7 %swap_att.1 = bf16[4,192,512]{2,1,0:T(8,128)(2,1)} custom-call(bf16[4,192,512]{2,1,0:T(8,128)(2,1)} %bitcast.85), custom_call_target="tpu_custom_call" | custom-call | tf_op jit(solution)/shard_map/swap_att/pallas_call | solution.py:127
  103.7 7.8 %middle.1 = (f32[512,768]{1,0:T(8,128)}, f32[512,2]{1,0:T(8,128)}, bf16[1280,768]{1,0:T(8,128)(2,1)}, f32[8,8,256]{2,1,0:T(8,128)}) custom-call(bf16[512,768]{1,0:T(8,128)(2,1)} %tokens.3, bf16[768,512]{1,0:T(8,128)(2,1)} %bitcast.77, bf16[768,768]{1,0:T(8,128)(2,1)} %w_out.3, f32[1,768]{1,0:T(1,128)} %reshape.143.gain, f32[1,768]{1,0:T(1,128)} %reshape.144.shift, ...), custom_call_target="tpu_custom_call" | custom-call | bytes 2783232 | tf_op jit(solution)/shard_map/middle/pallas_call | solution.py:69
  111.6 50.1 %dispatch.1 = (bf16[8,160,768]{2,1,0:T(8,128)(2,1)}, f32[8,8,256]{2,1,0:T(8,128)}) custom-call(bf16[8,160,768]{2,1,0:T(8,128)(2,1)} %bitcast.89, f32[8,8,256]{2,1,0:T(8,128)} %get-tuple-element.73.refs_1_), custom_call_target="tpu_custom_call" | custom-call | tf_op jit(solution)/shard_map/dispatch/pallas_call | solution.py:127
  161.8 1.2 copy-done.6
  163.0 35.4 %experts.1 = (bf16[1280,768]{1,0:T(8,128)(2,1)}, bf16[1280,768]{1,0:T(8,128)(2,1)}, f32[8,8,256]{2,1,0:T(8,128)}, bf16[1280,768]{1,0:T(8,128)(2,1)}, bf16[1280,7...) custom-call(bf16[1280,768]{1,0:T(8,128)(2,1)} %bitcast.96, bf16[1280,768]{1,0:T(8,128)(2,1)} %bitcast.86, ...), custom_call_target="tpu_custom_call" | custom-call | flops 24159191040 | bytes 41943040 | tf_op jit(solution)/shard_map/experts/pallas_call | solution.py:767
  198.4 48.4 %collect.1 = (bf16[8,160,768]{2,1,0:T(8,128)(2,1)}, f32[8,8,256]{2,1,0:T(8,128)}) custom-call(bf16[8,160,768]{2,1,0:T(8,128)(2,1)} %bitcast.88, f32[8,8,256]{2,1,0:T(8,128)} %get-tuple-element.80.refs_1_), custom_call_target="tpu_custom_call" | custom-call | tf_op jit(solution)/shard_map/collect/pallas_call | solution.py:127
  246.8 9.8 %convolution_convert_fusion.1 = bf16[768,3072]{1,0:T(8,128)(2,1)S(1)} fusion(bf16[1280,768]{1,0:T(8,128)(2,1)S(1)} %copy-done.19, bf16[1280,3072]{1,0:T(8,128)(2,1)} %get-tuple-element.101), kind=kOutput, calls=%fused_computation.1 | convolution fusion | flops 6042157056 | bytes 14548992 | tf_op jit(solution)/shard_map/dot_general | solution.py:807
  256.7 2.4 copy.87
  259.1 0.0 reduce-scatter.5.cloned.1.call-start
  259.2 1.5 copy-done.20
  260.7 11.6 %convolution_convert_fusion = bf16[3072,768]{1,0:T(8,128)(2,1)} fusion(bf16[1280,3072]{1,0:T(8,128)(2,1)} %get-tuple-element.102, bf16[1280,768]{1,0:T(8,128)(2,1)S(1)} %copy-done.20), kind=kOutput, calls=%fused_computation | convolution fusion | flops 6042157056 | bytes 14548992 | tf_op jit(solution)/shard_map/dot_general | solution.py:808
  272.3 7.4 %all-to-all-start.1 = ((bf16[8,160,768]{2,1,0:T(8,128)(2,1)}), bf16[8,160,768]{2,1,0:T(8,128)(2,1)}, u32[]{:S(2)}, u32[]{:S(2)}) async-start(bf16[8,160,768]{2,1,0:T(8,128)(2,1)} %bitcast.12), calls=%async_computation.1 | async-start | bytes 3932160 | tf_op jit(solution)/shard_map/all_to_all | solution.py:802
  279.7 0.6 compare_reduce_fusion
  280.3 0.6 broadcast_select_fusion
  281.0 14.4 %second.1 = (f32[512,768]{1,0:T(8,128)}, bf16[768,512]{1,0:T(8,128)(2,1)}, bf16[768,768]{1,0:T(8,128)(2,1)}, f32[2,768]{1,0:T(2,128)}, f32[8,768]{1,0:T(8,128)}) custom-call(f32[512,768]{1,0:T(8,128)} %get-tuple-element.69.residual, bf16[512,768]{1,0:T(8,128)(2,1)} %grad.3, bf16[1280,768]{1,0:T(8,128)(2,1)} %bitcast.90, ...), custom_call_target="tpu_custom_call" | custom-call | bytes 6391808 | tf_op jit(solution)/shard_map/second/pallas_call | solution.py:69
  295.4 20.8 %swap_datt.1 = bf16[4,192,512]{2,1,0:T(8,128)(2,1)} custom-call(bf16[4,192,512]{2,1,0:T(8,128)(2,1)} %bitcast.94), custom_call_target="tpu_custom_call" | custom-call | tf_op jit(solution)/shard_map/swap_datt/pallas_call | solution.py:127
  316.2 2.1 copy.84
  318.3 30.7 %attend_back.1 = (bf16[2048,768]{1,0:T(8,128)(2,1)}, bf16[576,768]{1,0:T(8,128)(2,1)}, f32[2,768]{1,0:T(2,128)}) custom-call(s32[1,3]{1,0:T(1,128)} %docs.3, bf16[2048,768]{1,0:T(8,128)(2,1)} %bitcast.74, f32[1,768]{1,0:T(1,128)} %reshape.139.gain, bf16[2048,768]{1,0:T(8,128)(2,1)} %get-tuple-element.89.h_one, bf16[576,2048]{1,0:T(8,128)(2,1)} %get-tuple-element.90.qkv_t, ...), custom_call_target="tpu_custom_call" | custom-call | bytes 11176972 | tf_op jit(solution)/shard_map/attend_back/pallas_call | solution.py:69
  349.1 2.0 copy-done.3
  351.1 50.3 %sum_dh.1.d_hidden = f32[512,768]{1,0:T(8,128)S(1)} custom-call(bf16[4,512,768]{2,1,0:T(8,128)(2,1)S(1)} %bitcast.71), custom_call_target="tpu_custom_call" | custom-call | tf_op jit(solution)/shard_map/sum_dh/pallas_call | solution.py:255
  401.4 1.1 copy-done.2
  402.6 0.6 pad.7.x
  403.2 15.9 %total.1 = f32[16,768]{1,0:T(8,128)} custom-call(f32[16,768]{1,0:T(8,128)} %pad.7.x), custom_call_target="tpu_custom_call" | custom-call | tf_op jit(solution)/shard_map/total/pallas_call | solution.py:217
  419.1 15.3 %sum_wout.1 = bf16[192,768]{1,0:T(8,128)(2,1)S(1)} custom-call(bf16[4,192,768]{2,1,0:T(8,128)(2,1)S(1)} %bitcast.72), custom_call_target="tpu_custom_call" | custom-call | tf_op jit(solution)/shard_map/sum_wout/pallas_call | solution.py:255
  434.4 0.1 pad_maximum_fusion
  434.5 29.5 %sum_w.1.x = bf16[96,768]{1,0:T(8,128)(2,1)S(1)} custom-call(bf16[8,96,768]{2,1,0:T(8,128)(2,1)S(1)} %bitcast.70), custom_call_target="tpu_custom_call" | custom-call | tf_op jit(solution)/shard_map/sum_w/pallas_call | solution.py:255
  464.0 0.7 copy-done.5
  464.7 29.9 %spread_expert.1 = bf16[8,96,768]{2,1,0:T(8,128)(2,1)} custom-call(bf16[96,768]{1,0:T(8,128)(2,1)} %copy-done.5), custom_call_target="tpu_custom_call" | custom-call | tf_op jit(solution)/shard_map/spread_expert/pallas_call | solution.py:933
  494.6 38.5 %spread_hidden.1 = bf16[4,768,768]{2,1,0:T(8,128)(2,1)} custom-call(bf16[768,768]{1,0:T(8,128)(2,1)} %bitcast.81), custom_call_target="tpu_custom_call" | custom-call | tf_op jit(solution)/shard_map/spread_hidden/pallas_call | solution.py:177
  533.1 4.1 fusion.2
  537.2 0.2 convert_bitcast_fusion.1
  537.5 2.0 copy.74
  539.4 1.4 convert_bitcast_fusion.2
  540.9 2.0 copy.73
  542.8 1.4 convert_bitcast_fusion
  544.3 2.0 copy.75
  546.2 4.0 input_grad.1
  550.2 0.6 slice_reduce_fusion
  550.8 0.5 multiply_bitcast_fusion
  551.3 0.6 slice_bitcast_fusion
  551.9 1.7 bitcast_convert_fusion
  553.6 5.3 output.1
  558.9 2.9 convert_multiply_fusion.1
  561.8 2.8 convert_multiply_fusion
  (48 shorter events, 0.2 us)
Async XLA Ops:
  7.2 41.6 %copy-start = (bf16[768,768]{1,0:T(8,128)(2,1)S(1)}, bf16[768,768]{1,0:T(8,128)(2,1)}, u32[]{:S(2)}) copy-start(bf16[768,768]{1,0:T(8,128)(2,1)} %param.22) | copy-start | bytes 3538948
  7.2 154.6 %all-gather.3.cloned.1.call-start = ((), (), s32[]{:S(2)}) async-start(), calls=%async_computation.4 | async-start | bytes 5898240 | tf_op jit(solution)/shard_map/all_gather | solution.py:705
  34.0 0.8 copy-start.10
  34.0 127.8 %all-gather.5.cloned.1.call-start = ((), (), s32[]{:S(2)}) async-start(), calls=%async_computation.5 | async-start | bytes 5898240 | tf_op jit(solution)/shard_map/all_gather | solution.py:706
  39.8 5.8 %copy-start.14 = (f32[768]{0:T(1024)S(1)}, f32[768]{0:T(1024)}, u32[]{:S(2)}) copy-start(f32[768]{0:T(1024)} %param.20) | copy-start | bytes 9220
  39.8 6.3 %copy-start.15 = (f32[768]{0:T(1024)S(1)}, f32[768]{0:T(1024)}, u32[]{:S(2)}) copy-start(f32[768]{0:T(1024)} %param.26) | copy-start | bytes 9220
  39.8 6.9 %copy-start.16 = (f32[768]{0:T(1024)S(1)}, f32[768]{0:T(1024)}, u32[]{:S(2)}) copy-start(f32[768]{0:T(1024)} %param.27) | copy-start | bytes 9220
  39.9 7.5 %copy-start.17 = (f32[768]{0:T(1024)S(1)}, f32[768]{0:T(1024)}, u32[]{:S(2)}) copy-start(f32[768]{0:T(1024)} %param.21) | copy-start | bytes 9220
  39.9 8.1 %copy-start.11 = (bf16[768,8]{0,1:T(8,128)(2,1)S(1)}, bf16[768,8]{0,1:T(8,128)(2,1)}, u32[]{:S(2)}) copy-start(bf16[768,8]{0,1:T(8,128)(2,1)} %param.28) | copy-start | bytes 36868
  39.9 121.9 %all-to-all-start = ((bf16[8,160,768]{2,1,0:T(8,128)(2,1)}), bf16[8,160,768]{2,1,0:T(8,128)(2,1)S(1)}, u32[]{:S(2)}, u32[]{:S(2)}) async-start(bf16[8,160,768]{2,1,0:T(8,128)(2,1)} %bitcast.87), calls=%async_computation | async-start | bytes 3932160 | tf_op jit(solution)/shard_map/all_to_all | solution.py:699
  45.6 513.3 %reduce-scatter.3.cloned.1.call-start = ((), (), s32[]{:S(2)}) async-start(), calls=%async_computation.6 | async-start | bytes 5898240 | tf_op jit(solution)/shard_map/reduce_scatter | solution.py:811
  161.7 1.3 copy-start.6
  198.4 48.4 %copy-start.19 = (bf16[1280,768]{1,0:T(8,128)(2,1)S(1)}, bf16[1280,768]{1,0:T(8,128)(2,1)}, u32[]{:S(2)}) copy-start(bf16[1280,768]{1,0:T(8,128)(2,1)} %get-tuple-element.100) | copy-start | bytes 5898244
  259.1 1.5 copy-start.20
  259.1 302.7 %reduce-scatter.5.cloned.1.call-start = ((), (), s32[]{:S(2)}) async-start(), calls=%async_computation.7 | async-start | bytes 5898240 | tf_op jit(solution)/shard_map/reduce_scatter | solution.py:812
  272.2 8.1 %copy-start.18 = (f32[1,128]{1,0:T(1,128)S(1)}, f32[1,128]{1,0:T(1,128)}, u32[]{:S(2)}) copy-start(f32[1,128]{1,0:T(1,128)} %get-tuple-element.96) | copy-start | bytes 1540
  272.3 281.3 %all-to-all-start.1 = ((bf16[8,160,768]{2,1,0:T(8,128)(2,1)}), bf16[8,160,768]{2,1,0:T(8,128)(2,1)}, u32[]{:S(2)}, u32[]{:S(2)}) async-start(bf16[8,160,768]{2,1,0:T(8,128)(2,1)} %bitcast.12), calls=%async_computation.1 | async-start | bytes 3932160 | tf_op jit(solution)/shard_map/all_to_all | solution.py:802
  349.1 2.0 copy-start.3
  351.0 51.5 %copy-start.9 = (f32[8,768]{1,0:T(8,128)S(1)}, f32[8,768]{1,0:T(8,128)}, u32[]{:S(2)}) copy-start(f32[8,768]{1,0:T(8,128)} %get-tuple-element.97) | copy-start | bytes 73732
  351.1 51.5 %copy-start.12 = (f32[2,768]{1,0:T(2,128)S(1)}, f32[2,768]{1,0:T(2,128)}, u32[]{:S(2)}) copy-start(f32[2,768]{1,0:T(2,128)} %get-tuple-element.95) | copy-start | bytes 18436
  351.1 51.5 %copy-start.13 = (f32[2,768]{1,0:T(2,128)S(1)}, f32[2,768]{1,0:T(2,128)}, u32[]{:S(2)}) copy-start(f32[2,768]{1,0:T(2,128)} %get-tuple-element.94) | copy-start | bytes 18436
  351.1 68.0 %copy-start.4 = (bf16[768,768]{1,0:T(8,128)(2,1)S(1)}, bf16[768,768]{1,0:T(8,128)(2,1)}, u32[]{:S(2)}) copy-start(bf16[768,768]{1,0:T(8,128)(2,1)} %get-tuple-element.99) | copy-start | bytes 3538948
  401.4 1.1 copy-start.2
  402.5 31.9 %copy-start.7 = (bf16[576,768]{1,0:T(8,128)(2,1)S(1)}, bf16[576,768]{1,0:T(8,128)(2,1)}, u32[]{:S(2)}) copy-start(bf16[576,768]{1,0:T(8,128)(2,1)} %get-tuple-element.98) | copy-start | bytes 2654212
  464.0 0.7 copy-start.5
  546.2 4.0 copy-start.8
  558.9 5.8 %copy-start.1 = (bf16[768,768]{1,0:T(8,128)(2,1)S(1)}, bf16[768,768]{1,0:T(8,128)(2,1)}, u32[]{:S(2)}) copy-start(bf16[768,768]{1,0:T(8,128)(2,1)} %param.22) | copy-start | bytes 3538948
Sparse Core Ops, SparseCore 0:
  34.1 38.3 all-gather.2
  74.0 45.8 all-gather.4
  259.3 59.0 reduce-scatter.2
  320.9 61.5 reduce-scatter.4

commit v2 on v1

--- a/solution.py
+++ b/solution.py
@@ -188,50 +188,6 @@
     )(x)
 
 
-def total_body(sizes, x, o, first, second, s1, r1, s2, r2):
-    along = ("hidden", "expert")
-    me = [lax.axis_index(axis) for axis in along]
-    peers = [
-        [{axis: lax.rem(me[n] + step, sizes[n])} for step in range(1, sizes[n])]
-        for n, axis in enumerate(along)
-    ]
-    greet(peers[0] + peers[1])
-    held = x
-    for n, (box, send, recv) in enumerate(((first, s1, r1), (second, s2, r2))):
-        copies = []
-        for at, peer in enumerate(peers[n]):
-            copy = remote(held, box.at[at], send.at[at], recv.at[at], peer)
-            copy.start()
-            copies.append(copy)
-        for copy in copies:
-            copy.wait()
-        summed = held[...]
-        for at in range(sizes[n] - 1):
-            summed = summed + box[at]
-        o[...] = summed
-        held = o
-
-
-def total_all(x, name, cid):
-    sizes = (lax.axis_size("hidden"), lax.axis_size("expert"))
-    return pl.pallas_call(
-        partial(total_body, sizes),
-        name=name,
-        out_shape=shape_of(x.shape, x.dtype),
-        in_specs=[VMEM],
-        out_specs=VMEM,
-        scratch_shapes=[
-            pltpu.VMEM((sizes[0] - 1, *x.shape), x.dtype),
-            pltpu.VMEM((sizes[1] - 1, *x.shape), x.dtype),
-            DMA((sizes[0] - 1,)),
-            DMA((sizes[0] - 1,)),
-            DMA((sizes[1] - 1,)),
-            DMA((sizes[1] - 1,)),
-        ],
-        compiler_params=pltpu.CompilerParams(collective_id=cid, has_side_effects=True),
-    )(x)
-
-
 def sum_scatter_body(axis, size, x, o, box, send, recv):
     me = lax.axis_index(axis)
     peers = [lax.rem(me + step, size) for step in range(1, size)]
@@ -267,6 +223,598 @@
             collective_id=cid, has_side_effects=True, vmem_limit_bytes=40 << 20
         ),
     )(x)
+
+
+def moe_body(
+    size,
+    capacity,
+    padded,
+    per,
+    x_slots,
+    gate_rows,
+    g_in,
+    ups,
+    downs,
+    dx_back,
+    dg_back,
+    y_out,
+    up_part,
+    down_part,
+    xv,
+    gv,
+    gates_v,
+    up_v,
+    down_v,
+    act,
+    dz,
+    xg,
+    dy,
+    xg_t,
+    dy_t,
+    dxv,
+    yv,
+    dgv,
+    y_acc,
+    dx_acc,
+    load_sem,
+    g_sem,
+    own_sem,
+    xs_sem,
+    xr_sem,
+    gs_sem,
+    gr_sem,
+    ds_sem,
+    dr_sem,
+    ts_sem,
+    tr_sem,
+    out_sem,
+):
+    me = lax.axis_index("expert")
+    shards_n = ups.shape[0]
+    tall = per * capacity
+    steps = size // per
+
+    def to_peer(p):
+        return lax.rem(me + 3 * p, size)
+
+    def from_peer(p):
+        return lax.rem(me + 3 * (size - p), size)
+
+    def rows_of(p):
+        return pl.ds(pl.multiple_of(p * capacity, capacity), capacity)
+
+    def send_x(p):
+        peer = to_peer(p)
+        return remote(
+            x_slots.at[peer], xv.at[rows_of(p)], xs_sem.at[p], xr_sem.at[p], {"expert": peer}
+        )
+
+    def send_gate(p):
+        peer = to_peer(p)
+        return remote(
+            gate_rows.at[peer], gates_v.at[p], gs_sem.at[p], gr_sem.at[p], {"expert": peer}
+        )
+
+    def send_dx(p):
+        peer = from_peer(p)
+        return remote(
+            dxv.at[rows_of(p)], dx_back.at[me], ds_sem.at[p], dr_sem.at[p], {"expert": peer}
+        )
+
+    def send_dg(p):
+        peer = from_peer(p)
+        return remote(dgv.at[p], dg_back.at[me], ts_sem.at[p], tr_sem.at[p], {"expert": peer})
+
+    def load_g(p):
+        return pltpu.make_async_copy(g_in.at[from_peer(p)], gv.at[rows_of(p)], g_sem.at[p])
+
+    def save_y(p):
+        return pltpu.make_async_copy(yv.at[rows_of(p)], y_out.at[from_peer(p)], out_sem.at[p])
+
+    own_x = pltpu.make_async_copy(x_slots.at[me], xv.at[rows_of(0)], own_sem.at[0])
+    own_gate = pltpu.make_async_copy(gate_rows.at[me], gates_v.at[0], own_sem.at[1])
+    own_dx = pltpu.make_async_copy(dxv.at[rows_of(0)], dx_back.at[me], own_sem.at[2])
+    own_dg = pltpu.make_async_copy(dgv.at[0], dg_back.at[me], own_sem.at[3])
+    loads = [pltpu.make_async_copy(ups, up_v, load_sem.at[0])]
+    loads += [pltpu.make_async_copy(downs, down_v, load_sem.at[1])]
+    own_x.start()
+    own_gate.start()
+    for p in range(size):
+        load_g(p).start()
+    for load in loads:
+        load.start()
+    greet([{"expert": lax.rem(me + step, size)} for step in range(1, size)])
+    for p in range(1, size):
+        send_x(p).start()
+        send_gate(p).start()
+    own_x.wait()
+    own_gate.wait()
+    for load in loads:
+        load.wait()
+
+    def step_body(step, _):
+        base = step * per
+        for s in range(per):
+
+            @pl.when(base + s > 0)
+            def _arrive(s=s):
+                send_x(base + s).wait_recv()
+                send_gate(base + s).wait_recv()
+
+            load_g(base + s).wait()
+        rows = pl.ds(pl.multiple_of(step * tall, tall), tall)
+        x, g = xv[rows, :], gv[rows, :]
+        y_acc[...] = jnp.zeros_like(y_acc)
+        dx_acc[...] = jnp.zeros_like(dx_acc)
+
+        def shard_body(c, _):
+            z = mm(x, up_v[c])
+            du = mm_nt(g, down_v[c])
+            square = z * z
+            t = jnp.tanh(z * (GELU_A + GELU_A * GELU_B * square))
+            plus = 0.5 + 0.5 * t
+            hidden = (z * plus).astype(BF)
+            slope = plus + 0.5 * z * (1.0 - t * t) * (GELU_A + 3.0 * GELU_A * GELU_B * square)
+            back = (slope * du).astype(BF)
+            act[c, rows, :] = hidden
+            dz[c, rows, :] = back
+            y_acc[...] += mm(hidden, down_v[c])
+            dx_acc[...] += mm_nt(back, up_v[c])
+            return 0
+
+        lax.fori_loop(0, shards_n, shard_body, 0)
+        dxv[rows, :] = dx_acc[...].astype(BF)
+        y_low = y_acc[...].astype(BF)
+        yv[rows, :] = y_low
+        dots = jnp.sum(y_low.astype(F32) * g.astype(F32), axis=1, keepdims=True)
+        for s in range(per):
+            p = base + s
+            part = slice(s * capacity, (s + 1) * capacity)
+            tall_dots = jnp.broadcast_to(dots[part], (capacity, LANES))
+            if padded > capacity:
+                blank = jnp.zeros((padded - capacity, LANES), F32)
+                tall_dots = jnp.concatenate([tall_dots, blank], axis=0)
+            dgv[p] = tall_dots.T[0:8]
+
+            @pl.when(p > 0)
+            def _give(p=p):
+                send_dx(p).start()
+                send_dg(p).start()
+
+            @pl.when(p == 0)
+            def _keep():
+                own_dx.start()
+                own_dg.start()
+
+            save_y(p).start()
+        for s in range(per):
+            p = base + s
+            part = slice(s * capacity, (s + 1) * capacity)
+            gate = gates_v[p].T[0:capacity, 0:1]
+            xg[rows_of(p), :] = (x[part].astype(F32) * gate).astype(BF)
+            dy[rows_of(p), :] = (g[part].astype(F32) * gate).astype(BF)
+        return 0
+
+    lax.fori_loop(0, steps, step_body, 0)
+
+    total = size * capacity
+    turn = 256
+    for k in range(total // turn):
+        rows = slice(k * turn, (k + 1) * turn)
+        xg_t[:, rows] = xg[rows, :].astype(F32).T.astype(BF)
+        dy_t[:, rows] = dy[rows, :].astype(F32).T.astype(BF)
+    model = xg_t.shape[0]
+    bands = model // turn
+
+    def weight_body(n, _):
+        c, band = n // bands, lax.rem(n, bands)
+        lines = pl.ds(pl.multiple_of(band * turn, turn), turn)
+        up_v[c, lines, :] = mm(xg_t[lines, :], dz[c]).astype(BF)
+        down_v[c, lines, :] = mm(dy_t[lines, :], act[c]).astype(BF)
+        return 0
+
+    lax.fori_loop(0, shards_n * bands, weight_body, 0)
+    keep_up = pltpu.make_async_copy(up_v, up_part, load_sem.at[0])
+    keep_down = pltpu.make_async_copy(down_v, down_part, load_sem.at[1])
+    keep_up.start()
+    keep_down.start()
+    for p in range(1, size):
+        send_x(p).wait_send()
+        send_gate(p).wait_send()
+        send_dx(p).wait()
+        send_dg(p).wait()
+    for p in range(size):
+        save_y(p).wait()
+    own_dx.wait()
+    own_dg.wait()
+    keep_up.wait()
+    keep_down.wait()
+
+
+def run_experts(x_slots, gate_rows, g_in, ups, downs, cid):
+    size = lax.axis_size("expert")
+    experts, capacity, model = x_slots.shape
+    padded = gate_rows.shape[2]
+    shards_n, _unused, width = ups.shape
+    total = experts * capacity
+    per = 1
+    while per * 2 * capacity <= 320 and size % (per * 2) == 0:
+        per *= 2
+    tall = per * capacity
+    rows2 = (total, model)
+    return pl.pallas_call(
+        partial(moe_body, size, capacity, padded, per),
+        name="experts",
+        out_shape=[
+            shape_of(x_slots.shape, BF),
+            shape_of(gate_rows.shape, F32),
+            shape_of(x_slots.shape, BF),
+            shape_of((shards_n, model, width), BF),
+            shape_of((shards_n, model, width), BF),
+        ],
+        in_specs=[ANY] * 5,
+        out_specs=[ANY] * 5,
+        scratch_shapes=[
+            pltpu.VMEM(rows2, BF),
+            pltpu.VMEM(rows2, BF),
+            pltpu.VMEM(gate_rows.shape, F32),
+            pltpu.VMEM((shards_n, model, width), BF),
+            pltpu.VMEM((shards_n, width, model), BF),
+            pltpu.VMEM((shards_n, total, width), BF),
+            pltpu.VMEM((shards_n, total, width), BF),
+            pltpu.VMEM(rows2, BF),
+            pltpu.VMEM(rows2, BF),
+            pltpu.VMEM((model, total), BF),
+            pltpu.VMEM((model, total), BF),
+            pltpu.VMEM(rows2, BF),
+            pltpu.VMEM(rows2, BF),
+            pltpu.VMEM(gate_rows.shape, F32),
+            pltpu.VMEM((tall, model), F32),
+            pltpu.VMEM((tall, model), F32),
+            DMA((2,)),
+            DMA((size,)),
+            DMA((4,)),
+        ]
+        + [DMA((size,))] * 9,
+        compiler_params=pltpu.CompilerParams(
+            collective_id=cid, has_side_effects=True, vmem_limit_bytes=60 << 20
+        ),
+        cost_estimate=pl.CostEstimate(
+            flops=12 * total * model * width * shards_n, bytes_accessed=40 << 20, transcendentals=0
+        ),
+    )(x_slots, gate_rows, g_in, ups, downs)
+
+
+def tail_body(
+    n_e,
+    n_h,
+    chunks,
+    dh,
+    w_all,
+    small,
+    tokens,
+    gain,
+    d_res,
+    residual,
+    gates,
+    pos,
+    y_back,
+    input_grad,
+    output,
+    full,
+    total,
+    mine,
+    beside,
+    across,
+    passing,
+    w_box,
+    piece,
+    small_mid,
+    small_h,
+    small_e,
+    mine_sem,
+    cs_sem,
+    cr_sem,
+    as_sem,
+    ar_sem,
+    ws_sem,
+    wr_sem,
+    hs_sem,
+    hr_sem,
+    es_sem,
+    er_sem,
+    keep_sem,
+    zs_sem,
+    zr_sem,
+    xs_sem,
+    xr_sem,
+    ys_sem,
+    yr_sem,
+    ms_sem,
+    mr_sem,
+):
+    e, h = lax.axis_index("expert"), lax.axis_index("hidden")
+    far, high = n_h // 2, n_e // 2
+    pair, core = h // 2, lax.rem(h, 2)
+    eh, el = e // 2, lax.rem(e, 2)
+    mate = pair * 2 + 1 - core
+    greet(
+        [{"expert": lax.rem(e + step, n_e)} for step in range(1, n_e)]
+        + [{"hidden": lax.rem(h + step, n_h)} for step in range(1, n_h)]
+    )
+    w_sends = []
+    for at in range(n_e - 1):
+        peer = lax.rem(e + 1 + at, n_e)
+        copy = remote(
+            w_all.at[peer], w_box.at[at], ws_sem.at[at], wr_sem.at[at], {"expert": peer}
+        )
+        copy.start()
+        w_sends.append(copy)
+    rows = dh.shape[1] // chunks
+    core_sends = {}
+    for step in list(range(1, far)) + [0]:
+        there = lax.rem(pair + step, far)
+        for k in range(chunks):
+            part = pl.ds(k * rows, rows)
+            copy = remote(
+                dh.at[there * 2 + 1 - core, part],
+                beside.at[step, part],
+                cs_sem.at[step, k],
+                cr_sem.at[step, k],
+                {"hidden": mate},
+            )
+            copy.start()
+            core_sends[step, k] = copy
+    loads = []
+    for step in range(far):
+        there = lax.rem(pair + step, far)
+        load = pltpu.make_async_copy(dh.at[there * 2 + core], mine.at[step], mine_sem.at[step])
+        load.start()
+        loads.append(load)
+    small_sends = []
+    for at in range(n_h - 1):
+        peer = lax.rem(h + 1 + at, n_h)
+        copy = remote(small, small_h.at[at], hs_sem.at[at], hr_sem.at[at], {"hidden": peer})
+        copy.start()
+        small_sends.append(copy)
+    for load in loads:
+        load.wait()
+    far_sends = []
+    for step in range(1, far):
+        there = lax.rem(pair + step, far)
+        for k in range(chunks):
+            part = pl.ds(k * rows, rows)
+            core_sends[step, k].wait_recv()
+            both = mine[step, part, :].astype(F32) + beside[step, part, :].astype(F32)
+            passing[step - 1, part, :] = both.astype(BF)
+            copy = remote(
+                passing.at[step - 1, part],
+                across.at[step - 1, part],
+                as_sem.at[step - 1, k],
+                ar_sem.at[step - 1, k],
+                {"hidden": there * 2 + core},
+            )
+            copy.start()
+            far_sends.append(copy)
+    for copy in small_sends:
+        copy.wait_recv()
+    summed = small[...]
+    for at in range(n_h - 1):
+        summed = summed + small_h[at]
+    small_mid[...] = summed
+    small_out = []
+    for at in range(n_e - 1):
+        peer = lax.rem(e + 1 + at, n_e)
+        copy = remote(small_mid, small_e.at[at], es_sem.at[at], er_sem.at[at], {"expert": peer})
+        copy.start()
+        small_out.append(copy)
+    for copy in w_sends:
+        copy.wait_recv()
+    acc = w_all[e].astype(F32)
+    for at in range(n_e - 1):
+        acc = acc + w_box[at].astype(F32)
+    piece[...] = acc.astype(BF)
+    keep = pltpu.make_async_copy(piece, full.at[h, e], keep_sem)
+    keep.start()
+    started = []
+
+    def slot(eh_of, el_of, pair_of, core_of):
+        return full.at[pair_of * 2 + core_of, eh_of * 2 + el_of]
+
+    def back(step, size, place):
+        return lax.rem(place + size - step, size)
+
+    def give_z(source):
+        for s in range(1, high):
+            there = lax.rem(eh + s, high) * 2 + el
+            copy = remote(
+                source, slot(eh, el, pair, core), zs_sem.at[s], zr_sem.at[s], {"expert": there}
+            )
+            copy.start()
+            started.append(copy)
+
+    def z_arrival(s):
+        place = slot(back(s, high, eh), el, pair, core)
+        return place, remote(place, place, zs_sem.at[s], zr_sem.at[s], {"expert": e})
+
+    def give_x(source, s):
+        target = slot(back(s, high, eh), el, pair, core)
+        copy = remote(
+            source, target, xs_sem.at[s], xr_sem.at[s], {"expert": eh * 2 + 1 - el}
+        )
+        copy.start()
+        started.append(copy)
+
+    def x_arrival(s):
+        place = slot(back(s, high, eh), 1 - el, pair, core)
+        return place, remote(place, place, xs_sem.at[s], xr_sem.at[s], {"expert": e})
+
+    def give_y(source, s, flag):
+        target = slot(back(s, high, eh), el if flag == 0 else 1 - el, pair, core)
+        for t in range(1, far):
+            there = lax.rem(pair + t, far) * 2 + core
+            at = 2 * s + flag
+            copy = remote(
+                source, target, ys_sem.at[t, at], yr_sem.at[t, at], {"hidden": there}
+            )
+            copy.start()
+            started.append(copy)
+
+    def y_arrival(t, s, flag):
+        other = el if flag == 0 else 1 - el
+        place = slot(back(s, high, eh), other, back(t, far, pair), core)
+        at = 2 * s + flag
+        return place, remote(place, place, ys_sem.at[t, at], yr_sem.at[t, at], {"hidden": h})
+
+    def give_mate(source, t, s, flag):
+        other = el if flag == 0 else 1 - el
+        target = slot(back(s, high, eh), other, back(t, far, pair), core)
+        at = 2 * s + flag
+        copy = remote(source, target, ms_sem.at[t, at], mr_sem.at[t, at], {"hidden": mate})
+        copy.start()
+        started.append(copy)
+
+    def mate_arrival(t, s, flag):
+        other = el if flag == 0 else 1 - el
+        place = slot(back(s, high, eh), other, back(t, far, pair), 1 - core)
+        at = 2 * s + flag
+        return place, remote(place, place, ms_sem.at[t, at], mr_sem.at[t, at], {"hidden": h})
+
+    give_z(piece)
+    give_x(piece, 0)
+    give_y(piece, 0, 0)
+    give_mate(piece, 0, 0, 0)
+    for s in range(1, high):
+        place, arrival = z_arrival(s)
+        arrival.wait_recv()
+        give_x(place, s)
+        give_y(place, s, 0)
+        give_mate(place, 0, s, 0)
+    for s in range(high):
+        place, arrival = x_arrival(s)
+        arrival.wait_recv()
+        give_y(place, s, 1)
+        give_mate(place, 0, s, 1)
+    place_of = iota((residual.shape[0], y_back.shape[0]), 1)
+    result = residual[...]
+    for j in range(2):
+        pick = (place_of == pos[:, j : j + 1]).astype(BF)
+        result = result + gates[:, j : j + 1] * mm(pick, y_back[...])
+    output[...] = result.astype(BF)
+    for copy in small_out:
+        copy.wait_recv()
+    summed = small_mid[...]
+    for at in range(n_e - 1):
+        summed = summed + small_e[at]
+    total[...] = summed
+    for k in range(chunks):
+        part = pl.ds(k * rows, rows)
+        core_sends[0, k].wait_recv()
+    for copy in far_sends:
+        copy.wait_recv()
+    grad = mine[0].astype(F32) + beside[0].astype(F32)
+    for step in range(far - 1):
+        grad = grad + across[step].astype(F32)
+    normed, inverse = norm_parts(tokens[...].astype(F32))
+    input_grad[...] = (d_res[...] + norm_back(grad, normed, inverse, gain[...])).astype(BF)
+    for t in range(1, far):
+        for s in range(high):
+            for flag in range(2):
+                place, arrival = y_arrival(t, s, flag)
+                arrival.wait_recv()
+                give_mate(place, t, s, flag)
+    for t in range(far):
+        for s in range(high):
+            for flag in range(2):
+                _place, arrival = mate_arrival(t, s, flag)
+                arrival.wait_recv()
+    keep.wait()
+    for copy in started + w_sends + small_sends + small_out + far_sends:
+        copy.wait_send()
+    for copy in core_sends.values():
+        copy.wait_send()
+
+
+def run_tail(dh, w_all, small, tokens, gain, d_res, residual, gates, pos, y_back, cid):
+    n_e, n_h = lax.axis_size("expert"), lax.axis_size("hidden")
+    far, high = n_h // 2, n_e // 2
+    chunks = 4
+    _unused, rows, model = dh.shape
+    piece = w_all.shape[1:]
+    return pl.pallas_call(
+        partial(tail_body, n_e, n_h, chunks),
+        name="tail",
+        out_shape=[
+            shape_of((rows, model), BF),
+            shape_of((rows, model), BF),
+            shape_of((n_h, n_e, *piece), BF),
+            shape_of(small.shape, F32),
+        ],
+        in_specs=[ANY] + [VMEM] * 9,
+        out_specs=[VMEM, VMEM, ANY, VMEM],
+        scratch_shapes=[
+            pltpu.VMEM((far, rows, model), BF),
+            pltpu.VMEM((far, rows, model), BF),
+            pltpu.VMEM((far - 1, rows, model), BF),
+            pltpu.VMEM((far - 1, rows, model), BF),
+            pltpu.VMEM((n_e - 1, *piece), BF),
+            pltpu.VMEM(piece, BF),
+            pltpu.VMEM(small.shape, F32),
+            pltpu.VMEM((n_h - 1, *small.shape), F32),
+            pltpu.VMEM((n_e - 1, *small.shape), F32),
+            DMA((far,)),
+            DMA((far, chunks)),
+            DMA((far, chunks)),
+            DMA((far - 1, chunks)),
+            DMA((far - 1, chunks)),
+            DMA((n_e - 1,)),
+            DMA((n_e - 1,)),
+            DMA((n_h - 1,)),
+            DMA((n_h - 1,)),
+            DMA((n_e - 1,)),
+            DMA((n_e - 1,)),
+            DMA,
+            DMA((high,)),
+            DMA((high,)),
+            DMA((high,)),
+            DMA((high,)),
+            DMA((far, n_e)),
+            DMA((far, n_e)),
+            DMA((far, n_e)),
+            DMA((far, n_e)),
+        ],
+        compiler_params=pltpu.CompilerParams(
+            collective_id=cid, has_side_effects=True, vmem_limit_bytes=56 << 20
+        ),
+    )(dh, w_all, small, tokens, gain, d_res, residual, gates, pos, y_back)
+
+
+def turn_body(width, full, q_out, k_out, v_out, o_out):
+    for n, out in enumerate((q_out, k_out, v_out)):
+        part = full[:, n * width : (n + 1) * width, :].astype(F32)
+        out[...] = part.reshape(-1, part.shape[2]).T
+    part = full[:, 3 * width :, :].astype(F32)
+    o_out[...] = part.reshape(-1, part.shape[2])
+
+
+def turn_weights(full, width):
+    n_h, deep, model = full.shape
+    cols = 256
+    across = pl.BlockSpec((cols, model), lambda i: (i, 0))
+    down = pl.BlockSpec((model, cols), lambda i: (0, i))
+    square = shape_of((model, model), F32)
+    return pl.pallas_call(
+        partial(turn_body, width),
+        name="turn_weights",
+        grid=(model // cols,),
+        out_shape=[square] * 4,
+        in_specs=[pl.BlockSpec((n_h, deep, cols), lambda i: (0, 0, i))],
+        out_specs=[across, across, across, down],
+        compiler_params=pltpu.CompilerParams(
+            dimension_semantics=("arbitrary",), vmem_limit_bytes=40 << 20
+        ),
+        cost_estimate=pl.CostEstimate(flops=0, bytes_accessed=14 << 20, transcendentals=0),
+    )(full)
 
 
 def route_body(experts, capacity, ids, ids_t, grad, pos, pos_t, slot, count, out):
@@ -345,6 +893,7 @@
 
     lax.fori_loop(0, blocks, project, 0)
     lse[...] = jnp.zeros_like(lse)
+    per_device = out_t.shape[2] // BLOCK
 
     def attend(i, _):
         base = i * BLOCK
@@ -383,9 +932,10 @@
             jnp.zeros((HEAD_DIM, BLOCK), F32),
         )
         final = lax.fori_loop(first, i + 1, step, (empty,) * heads)
+        cols = pl.ds(pl.multiple_of(lax.rem(i, per_device) * BLOCK, BLOCK), BLOCK)
         for n in range(heads):
             top, total, acc = final[n]
-            out_t[n * HEAD_DIM : (n + 1) * HEAD_DIM, rows] = (acc / total).astype(BF)
+            out_t[i // per_device, n * HEAD_DIM : (n + 1) * HEAD_DIM, cols] = (acc / total).astype(BF)
             lse[n : n + 1, rows] = top + jnp.log(total)
         return 0
 
@@ -441,43 +991,6 @@
             mix = jnp.where(here, gate[j], mix)
         line = jnp.sum(mix, axis=0, keepdims=True)
         gate_rows[e] = jnp.broadcast_to(line, (8, padded))
-
-
-def experts_body(
-    sources, capacity, padded, xs, gs, gate_rows, ups, downs, y, dx, dg, xg, dy, act, dz
-):
-    rows = xs.shape[0]
-    shards = ups.shape[0]
-    width = ups.shape[2]
-    x, g = xs[...], gs[...]
-    y_acc = jnp.zeros((rows, x.shape[1]), F32)
-    dx_acc = jnp.zeros((rows, x.shape[1]), F32)
-    for c in range(shards):
-        z = mm(x, ups[c])
-        du = mm_nt(g, downs[c])
-        square = z * z
-        t = jnp.tanh(z * (GELU_A + GELU_A * GELU_B * square))
-        plus = 0.5 + 0.5 * t
-        hidden = (z * plus).astype(BF)
-        slope = plus + 0.5 * z * (1.0 - t * t) * (GELU_A + 3.0 * GELU_A * GELU_B * square)
-        back = (slope * du).astype(BF)
-        act[:, c * width : (c + 1) * width] = hidden
-        dz[:, c * width : (c + 1) * width] = back
-        y_acc = y_acc + mm(hidden, downs[c])
-        dx_acc = dx_acc + mm_nt(back, ups[c])
-    y_low = y_acc.astype(BF)
-    y[...] = y_low
-    dx[...] = dx_acc.astype(BF)
-    dots = jnp.sum(y_low.astype(F32) * g.astype(F32), axis=1, keepdims=True)
-    for s in range(sources):
-        part = slice(s * capacity, (s + 1) * capacity)
-        gate = gate_rows[s].T[0:capacity, 0:1]
-        xg[part, :] = (x[part].astype(F32) * gate).astype(BF)
-        dy[part, :] = (g[part].astype(F32) * gate).astype(BF)
-        tall = jnp.broadcast_to(dots[part], (capacity, LANES))
-        if padded > capacity:
-            tall = jnp.concatenate([tall, jnp.zeros((padded - capacity, LANES), F32)], axis=0)
-        dg[s] = tall.T[0:8]
 
 
 def second_body(
@@ -537,16 +1050,6 @@
     w_out_grad[...] = mm(att_t[...], branch).astype(BF)
 
 
-def output_body(residual, gates, pos, y, out):
-    rows, total = residual.shape[0], y.shape[0]
-    place = iota((rows, total), 1)
-    result = residual[...]
-    for j in range(2):
-        pick = (place == pos[:, j : j + 1]).astype(BF)
-        result = result + gates[:, j : j + 1] * mm(pick, y[...])
-    out[...] = result.astype(BF)
-
-
 def backward_body(
     heads,
     docs,
@@ -575,9 +1078,14 @@
     blocks = count // BLOCK
     ends = doc_bounds(docs, docs.shape[1])
     dq_acc[...] = jnp.zeros_like(dq_acc)
+    per_device = out_t.shape[2] // BLOCK
+
+    def cols_of(i):
+        return pl.ds(pl.multiple_of(lax.rem(i, per_device) * BLOCK, BLOCK), BLOCK)
 
     def prepare(i, _):
         rows = pl.ds(pl.multiple_of(i * BLOCK, BLOCK), BLOCK)
+        cols = cols_of(i)
         for n in range(heads):
             lo = n * HEAD_DIM
             here = slice(lo, lo + HEAD_DIM)
@@ -587,7 +1095,8 @@
             values[n, rows, :] = (
                 qkv_t[2 * width + lo : 2 * width + lo + HEAD_DIM, rows].astype(F32).T.astype(BF)
             )
-            product = out_t[here, rows].astype(F32) * d_att_t[here, rows].astype(F32)
+            product = out_t[i // per_device, here, cols].astype(F32)
+            product = product * d_att_t[i // per_device, here, cols].astype(F32)
             dots[n : n + 1, rows] = jnp.sum(product, axis=0, keepdims=True)
         return 0
 
@@ -610,7 +1119,7 @@
             for n in range(heads):
                 here = slice(n * HEAD_DIM, (n + 1) * HEAD_DIM)
                 query = qkv_t[here, rows] * jnp.asarray(SCALE, BF)
-                d_att = d_att_t[here, rows]
+                d_att = d_att_t[i // per_device, here, cols_of(i)]
                 score = mm(keys[n, part, :], query) - lse[n : n + 1, rows]
                 weight = jnp.exp(jnp.where(allowed, score, MASKED))
                 d_weight = mm(values[n, part, :], d_att)
@@ -644,12 +1153,6 @@
 
     lax.fori_loop(0, blocks, finish, 0)
     w_grad[...] = w_acc[...].astype(BF)
-
-
-def input_body(tokens, gain, d_res, d_hidden, out):
-    normed, inverse = norm_parts(tokens[...].astype(F32))
-    grad = d_hidden[...].astype(F32)
-    out[...] = (d_res[...] + norm_back(grad, normed, inverse, gain[...])).astype(BF)
 
 
 def shards(
@@ -673,6 +1176,7 @@
     n_expert, n_hidden = lax.axis_size("expert"), lax.axis_size("hidden")
     experts = n_expert * w_up.shape[0]
     capacity = max(2, rows * 2 * 5 // (4 * experts))
+    capacity = -(-capacity // 16) * 16
     padded = -(-capacity // LANES) * LANES
     total = experts * capacity
     group = rows * n_hidden
@@ -698,7 +1202,7 @@
     )
     g_in = lax.all_to_all(
         g_slots.reshape(experts, capacity, model), "expert", split_axis=0, concat_axis=0, tiled=True
-    ).reshape(total, model)
+    )
 
     all_tokens = gather_hidden(tokens, "gather_tokens", 1).reshape(group, model)
     up_src, down_src, all_tokens = lax.optimization_barrier((w_up, w_down, all_tokens))
@@ -715,7 +1219,7 @@
         [
             shape_of((group, model), BF),
             shape_of((3 * width, group), BF),
-            shape_of((width, group), BF),
+            shape_of((n_hidden, width, rows), BF),
             shape_of((8, group), F32),
         ],
         doc_lengths,
@@ -726,8 +1230,7 @@
         specs=[SMEM, VMEM, VMEM, VMEM, VMEM],
         scratch=[pltpu.VMEM((heads, group, HEAD_DIM), BF)],
     )
-    att_split = att_own.reshape(width, n_hidden, rows).transpose(1, 0, 2)
-    (att_t,) = exchange("hidden", [att_split], "swap_att", 2)
+    (att_t,) = exchange("hidden", [att_own], "swap_att", 2)
     att_t = att_t.reshape(model, rows)
 
     residual, gates, x_slots, gate_rows = local_call(
@@ -749,69 +1252,17 @@
         slot,
         pos_t,
     )
-    x_in, gate_in = exchange(
-        "expert", [x_slots.reshape(experts, capacity, model), gate_rows], "dispatch", 3
-    )
-    x_in = x_in.reshape(total, model)
-
-    per = max(1, 320 // capacity)
-    steps = experts // per
-    tall = per * capacity
-    hidden_units = n_hidden * w_up.shape[2]
-
-    def by_rows(width_of):
-        return pl.BlockSpec((tall, width_of), lambda i: (i, 0))
-
-    whole_w = pl.BlockSpec((n_hidden, *w_up.shape[1:]), lambda i: (0, 0, 0))
-    by_source = pl.BlockSpec((per, 8, padded), lambda i: (i, 0, 0))
-    y_out, dx_out, dg_rows, xg, dy, act, dz = pl.pallas_call(
-        partial(experts_body, per, capacity, padded),
-        name="experts",
-        grid=(steps,),
-        out_shape=[
-            shape_of((total, model), BF),
-            shape_of((total, model), BF),
-            shape_of((experts, 8, padded), F32),
-            shape_of((total, model), BF),
-            shape_of((total, model), BF),
-            shape_of((total, hidden_units), BF),
-            shape_of((total, hidden_units), BF),
-        ],
-        in_specs=[by_rows(model), by_rows(model), by_source, whole_w, whole_w],
-        out_specs=[
-            by_rows(model),
-            by_rows(model),
-            by_source,
-            by_rows(model),
-            by_rows(model),
-            by_rows(hidden_units),
-            by_rows(hidden_units),
-        ],
-        compiler_params=pltpu.CompilerParams(
-            dimension_semantics=("arbitrary",), vmem_limit_bytes=60 << 20
-        ),
-        cost_estimate=pl.CostEstimate(
-            flops=8 * total * model * hidden_units, bytes_accessed=40 << 20, transcendentals=0
-        ),
-    )(x_in, g_in, gate_in, ups, downs)
-
-    dx_back, dg_back = exchange(
-        "expert", [dx_out.reshape(experts, capacity, model), dg_rows], "collect", 4
-    )
-    dx_back, y_out, act, dz = lax.optimization_barrier((dx_back, y_out, act, dz))
-    y_back = lax.all_to_all(
-        y_out.reshape(experts, capacity, model), "expert", split_axis=0, concat_axis=0, tiled=True
-    ).reshape(total, model)
+    dx_back, dg_back, y_out, up_part, down_part = run_experts(
+        x_slots.reshape(experts, capacity, model), gate_rows, g_in, ups, downs, 3
+    )
+    y_back = lax.all_to_all(y_out, "expert", split_axis=0, concat_axis=0, tiled=True)
+    y_back = y_back.reshape(total, model)
 
     trainable = (lax.axis_index("expert") >= experts // 2).astype(F32)
-    up_part = lax.dot_general(xg, dz, (((0,), (0,)), ((), ())), preferred_element_type=F32)
-    down_part = lax.dot_general(act, dy, (((0,), (0,)), ((), ())), preferred_element_type=F32)
-    up_part = up_part.astype(BF).reshape(model, n_hidden, -1).transpose(1, 0, 2)
-    down_part = down_part.astype(BF).reshape(n_hidden, -1, model)
     up_grad = lax.psum_scatter(up_part, "hidden", scatter_dimension=0, tiled=True)
     down_grad = lax.psum_scatter(down_part, "hidden", scatter_dimension=0, tiled=True)
     up_grad = up_grad.astype(F32) * trainable
-    down_grad = down_grad.astype(F32) * trainable
+    down_grad = down_grad.astype(F32).transpose(0, 2, 1) * trainable
 
     d_res, d_att_t, w_out_part, sums_two, router_part = local_call(
         partial(second_body, experts, capacity, padded),
@@ -838,7 +1289,6 @@
         w_router,
     )
     (d_att_in,) = exchange("hidden", [d_att_t.reshape(n_hidden, width, rows)], "swap_datt", 5)
-    d_att_own = d_att_in.transpose(1, 0, 2).reshape(width, group)
 
     d_hidden, w_part, sums_one = local_call(
         partial(backward_body, heads),
@@ -855,7 +1305,7 @@
         qkv_t,
         att_own,
         lse,
-        d_att_own,
+        d_att_in,
         w_t,
         specs=[SMEM] + [VMEM] * 8,
         scratch=[
@@ -869,32 +1319,28 @@
             pltpu.VMEM((3 * width, model), F32),
         ],
     )
-    output = local_call(
-        output_body, "output", shape_of((rows, model), BF), residual, gates, pos, y_back
-    )
-    d_hidden_own = sum_scatter(
-        "hidden", d_hidden.reshape(n_hidden, rows, model), "sum_dh", 6, F32
-    )
-    input_grad = local_call(
-        input_body, "input_grad", shape_of((rows, model), BF), tokens, g1, d_res, d_hidden_own
-    )
-
     w_out_own = sum_scatter(
         "hidden", w_out_part.reshape(n_hidden, width, model), "sum_wout", 7, BF
     )
+
     w_all = jnp.concatenate([w_part, w_out_own], axis=0)
-    piece = sum_scatter(
-        "expert", w_all.reshape(n_expert, 4 * width // n_expert, model), "sum_w", 8, BF
-    )
-    pieces = exchange_all(piece, "spread_expert", 9).reshape(4 * width, model)
-    full = gather_hidden(pieces, "spread_hidden", 10).reshape(n_hidden, 4, width, model)
-    w_grads = [full[:, n].reshape(model, model).T.astype(F32) for n in range(3)]
-    w_out_grad = full[:, 3].reshape(model, model).astype(F32)
     counts = jnp.zeros((1, model), F32).at[:, :experts].set(count[:, :experts])
     small = jnp.concatenate([sums_one, sums_two, counts, router_part], axis=0)
-    short = small.shape[0]
-    small = jnp.pad(small, ((0, -short % 8), (0, 0)))
-    small = total_all(small, "total", 11)
+    small = jnp.pad(small, ((0, -small.shape[0] % 8), (0, 0)))
+    input_grad, output, full, small = run_tail(
+        d_hidden.reshape(n_hidden, rows, model),
+        w_all.reshape(n_expert, 4 * width // n_expert, model),
+        small,
+        tokens,
+        g1,
+        d_res,
+        residual,
+        gates,
+        pos,
+        y_back,
+        8,
+    )
+    w_grads = turn_weights(full.reshape(n_hidden, 4 * width, model), width)
     load = small[4, :experts] * experts / (rows * n_expert * n_hidden * 2)
     return (
         output,
@@ -902,7 +1348,6 @@
         small[0],
         small[1],
         *w_grads,
-        w_out_grad,
         small[2],
         small[3],
         small[5 : 5 + experts].T,
@@ -912,35 +1357,6 @@
     )
 
 
-def spread_body(axis, size, x, o, local_sem, send_sem, recv_sem):
-    me = lax.axis_index(axis)
-    peers = [lax.rem(me + step, size) for step in range(1, size)]
-    greet([{axis: peer} for peer in peers])
-    copies = []
-    for at, peer in enumerate(peers):
-        copy = remote(x, o.at[me], send_sem.at[at], recv_sem.at[at], {axis: peer})
-        copy.start()
-        copies.append(copy)
-    own = pltpu.make_async_copy(x, o.at[me], local_sem)
-    own.start()
-    own.wait()
-    for copy in copies:
-        copy.wait()
-
-
-def exchange_all(x, name, cid):
-    size = lax.axis_size("expert")
-    return pl.pallas_call(
-        partial(spread_body, "expert", size),
-        name=name,
-        out_shape=shape_of((size, *x.shape), x.dtype),
-        in_specs=[ANY],
-        out_specs=ANY,
-        scratch_shapes=[DMA, DMA((size - 1,)), DMA((size - 1,))],
-        compiler_params=pltpu.CompilerParams(collective_id=cid, has_side_effects=True),
-    )(x)
-
-
 def solution(mesh):
     in_specs = (
         P(("expert", "hidden"), None),

time: 581 us -> 427 us (0.73); the launches traced: 572 us -> 428 us
  Pallas kernels: 477 us -> 362 us
  matrix products: 21.4 us -> 0 us
  local copies, waits for them, and re-layouts: 31.3 us -> 15.5 us
  waiting for transfers between devices: 0.79 us -> 7.78 us
    pallas_call x4 -> x2, Pallas kernels: 141 us -> 44.2 us  [exchange(): pl.pallas_call(partial(exchange_body, axis, size, count), name=name, out_...]
    pallas_call x3, Pallas kernels: 81.2 us -> 174 us  [the longest x1 90.8 us: run_experts(): pl.pallas_call(partial(moe_body, size, capacity, padded, per), name='expe...]
    pallas_call x3 -> x1, Pallas kernels: 95.2 us -> 24.1 us  [sum_scatter(): pl.pallas_call(partial(sum_scatter_body, axis, size), name=name, out_shap...]
    pallas_call x2 -> x1, Pallas kernels: 65.2 us -> 26.7 us  [gather_hidden(): pl.pallas_call(partial(gather_body, size, chunks), name=name, out_shape=s...]
    dot_general x2 -> x0, matrix products: 21.4 us -> none  [the longest x1 11.6 us: shards(): lax.dot_general(act, dy, (((0,), (0,)), ((), ())), preferred_element_type...]
    reshape x3 -> x0, local copies, waits for them, and re-layouts: 6.7 us -> none  [the longest x1 2.44 us: shards(): up_part = up_part.astype(BF).reshape(model, n_hidden, -1).transpose(1, 0, 2)]
    all_gather x1, waiting for transfers between devices: 0.02 us -> 6.5 us  [shards(): downs = lax.all_gather(down_src, 'hidden', axis=0, tiled=True)]
    unnamed x50 -> x44, local copies, waits for them, and re-layouts: 14.5 us -> 9.53 us
  transfers between devices with their start and end apart: 6 -> 6, of which waited for: 0 -> 1; matrix products, arithmetic and copies ran while one was open for 8% -> 4% of each run, Pallas kernels for 64% -> 57%
where the time goes in v2:
time: 427 us; the launch traced here: 428 us
  Pallas kernels  362 us (85%)
  starting transfers between devices  17.7 us (4%)
  local copies, waits for them, and re-layouts  15.5 us (4%)
  between operations  14 us (3%)
  other arithmetic  10.2 us (2%)
  waiting for transfers between devices  7.78 us (2%)
    pallas_call x5, Pallas kernels, local_call(): pl.pallas_call(body, name=name, out_shape=outs, in_specs=specs or [VMEM]...  93.3 us
    pallas_call x1, Pallas kernels, run_experts(): pl.pallas_call(partial(moe_body, size, capacity, padded, per), name='expe...  90.8 us
    pallas_call x1, Pallas kernels, run_tail(): pl.pallas_call(partial(tail_body, n_e, n_h, chunks), name='tail', out_sha...  79.5 us
    pallas_call x2, Pallas kernels, exchange(): pl.pallas_call(partial(exchange_body, axis, size, count), name=name, out_...  44.2 us
    pallas_call x1, Pallas kernels, gather_hidden(): pl.pallas_call(partial(gather_body, size, chunks), name=name, out_shape=s...  26.7 us
    pallas_call x1, Pallas kernels, sum_scatter(): pl.pallas_call(partial(sum_scatter_body, axis, size), name=name, out_shap...  24.1 us
    all_to_all x1, starting transfers between devices, shards(): lax.all_to_all(y_out, 'expert', split_axis=0, concat_axis=0, tiled=True)  11.9 us
    unnamed x44, local copies, waits for them, and re-layouts  9.53 us
  transfers between devices with their start and end apart: 6, of which 1 were waited for; matrix products, arithmetic and copies ran while one was open for 4% of the time, Pallas kernels for 57%

profile of v2, /device:TPU:17, one launch (start us, length us, event | category | flops | bytes accessed | tf_op | source)
XLA Modules:
  0.0 427.6 jit_solution(13213424746816008751)
XLA Ops:
  7.2 0.0 copy-start
  7.2 0.0 all-gather.3.cloned.1.call-start
  7.2 26.7 %gather_tokens.1 = bf16[4,512,768]{2,1,0:T(8,128)(2,1)} custom-call(bf16[512,768]{1,0:T(8,128)(2,1)} %tokens.3), custom_call_target="tpu_custom_call" | custom-call | tf_op jit(solution)/shard_map/gather_tokens/pallas_call | solution.py:177
  34.0 0.0 copy-start.10
  34.0 0.0 all-gather.3.cloned.1.call-update
  34.0 0.0 all-gather.5.cloned.1.call-start
  34.0 0.7 all-gather.5.cloned.1.call-update
  34.8 0.9 copy.43.ids
  35.6 4.2 route.1
  39.8 0.0 copy-start.16
  39.9 0.0 copy-start.11
  39.9 5.7 %all-to-all-start = ((bf16[8,160,768]{2,1,0:T(8,128)(2,1)}), bf16[8,160,768]{2,1,0:T(8,128)(2,1)S(1)}, u32[]{:S(2)}, u32[]{:S(2)}) async-start(bf16[8,160,768]{2,1,0:T(8,128)(2,1)} %bitcast.30), calls=%async_computation | async-start | bytes 3932160 | tf_op jit(solution)/shard_map/all_to_all | solution.py:1203
  45.6 0.0 reduce-scatter.5.cloned.1.call-start
  45.6 0.6 reshape.104.gain
  46.2 0.6 reshape.107.gain
  46.8 0.6 reshape.108.shift
  47.4 0.6 reshape.105.shift
  47.9 0.0 copy-done.11
  48.0 0.8 copy.42.w_router
  48.8 0.0 copy-done
  48.8 0.2 constant_dynamic-slice_fusion.2
  49.0 0.2 copy.47
  49.1 1.6 constant_dynamic-slice_fusion
  50.7 0.2 copy.49
  50.9 0.2 copy.48
  51.0 1.0 pad_maximum_fusion.1.w_t
  52.0 32.1 %attend.1 = (bf16[2048,768]{1,0:T(8,128)(2,1)}, bf16[576,2048]{1,0:T(8,128)(2,1)}, bf16[4,192,512]{2,1,0:T(8,128)(2,1)}, f32[8,2048]{1,0:T(8,128)}) custom-call(s32[1,3]{1,0:T(1,128)} %docs.3, bf16[2048,768]{1,0:T(8,128)(2,1)} %bitcast.23, f32[1,768]{1,0:T(1,128)} %reshape.104.gain, f32[1,768]{1,0:T(1,128)} %reshape.105.shift, ...), custom_call_target="tpu_custom_call" | custom-call | bytes 4036620 | tf_op jit(solution)/shard_map/attend/pallas_call | solution.py:69
  84.1 21.4 %swap_att.1 = bf16[4,192,512]{2,1,0:T(8,128)(2,1)} custom-call(bf16[4,192,512]{2,1,0:T(8,128)(2,1)} %get-tuple-element.66.refs_0_.out_t), custom_call_target="tpu_custom_call" | custom-call | tf_op jit(solution)/shard_map/swap_att/pallas_call | solution.py:127
  105.5 7.9 %middle.1 = (f32[512,768]{1,0:T(8,128)}, f32[512,2]{1,0:T(8,128)}, bf16[1280,768]{1,0:T(8,128)(2,1)}, f32[8,8,256]{2,1,0:T(8,128)}) custom-call(bf16[512,768]{1,0:T(8,128)(2,1)} %tokens.3, bf16[768,512]{1,0:T(8,128)(2,1)} %bitcast.26, bf16[768,768]{1,0:T(8,128)(2,1)} %w_out.3, f32[1,768]{1,0:T(1,128)} %reshape.107.gain, f32[1,768]{1,0:T(1,128)} %reshape.108.shift, ...), custom_call_target="tpu_custom_call" | custom-call | bytes 2783232 | tf_op jit(solution)/shard_map/middle/pallas_call | solution.py:69
  113.4 0.0 all-to-all-done.g_in
  113.4 0.0 all-gather.3.cloned.1.call-done.ups
  113.4 6.5 %all-gather.5.cloned.1.call-done.downs = bf16[4,768,768]{2,1,0:T(8,128)(2,1)} async-done(((bf16[1,768,768]{2,1,0:T(8,128)(2,1)}), bf16[4,768,768]{2,1,0:T(8,128)(2,1)}) %all-gather.5.cloned.1.call-update) | async-done | bytes 4718608 | tf_op jit(solution)/shard_map/all_gather | solution.py:1210
  119.9 90.8 %experts.1 = (bf16[8,160,768]{2,1,0:T(8,128)(2,1)}, f32[8,8,256]{2,1,0:T(8,128)}, bf16[8,160,768]{2,1,0:T(8,128)(2,1)}, bf16[4,768,768]{2,1,0:T(8,128)(2,1)}, bf16[4,768,768]{2,1,0:T(8,128)(2,1)}) custom-call(bf16[8,160,768]{2,1,0:T(8,128)(2,1)} %bitcast.37, f32[8,8,256]{2,1,0:T(8,128)} %get-tuple-element.72.gate_rows, bf16[8,160,768]{2,1,0:T(8,128)(2,1)} %copy-done.5, ...), custom_call_target="tpu_custom_call" | custom-call | flops 36238786560 | bytes 41943040 | tf_op jit(solution)/shard_map/experts/pallas_call | solution.py:445
  210.7 0.0 reduce-scatter.5.cloned.1.call-update
  210.7 0.0 reduce-scatter.3.cloned.1.call-start
  210.8 0.5 reduce-scatter.3.cloned.1.call-update
  211.3 0.0 copy-start.17
  211.3 11.9 %all-to-all-start.1 = ((bf16[8,160,768]{2,1,0:T(8,128)(2,1)}), bf16[8,160,768]{2,1,0:T(8,128)(2,1)S(1)}, u32[]{:S(2)}, u32[]{:S(2)}) async-start(bf16[8,160,768]{2,1,0:T(8,128)(2,1)} %get-tuple-element.89), calls=%async_computation.1 | async-start | bytes 3932160 | tf_op jit(solution)/shard_map/all_to_all | solution.py:1258
  223.2 0.6 compare_reduce_fusion
  223.9 0.7 broadcast_select_fusion
  224.5 14.6 %second.1 = (f32[512,768]{1,0:T(8,128)}, bf16[768,512]{1,0:T(8,128)(2,1)}, bf16[768,768]{1,0:T(8,128)(2,1)}, f32[2,768]{1,0:T(2,128)}, f32[8,768]{1,0:T(8,128)}) custom-call(f32[512,768]{1,0:T(8,128)} %get-tuple-element.70.residual, bf16[512,768]{1,0:T(8,128)(2,1)} %grad.3, bf16[1280,768]{1,0:T(8,128)(2,1)} %bitcast.31, ...), custom_call_target="tpu_custom_call" | custom-call | bytes 6391808 | tf_op jit(solution)/shard_map/second/pallas_call | solution.py:69
  239.1 22.8 %swap_datt.1.d_att_t = bf16[4,192,512]{2,1,0:T(8,128)(2,1)} custom-call(bf16[4,192,512]{2,1,0:T(8,128)(2,1)} %bitcast.35), custom_call_target="tpu_custom_call" | custom-call | tf_op jit(solution)/shard_map/swap_datt/pallas_call | solution.py:127
  261.9 24.1 %sum_wout.1 = bf16[192,768]{1,0:T(8,128)(2,1)S(1)} custom-call(bf16[4,192,768]{2,1,0:T(8,128)(2,1)S(1)} %bitcast.22), custom_call_target="tpu_custom_call" | custom-call | tf_op jit(solution)/shard_map/sum_wout/pallas_call | solution.py:211
  286.0 0.0 copy-start.9
  286.0 34.5 %attend_back.1 = (bf16[2048,768]{1,0:T(8,128)(2,1)}, bf16[576,768]{1,0:T(8,128)(2,1)}, f32[2,768]{1,0:T(2,128)}) custom-call(s32[1,3]{1,0:T(1,128)} %docs.3, bf16[2048,768]{1,0:T(8,128)(2,1)} %bitcast.24, f32[1,768]{1,0:T(1,128)} %reshape.104.gain, bf16[2048,768]{1,0:T(8,128)(2,1)} %get-tuple-element.64.h_one, bf16[576,2048]{1,0:T(8,128)(2,1)} %get-tuple-element.65.qkv_t, ...), custom_call_target="tpu_custom_call" | custom-call | bytes 11176972 | tf_op jit(solution)/shard_map/attend_back/pallas_call | solution.py:69
  320.5 0.0 copy-done.12
  320.5 0.7 fusion
  321.2 0.6 pad.7.small
  321.9 2.3 pad_maximum_fusion
  324.1 0.0 all-to-all-done.1
  324.1 1.3 copy-done.4
  325.4 79.5 %tail.1 = (bf16[512,768]{1,0:T(8,128)(2,1)}, bf16[512,768]{1,0:T(8,128)(2,1)}, bf16[4,8,96,768]{3,2,1,0:T(8,128)(2,1)}, f32[16,768]{1,0:T(8,128)}) custom-call(bf16[4,512,768]{2,1,0:T(8,128)(2,1)} %bitcast.29, bf16[8,96,768]{2,1,0:T(8,128)(2,1)} %bitcast.28, f32[16,768]{1,0:T(8,128)} %pad.7.small, bf16[512,768]{1,0:T(8,128)(2,1)} %tokens.3, ...), custom_call_target="tpu_custom_call" | custom-call | tf_op jit(solution)/shard_map/tail/pallas_call | solution.py:744
  404.9 0.0 copy-start.2
  404.9 2.3 copy-done.2
  407.2 4.0 turn_weights.1
  411.2 0.6 slice_reduce_fusion
  411.8 0.5 multiply_bitcast_fusion.1
  412.4 0.6 slice_bitcast_fusion
  413.0 1.4 multiply_bitcast_fusion
  414.4 2.0 copy.46
  416.4 3.0 convert_multiply_fusion
  419.3 0.0 copy-done.7
  419.3 0.9 copy.52
  420.2 0.9 copy.53
  (25 shorter events, 0.0 us)
Async XLA Ops:
  7.2 41.6 %copy-start = (bf16[768,768]{1,0:T(8,128)(2,1)S(1)}, bf16[768,768]{1,0:T(8,128)(2,1)}, u32[]{:S(2)}) copy-start(bf16[768,768]{1,0:T(8,128)(2,1)} %param.22) | copy-start | bytes 3538948
  7.2 106.2 %all-gather.3.cloned.1.call-start = ((), (), s32[]{:S(2)}) async-start(), calls=%async_computation.4 | async-start | bytes 5898240 | tf_op jit(solution)/shard_map/all_gather | solution.py:1209
  34.0 0.8 copy-start.10
  34.0 85.9 %all-gather.5.cloned.1.call-start = ((), (), s32[]{:S(2)}) async-start(), calls=%async_computation.5 | async-start | bytes 5898240 | tf_op jit(solution)/shard_map/all_gather | solution.py:1210
  39.8 5.8 %copy-start.13 = (f32[768]{0:T(1024)S(1)}, f32[768]{0:T(1024)}, u32[]{:S(2)}) copy-start(f32[768]{0:T(1024)} %param.20) | copy-start | bytes 9220
  39.8 6.3 %copy-start.14 = (f32[768]{0:T(1024)S(1)}, f32[768]{0:T(1024)}, u32[]{:S(2)}) copy-start(f32[768]{0:T(1024)} %param.26) | copy-start | bytes 9220
  39.8 6.9 %copy-start.15 = (f32[768]{0:T(1024)S(1)}, f32[768]{0:T(1024)}, u32[]{:S(2)}) copy-start(f32[768]{0:T(1024)} %param.27) | copy-start | bytes 9220
  39.8 7.5 %copy-start.16 = (f32[768]{0:T(1024)S(1)}, f32[768]{0:T(1024)}, u32[]{:S(2)}) copy-start(f32[768]{0:T(1024)} %param.21) | copy-start | bytes 9220
  39.9 8.1 %copy-start.11 = (bf16[768,8]{0,1:T(8,128)(2,1)S(1)}, bf16[768,8]{0,1:T(8,128)(2,1)}, u32[]{:S(2)}) copy-start(bf16[768,8]{0,1:T(8,128)(2,1)} %param.28) | copy-start | bytes 36868
  39.9 73.5 %all-to-all-start = ((bf16[8,160,768]{2,1,0:T(8,128)(2,1)}), bf16[8,160,768]{2,1,0:T(8,128)(2,1)S(1)}, u32[]{:S(2)}, u32[]{:S(2)}) async-start(bf16[8,160,768]{2,1,0:T(8,128)(2,1)} %bitcast.30), calls=%async_computation | async-start | bytes 3932160 | tf_op jit(solution)/shard_map/all_to_all | solution.py:1203
  45.6 367.4 %reduce-scatter.5.cloned.1.call-start = ((), (), s32[]{:S(2)}) async-start(), calls=%async_computation.7 | async-start | bytes 5898240 | tf_op jit(solution)/shard_map/reduce_scatter | solution.py:1263
  113.4 6.5 %copy-start.5 = (bf16[8,160,768]{2,1,0:T(8,128)(2,1)}, bf16[8,160,768]{2,1,0:T(8,128)(2,1)S(1)}, u32[]{:S(2)}) copy-start(bf16[8,160,768]{2,1,0:T(8,128)(2,1)S(1)} %all-to-all-done.g_in) | copy-start | bytes 5898244
  210.7 205.6 %reduce-scatter.3.cloned.1.call-start = ((), (), s32[]{:S(2)}) async-start(), calls=%async_computation.6 | async-start | bytes 5898240 | tf_op jit(solution)/shard_map/reduce_scatter | solution.py:1262
  211.3 12.5 %copy-start.17 = (f32[1,128]{1,0:T(1,128)S(1)}, f32[1,128]{1,0:T(1,128)}, u32[]{:S(2)}) copy-start(f32[1,128]{1,0:T(1,128)} %get-tuple-element.86) | copy-start | bytes 1540
  211.3 112.8 %all-to-all-start.1 = ((bf16[8,160,768]{2,1,0:T(8,128)(2,1)}), bf16[8,160,768]{2,1,0:T(8,128)(2,1)S(1)}, u32[]{:S(2)}, u32[]{:S(2)}) async-start(bf16[8,160,768]{2,1,0:T(8,128)(2,1)} %get-tuple-element.89), calls=%async_computation.1 | async-start | bytes 3932160 | tf_op jit(solution)/shard_map/all_to_all | solution.py:1258
  239.1 22.8 %copy-start.3 = (bf16[768,768]{1,0:T(8,128)(2,1)S(1)}, bf16[768,768]{1,0:T(8,128)(2,1)}, u32[]{:S(2)}) copy-start(bf16[768,768]{1,0:T(8,128)(2,1)} %get-tuple-element.83) | copy-start | bytes 3538948
  286.0 34.5 %copy-start.9 = (f32[8,768]{1,0:T(8,128)S(1)}, f32[8,768]{1,0:T(8,128)}, u32[]{:S(2)}) copy-start(f32[8,768]{1,0:T(8,128)} %get-tuple-element.87) | copy-start | bytes 73732
  286.0 34.5 %copy-start.12 = (f32[2,768]{1,0:T(2,128)S(1)}, f32[2,768]{1,0:T(2,128)}, u32[]{:S(2)}) copy-start(f32[2,768]{1,0:T(2,128)} %get-tuple-element.85) | copy-start | bytes 18436
  324.1 1.3 copy-start.4
  404.9 2.3 copy-start.2
  407.2 4.0 copy-start.8
  416.4 3.0 copy-start.7
  416.4 3.9 copy-start.6
  416.4 4.8 %copy-start.1 = (bf16[768,768]{1,0:T(8,128)(2,1)S(1)}, bf16[768,768]{1,0:T(8,128)(2,1)}, u32[]{:S(2)}) copy-start(bf16[768,768]{1,0:T(8,128)(2,1)} %param.22) | copy-start | bytes 3538948
Sparse Core Ops, SparseCore 0:
  34.1 38.2 all-gather.2
  74.0 45.8 all-gather.4
  210.9 72.2 reduce-scatter.4
  285.7 48.6 reduce-scatter.2

commit v3 on v2

v3 whole, which is shorter than its diff:
```python
from functools import partial

import jax
import jax.numpy as jnp
from jax import lax
from jax.experimental import pallas as pl
from jax.experimental.pallas import tpu as pltpu
from jax.sharding import PartitionSpec as P

HEAD_DIM = 64
HEADS = 12
EPSILON = 1e-05
SCALE = 0.125
MASKED = -1e30
BLOCK = 256
LONGEST = 1024
REACH = LONGEST // BLOCK + 1
LANES = 128
BF = jnp.bfloat16
F32 = jnp.float32
I32 = jnp.int32
MESH = pl.DeviceIdType.MESH
ANY = pl.BlockSpec(memory_space=pl.ANY)
SMEM = pl.BlockSpec(memory_space=pltpu.SMEM)
VMEM = pl.BlockSpec(memory_space=pltpu.VMEM)
DMA = pltpu.SemaphoreType.DMA
GELU_A = 0.7978845608028654
GELU_B = 0.044715


def mm(left, right):
    return jnp.dot(left, right, preferred_element_type=F32)


def mm_nt(left, right):
    return lax.dot_general(left, right, (((1,), (1,)), ((), ())), preferred_element_type=F32)


def mm_tn(left, right):
    return lax.dot_general(left, right, (((0,), (0,)), ((), ())), preferred_element_type=F32)


def iota(shape, axis):
    return lax.broadcasted_iota(I32, shape, axis)


def norm_parts(values):
    centred = values - jnp.mean(values, axis=-1, keepdims=True)
    inverse = lax.rsqrt(jnp.mean(centred * centred, axis=-1, keepdims=True) + EPSILON)
    return centred * inverse, inverse


def norm_back(grad_out, normed, inverse, gain):
    grad_normed = grad_out * gain
    first = jnp.mean(grad_normed, axis=-1, keepdims=True)
    second = jnp.mean(grad_normed * normed, axis=-1, keepdims=True)
    return inverse * (grad_normed - first - normed * second)


def split_two(value):
    high = value.astype(BF)
    return high, (value - high.astype(F32)).astype(BF)


def shape_of(shape, dtype):
    return jax.ShapeDtypeStruct(shape, dtype)


def greet(peers):
    barrier = pltpu.get_barrier_semaphore()
    for peer in peers:
        pl.semaphore_signal(barrier, inc=1, device_id=peer, device_id_type=MESH)
    pl.semaphore_wait(barrier, len(peers))


def remote(src, dst, send, recv, peer):
    return pltpu.make_async_remote_copy(
        src_ref=src, dst_ref=dst, send_sem=send, recv_sem=recv, device_id=peer, device_id_type=MESH
    )


def doc_bounds(docs):
    ends, at = [], 0
    for n in range(docs.shape[1] - 1):
        at = at + docs[0, n]
        ends.append(at)
    return ends


def start_of(place, ends):
    begin = jnp.zeros_like(place)
    for end in ends:
        begin = jnp.where(place >= end, end, begin)
    return begin


def aligned(at, size):
    return pl.ds(pl.multiple_of(at, size), size)


def find_slots(experts, capacity, ids, ids_t, pos, slot, count):
    rows = ids.shape[0]
    col = [ids[:, j : j + 1] for j in range(2)]
    row = [ids_t[j : j + 1, :] for j in range(2)]
    lane = iota((rows, LANES), 1)
    hot = [(lane == c).astype(BF) for c in col]
    either = hot[0] + hot[1]
    below = (iota((rows, rows), 0) > iota((rows, rows), 1)).astype(BF)
    before = mm(below, either)
    wide = max(experts, 16)
    deep = iota((wide, rows), 0)
    hot_t = [(deep == r).astype(BF) for r in row]
    above = (iota((rows, rows), 0) < iota((rows, rows), 1)).astype(BF)
    before_t = mm(hot_t[0] + hot_t[1], above)
    count[...] = jnp.sum(either.astype(F32), axis=0, keepdims=True)
    flat_t = []
    for j in range(2):
        at = jnp.sum(hot[j].astype(F32) * before, axis=1, keepdims=True).astype(I32)
        pos[:, j : j + 1] = col[j] * capacity + at
        slot[:, j : j + 1] = at
        at_t = jnp.sum(hot_t[j].astype(F32) * before_t, axis=0, keepdims=True).astype(I32)
        flat_t.append(row[j] * capacity + at_t)
    return flat_t


def fill_slots(flat_t, source, out):
    total, rows = out.shape[0], source.shape[0]
    half = total // 2
    for n in range(2):
        place = iota((half, rows), 0) + n * half
        pick = ((place == flat_t[0]) | (place == flat_t[1])).astype(BF)
        out[pl.ds(n * half, half), :] = mm(pick, source).astype(BF)


def attend_block(heads, ends, i, qkv, keys, scores, lse):
    width = heads * HEAD_DIM
    base = i * BLOCK
    rows = aligned(base, BLOCK)
    q_pos = base + iota((1, BLOCK), 1)
    begin = start_of(q_pos, ends)
    first = (i - (REACH - 1)) * (i // (REACH - 1))
    queries = [
        qkv[n * HEAD_DIM : (n + 1) * HEAD_DIM, rows] * jnp.asarray(SCALE, BF) for n in range(heads)
    ]
    tops = [jnp.full((1, BLOCK), MASKED, F32)] * heads
    for k in range(REACH):
        part = aligned((first + k) * BLOCK, BLOCK)
        k_pos = (first + k) * BLOCK + iota((BLOCK, BLOCK), 0)
        allowed = (k_pos <= q_pos) & (k_pos >= begin)
        for n in range(heads):
            score = jnp.where(allowed, mm(keys[n, part, :], queries[n]), MASKED)
            scores[n, k] = score
            tops[n] = jnp.maximum(tops[n], jnp.max(score, axis=0, keepdims=True))
    result = []
    for n in range(heads):
        total = jnp.zeros((1, BLOCK), F32)
        acc = jnp.zeros((HEAD_DIM, BLOCK), F32)
        lo = 2 * width + n * HEAD_DIM
        for k in range(REACH):
            weight = jnp.exp(scores[n, k] - tops[n])
            total = total + jnp.sum(weight, axis=0, keepdims=True)
            value = qkv[lo : lo + HEAD_DIM, aligned((first + k) * BLOCK, BLOCK)]
            acc = acc + mm(value, weight.astype(BF))
        lse[n : n + 1, rows] = tops[n] + jnp.log(total)
        result.append((acc / total).astype(BF))
    return result


def front_body(
    n_e,
    n_h,
    experts,
    capacity,
    padded,
    heads,
    chunks,
    docs,
    ids,
    ids_t,
    g1,
    s1,
    g2,
    s2,
    w_router,
    tokens,
    out_grad,
    w_query,
    w_key,
    w_value,
    w_out,
    w_up,
    w_down,
    all_tokens,
    qkv_out,
    att_out,
    att_t_out,
    w_t_out,
    g_in,
    x_slots,
    ups,
    downs,
    pos,
    slot,
    count,
    lse,
    residual,
    gates,
    gate_rows,
    tv,
    gv,
    wv,
    wo,
    w_t,
    qkv,
    keys,
    scores,
    att_v,
    att_in,
    g_slots,
    xs_v,
    own_sem,
    w_sem,
    save_sem,
    ty_s,
    ty_r,
    tc_s,
    tc_r,
    tf_s,
    tf_r,
    gs_s,
    gs_r,
    at_s,
    at_r,
    wy_s,
    wy_r,
    wc_s,
    wc_r,
    wf_s,
    wf_r,
):
    e, h = lax.axis_index("expert"), lax.axis_index("hidden")
    far = n_h // 2
    pair, core = h // 2, lax.rem(h, 2)
    mate = pair * 2 + 1 - core
    rows, model = tokens.shape
    width = heads * HEAD_DIM
    per_device = rows // BLOCK
    ends = doc_bounds(docs)

    def across(t):
        return lax.rem(pair + t, far) * 2 + core

    def origin(t):
        return lax.rem(pair + far - t, far) * 2 + core

    own_tokens = pltpu.make_async_copy(tokens, tv.at[h], own_sem.at[0])
    own_grad = pltpu.make_async_copy(out_grad, gv, own_sem.at[1])
    own_grad.start()
    own_tokens.start()
    w_loads = [
        pltpu.make_async_copy(w, wv.at[n], w_sem.at[n])
        for n, w in enumerate((w_query, w_key, w_value))
    ]
    w_loads.append(pltpu.make_async_copy(w_out, wo, w_sem.at[3]))
    for load in w_loads:
        load.start()
    greet(
        [{"hidden": lax.rem(h + step, n_h)} for step in range(1, n_h)]
        + [{"expert": lax.rem(e + step, n_e)} for step in range(1, n_e)]
    )

    piece = rows // chunks
    sends = []
    for k in range(chunks):
        part = pl.ds(k * piece, piece)
        for t in range(1, far):
            copy = remote(
                tokens.at[part],
                tv.at[h, part],
                ty_s.at[t, k],
                ty_r.at[t, k],
                {"hidden": across(t)},
            )
            copy.start()
            sends.append(copy)
    beside = remote(tokens, tv.at[h], tc_s, tc_r, {"hidden": mate})
    beside.start()
    sends.append(beside)

    flat_t = find_slots(experts, capacity, ids, ids_t, pos, slot, count)
    own_grad.wait()
    fill_slots(flat_t, gv[...], g_slots)
    for step in range(1, n_e):
        peer = lax.rem(e + step, n_e)
        copy = remote(
            g_slots.at[aligned(peer * capacity, capacity)],
            g_in.at[e],
            gs_s.at[step],
            gs_r.at[step],
            {"expert": peer},
        )
        copy.start()
        sends.append(copy)
    own_slots = pltpu.make_async_copy(
        g_slots.at[aligned(e * capacity, capacity)], g_in.at[e], own_sem.at[1]
    )
    own_slots.start()

    def pass_on(t, k):
        part = pl.ds(k * piece, piece)
        place = tv.at[origin(t), part]
        remote(place, place, ty_s.at[t, k], ty_r.at[t, k], {"hidden": across(t)}).wait_recv()
        copy = remote(place, place, tf_s.at[t, k], tf_r.at[t, k], {"hidden": mate})
        copy.start()
        sends.append(copy)

    todo = [(t, k) for k in range(chunks) for t in range(1, far)]
    third = -(-len(todo) // 4)

    def pass_some():
        for _ in range(min(third, len(todo))):
            pass_on(*todo.pop(0))

    pick = (iota((width, model), 1) == iota((width, model), 0) + h * width).astype(BF)
    for n in range(3):
        w_loads[n].wait()
        w_t[n * width : (n + 1) * width, :] = mm_nt(pick, wv[n]).astype(BF)
        if n == 1:
            pass_some()
    save_w = pltpu.make_async_copy(w_t, w_t_out, save_sem.at[0])
    save_w.start()

    def project(source):
        def one(b, _):
            normed, _unused = norm_parts(tv[source, aligned(b * BLOCK, BLOCK), :].astype(F32))
            hidden = (normed * g1[...] + s1[...]).astype(BF)
            block = mm_nt(w_t[...], hidden)
            cols = aligned(source * rows + b * BLOCK, BLOCK)
            qkv[:, cols] = block.astype(BF)
            for n in range(heads):
                lo = width + n * HEAD_DIM
                keys[n, cols, :] = block[lo : lo + HEAD_DIM].T.astype(BF)
            return 0

        lax.fori_loop(0, per_device, one, 0)

    pass_some()
    own_tokens.wait()
    project(h)
    pass_some()
    remote(tokens, tv.at[mate], tc_s, tc_r, {"hidden": mate}).wait_recv()
    project(mate)
    while todo:
        pass_some()

    def weight_part(which, k):
        deep = (w_up, w_down)[which].shape[1] // 2
        return pl.ds(k * deep, deep)

    for which, (source, target) in enumerate(((w_up, ups), (w_down, downs))):
        keep = pltpu.make_async_copy(source.at[0], target.at[h], own_sem.at[2 + which])
        keep.start()
        copy = remote(
            source.at[0], target.at[h], wc_s.at[which], wc_r.at[which], {"hidden": mate}
        )
        copy.start()
        sends.append(copy)
        for k in range(2):
            part = weight_part(which, k)
            for t in range(1, far):
                copy = remote(
                    source.at[0, part],
                    target.at[h, part],
                    wy_s.at[which, t, k],
                    wy_r.at[which, t, k],
                    {"hidden": across(t)},
                )
                copy.start()
                sends.append(copy)
    for t in range(1, far):
        project(origin(t))
    for t in range(1, far):
        there = lax.rem(pair + far - t, far) * 2 + 1 - core
        for k in range(chunks):
            place = tv.at[there, pl.ds(k * piece, piece)]
            remote(place, place, tf_s.at[t, k], tf_r.at[t, k], {"hidden": mate}).wait_recv()
        project(there)
    save_tokens = pltpu.make_async_copy(tv, all_tokens, save_sem.at[1])
    save_qkv = pltpu.make_async_copy(qkv, qkv_out, save_sem.at[2])
    save_tokens.start()
    save_qkv.start()

    lse[...] = jnp.zeros_like(lse)
    owners = []
    for t in range(1, far):
        owners.append(lax.rem(pair + t, far) * 2 + core)
        owners.append(lax.rem(pair + t, far) * 2 + 1 - core)
    owners += [mate, h]
    for at, owner in enumerate(owners):

        def one(b, _, owner=owner):
            done = attend_block(heads, ends, owner * per_device + b, qkv, keys, scores, lse)
            for n in range(heads):
                lo = n * HEAD_DIM
                att_v[owner, lo : lo + HEAD_DIM, aligned(b * BLOCK, BLOCK)] = done[n]
            return 0

        lax.fori_loop(0, per_device, one, 0)
        if at < len(owners) - 1:
            copy = remote(
                att_v.at[owner], att_in.at[h], at_s.at[at], at_r.at[at], {"hidden": owner}
            )
            copy.start()
            sends.append(copy)
    att_in[h] = att_v[h]
    save_att = pltpu.make_async_copy(att_v, att_out, save_sem.at[3])
    save_att.start()
    at = 0
    for t in range(1, far):
        for other in (core, 1 - core):
            place = att_in.at[lax.rem(pair + far - t, far) * 2 + other]
            remote(place, place, at_s.at[at], at_r.at[at], {"hidden": mate}).wait_recv()
            at += 1
    place = att_in.at[mate]
    remote(place, place, at_s.at[at], at_r.at[at], {"hidden": mate}).wait_recv()
    save_att_t = pltpu.make_async_copy(att_in, att_t_out, save_sem.at[4])
    save_att_t.start()

    w_loads[3].wait()
    res = tv[h].astype(F32) + mm_tn(att_in[...].reshape(model, rows), wo[...])
    residual[...] = res
    normed, _unused = norm_parts(res)
    hidden = (normed * g2[...] + s2[...]).astype(BF)
    fill_slots(flat_t, hidden, xs_v)
    save_x = [
        pltpu.make_async_copy(
            xs_v.at[pl.ds(n * capacity, capacity)], x_slots.at[n], save_sem.at[5 + n]
        )
        for n in range(experts)
    ]
    for save in save_x:
        save.start()
    logits = mm(hidden, w_router[...])
    lane = iota((rows, experts), 1)
    chosen = [
        jnp.sum(jnp.where(lane == ids[:, j : j + 1], logits, 0.0), axis=1, keepdims=True)
        for j in range(2)
    ]
    top = jnp.maximum(chosen[0], chosen[1])
    raised = [jnp.exp(c - top) for c in chosen]
    both = raised[0] + raised[1]
    gate = [r / both for r in raised]
    for j in range(2):
        gates[:, j : j + 1] = gate[j]
    column = iota((rows, padded), 1)
    for n in range(experts):
        mix = jnp.zeros((rows, padded), F32)
        for j in range(2):
            here = jnp.where(ids[:, j : j + 1] == n, slot[:, j : j + 1], -1) == column
            mix = jnp.where(here, gate[j], mix)
        line = jnp.sum(mix, axis=0, keepdims=True)
        gate_rows[n] = jnp.broadcast_to(line, (8, padded))

    for which, target in enumerate((ups, downs)):
        for k in range(2):
            part = weight_part(which, k)
            for t in range(1, far):
                place = target.at[origin(t), part]
                remote(
                    place, place, wy_s.at[which, t, k], wy_r.at[which, t, k], {"hidden": mate}
                ).wait_recv()
                copy = remote(
                    place, place, wf_s.at[which, t, k], wf_r.at[which, t, k], {"hidden": mate}
                )
                copy.start()
                sends.append(copy)
    for which, target in enumerate((ups, downs)):
        place = target.at[mate]
        remote(place, place, wc_s.at[which], wc_r.at[which], {"hidden": mate}).wait_recv()
        for k in range(2):
            part = weight_part(which, k)
            for t in range(1, far):
                there = lax.rem(pair + far - t, far) * 2 + 1 - core
                place = target.at[there, part]
                remote(
                    place, place, wf_s.at[which, t, k], wf_r.at[which, t, k], {"hidden": mate}
                ).wait_recv()
        pltpu.make_async_copy(target.at[h], target.at[h], own_sem.at[2 + which]).wait()
    for step in range(1, n_e):
        source = lax.rem(e + n_e - step, n_e)
        place = g_in.at[source]
        remote(place, place, gs_s.at[step], gs_r.at[step], {"expert": e}).wait_recv()
    own_slots.wait()
    for copy in sends:
        copy.wait_send()
    for save in [save_w, save_tokens, save_qkv, save_att, save_att_t, *save_x]:
        save.wait()


def run_front(
    docs, ids, g1, s1, g2, s2, w_router, tokens, out_grad, ws, w_up, w_down, capacity, heads, cid
):
    n_e, n_h = lax.axis_size("expert"), lax.axis_size("hidden")
    experts = n_e * w_up.shape[0]
    rows, model = tokens.shape
    padded = -(-capacity // LANES) * LANES
    width, group, total = heads * HEAD_DIM, rows * n_h, experts * capacity
    far, chunks = n_h // 2, 8

    def pairs(*shape):
        return [DMA(shape), DMA(shape)]

    return pl.pallas_call(
        partial(front_body, n_e, n_h, experts, capacity, padded, heads, chunks),
        name="front",
        out_shape=[
            shape_of((n_h, rows, model), BF),
            shape_of((3 * width, group), BF),
            shape_of((n_h, width, rows), BF),
            shape_of((n_h, width, rows), BF),
            shape_of((3 * width, model), BF),
            shape_of((experts, capacity, model), BF),
            shape_of((experts, capacity, model), BF),
            shape_of((n_h, *w_up.shape[1:]), BF),
            shape_of((n_h, *w_down.shape[1:]), BF),
            shape_of((rows, 2), I32),
            shape_of((rows, 2), I32),
            shape_of((1, LANES), F32),
            shape_of((8, group), F32),
            shape_of((rows, model), F32),
            shape_of((rows, 2), F32),
            shape_of((experts, 8, padded), F32),
        ],
        in_specs=[SMEM] + [VMEM] * 7 + [ANY] * 8,
        out_specs=[ANY] * 9 + [VMEM] * 7,
        scratch_shapes=[
            pltpu.VMEM((n_h, rows, model), BF),
            pltpu.VMEM((rows, model), BF),
            pltpu.VMEM((3, model, model), BF),
            pltpu.VMEM((model, model), BF),
            pltpu.VMEM((3 * width, model), BF),
            pltpu.VMEM((3 * width, group), BF),
            pltpu.VMEM((heads, group, HEAD_DIM), BF),
            pltpu.VMEM((heads, REACH, BLOCK, BLOCK), F32),
            pltpu.VMEM((n_h, width, rows), BF),
            pltpu.VMEM((n_h, width, rows), BF),
            pltpu.VMEM((total, model), BF),
            pltpu.VMEM((total, model), BF),
            DMA((4,)),
            DMA((4,)),
            DMA((5 + experts,)),
            *pairs(far, chunks),
            DMA,
            DMA,
            *pairs(far, chunks),
            *pairs(n_e),
            *pairs(n_h),
            *pairs(2, far, 2),
            *pairs(2),
            *pairs(2, far, 2),
        ],
        compiler_params=pltpu.CompilerParams(
            collective_id=cid, has_side_effects=True, vmem_limit_bytes=58 << 20
        ),
    )(docs, ids, ids.T, g1, s1, g2, s2, w_router, tokens, out_grad, *ws, w_up, w_down)


def moe_body(
    size,
    capacity,
    padded,
    per,
    x_slots,
    gate_rows,
    g_in,
    ups,
    downs,
    dx_back,
    dg_back,
    y_out,
    up_part,
    down_part,
    xv,
    gv,
    gates_v,
    up_v,
    down_v,
    act,
    dz,
    xg,
    dy,
    xg_t,
    dy_t,
    dxv,
    yv,
    dgv,
    y_acc,
    dx_acc,
    load_sem,
    g_sem,
    own_sem,
    xs_sem,
    xr_sem,
    gs_sem,
    gr_sem,
    ds_sem,
    dr_sem,
    ts_sem,
    tr_sem,
    out_sem,
):
    me = lax.axis_index("expert")
    shards_n = ups.shape[0]
    tall = per * capacity
    steps = size // per

    def to_peer(p):
        return lax.rem(me + 3 * p, size)

    def from_peer(p):
        return lax.rem(me + 3 * (size - p), size)

    def rows_of(p):
        return pl.ds(pl.multiple_of(p * capacity, capacity), capacity)

    def send_x(p):
        peer = to_peer(p)
        return remote(
            x_slots.at[peer], xv.at[rows_of(p)], xs_sem.at[p], xr_sem.at[p], {"expert": peer}
        )

    def send_gate(p):
        peer = to_peer(p)
        return remote(
            gate_rows.at[peer], gates_v.at[p], gs_sem.at[p], gr_sem.at[p], {"expert": peer}
        )

    def send_dx(p):
        peer = from_peer(p)
        return remote(
            dxv.at[rows_of(p)], dx_back.at[me], ds_sem.at[p], dr_sem.at[p], {"expert": peer}
        )

    def send_dg(p):
        peer = from_peer(p)
        return remote(dgv.at[p], dg_back.at[me], ts_sem.at[p], tr_sem.at[p], {"expert": peer})

    def load_g(p):
        return pltpu.make_async_copy(g_in.at[from_peer(p)], gv.at[rows_of(p)], g_sem.at[p])

    def save_y(p):
        return pltpu.make_async_copy(yv.at[rows_of(p)], y_out.at[from_peer(p)], out_sem.at[p])

    own_x = pltpu.make_async_copy(x_slots.at[me], xv.at[rows_of(0)], own_sem.at[0])
    own_gate = pltpu.make_async_copy(gate_rows.at[me], gates_v.at[0], own_sem.at[1])
    own_dx = pltpu.make_async_copy(dxv.at[rows_of(0)], dx_back.at[me], own_sem.at[2])
    own_dg = pltpu.make_async_copy(dgv.at[0], dg_back.at[me], own_sem.at[3])
    loads = [pltpu.make_async_copy(ups, up_v, load_sem.at[0])]
    loads += [pltpu.make_async_copy(downs, down_v, load_sem.at[1])]
    own_x.start()
    own_gate.start()
    for p in range(size):
        load_g(p).start()
    for load in loads:
        load.start()
    greet([{"expert": lax.rem(me + step, size)} for step in range(1, size)])
    for p in range(1, size):
        send_x(p).start()
        send_gate(p).start()
    own_x.wait()
    own_gate.wait()
    for load in loads:
        load.wait()

    def step_body(step, _):
        base = step * per
        for s in range(per):

            @pl.when(base + s > 0)
            def _arrive(s=s):
                send_x(base + s).wait_recv()
                send_gate(base + s).wait_recv()

            load_g(base + s).wait()
        rows = pl.ds(pl.multiple_of(step * tall, tall), tall)
        x, g = xv[rows, :], gv[rows, :]
        y_acc[...] = jnp.zeros_like(y_acc)
        dx_acc[...] = jnp.zeros_like(dx_acc)

        def shard_body(c, _):
            z = mm(x, up_v[c])
            du = mm_nt(g, down_v[c])
            square = z * z
            t = jnp.tanh(z * (GELU_A + GELU_A * GELU_B * square))
            plus = 0.5 + 0.5 * t
            hidden = (z * plus).astype(BF)
            slope = plus + 0.5 * z * (1.0 - t * t) * (GELU_A + 3.0 * GELU_A * GELU_B * square)
            back = (slope * du).astype(BF)
            act[c, rows, :] = hidden
            dz[c, rows, :] = back
            y_acc[...] += mm(hidden, down_v[c])
            dx_acc[...] += mm_nt(back, up_v[c])
            return 0

        lax.fori_loop(0, shards_n, shard_body, 0)
        dxv[rows, :] = dx_acc[...].astype(BF)
        y_low = y_acc[...].astype(BF)
        yv[rows, :] = y_low
        dots = jnp.sum(y_low.astype(F32) * g.astype(F32), axis=1, keepdims=True)
        for s in range(per):
            p = base + s
            part = slice(s * capacity, (s + 1) * capacity)
            tall_dots = jnp.broadcast_to(dots[part], (capacity, LANES))
            if padded > capacity:
                blank = jnp.zeros((padded - capacity, LANES), F32)
                tall_dots = jnp.concatenate([tall_dots, blank], axis=0)
            dgv[p] = tall_dots.T[0:8]

            @pl.when(p > 0)
            def _give(p=p):
                send_dx(p).start()
                send_dg(p).start()

            @pl.when(p == 0)
            def _keep():
                own_dx.start()
                own_dg.start()

            save_y(p).start()
        for s in range(per):
            p = base + s
            part = slice(s * capacity, (s + 1) * capacity)
            gate = gates_v[p].T[0:capacity, 0:1]
            xg[rows_of(p), :] = (x[part].astype(F32) * gate).astype(BF)
            dy[rows_of(p), :] = (g[part].astype(F32) * gate).astype(BF)
        return 0

    lax.fori_loop(0, steps, step_body, 0)

    total = size * capacity
    turn = 256
    for k in range(total // turn):
        rows = slice(k * turn, (k + 1) * turn)
        xg_t[:, rows] = xg[rows, :].astype(F32).T.astype(BF)
        dy_t[:, rows] = dy[rows, :].astype(F32).T.astype(BF)
    model = xg_t.shape[0]
    bands = model // turn

    def weight_body(n, _):
        c, band = n // bands, lax.rem(n, bands)
        lines = pl.ds(pl.multiple_of(band * turn, turn), turn)
        up_v[c, lines, :] = mm(xg_t[lines, :], dz[c]).astype(BF)
        down_v[c, lines, :] = mm(dy_t[lines, :], act[c]).astype(BF)
        return 0

    lax.fori_loop(0, shards_n * bands, weight_body, 0)
    keep_up = pltpu.make_async_copy(up_v, up_part, load_sem.at[0])
    keep_down = pltpu.make_async_copy(down_v, down_part, load_sem.at[1])
    keep_up.start()
    keep_down.start()
    for p in range(1, size):
        send_x(p).wait_send()
        send_gate(p).wait_send()
        send_dx(p).wait()
        send_dg(p).wait()
    for p in range(size):
        save_y(p).wait()
    own_dx.wait()
    own_dg.wait()
    keep_up.wait()
    keep_down.wait()


def run_experts(x_slots, gate_rows, g_in, ups, downs, cid):
    size = lax.axis_size("expert")
    experts, capacity, model = x_slots.shape
    padded = gate_rows.shape[2]
    shards_n, _unused, width = ups.shape
    total = experts * capacity
    per = 1
    while per * 2 * capacity <= 320 and size % (per * 2) == 0:
        per *= 2
    tall = per * capacity
    rows2 = (total, model)
    return pl.pallas_call(
        partial(moe_body, size, capacity, padded, per),
        name="experts",
        out_shape=[
            shape_of(x_slots.shape, BF),
            shape_of(gate_rows.shape, F32),
            shape_of(x_slots.shape, BF),
            shape_of((shards_n, model, width), BF),
            shape_of((shards_n, model, width), BF),
        ],
        in_specs=[ANY] * 5,
        out_specs=[ANY] * 5,
        scratch_shapes=[
            pltpu.VMEM(rows2, BF),
            pltpu.VMEM(rows2, BF),
            pltpu.VMEM(gate_rows.shape, F32),
            pltpu.VMEM((shards_n, model, width), BF),
            pltpu.VMEM((shards_n, width, model), BF),
            pltpu.VMEM((shards_n, total, width), BF),
            pltpu.VMEM((shards_n, total, width), BF),
            pltpu.VMEM(rows2, BF),
            pltpu.VMEM(rows2, BF),
            pltpu.VMEM((model, total), BF),
            pltpu.VMEM((model, total), BF),
            pltpu.VMEM(rows2, BF),
            pltpu.VMEM(rows2, BF),
            pltpu.VMEM(gate_rows.shape, F32),
            pltpu.VMEM((tall, model), F32),
            pltpu.VMEM((tall, model), F32),
            DMA((2,)),
            DMA((size,)),
            DMA((4,)),
        ]
        + [DMA((size,))] * 9,
        compiler_params=pltpu.CompilerParams(
            collective_id=cid, has_side_effects=True, vmem_limit_bytes=60 << 20
        ),
        cost_estimate=pl.CostEstimate(
            flops=12 * total * model * width * shards_n, bytes_accessed=40 << 20, transcendentals=0
        ),
    )(x_slots, gate_rows, g_in, ups, downs)


def tail_body(
    n_e,
    n_h,
    chunks,
    dh,
    w_all,
    small,
    tokens,
    gain,
    d_res,
    residual,
    gates,
    pos,
    y_back,
    input_grad,
    output,
    full,
    total,
    mine,
    beside,
    across,
    passing,
    w_box,
    piece,
    small_mid,
    small_h,
    small_e,
    mine_sem,
    cs_sem,
    cr_sem,
    as_sem,
    ar_sem,
    ws_sem,
    wr_sem,
    hs_sem,
    hr_sem,
    es_sem,
    er_sem,
    keep_sem,
    zs_sem,
    zr_sem,
    xs_sem,
    xr_sem,
    ys_sem,
    yr_sem,
    ms_sem,
    mr_sem,
):
    e, h = lax.axis_index("expert"), lax.axis_index("hidden")
    far, high = n_h // 2, n_e // 2
    pair, core = h // 2, lax.rem(h, 2)
    eh, el = e // 2, lax.rem(e, 2)
    mate = pair * 2 + 1 - core
    greet(
        [{"expert": lax.rem(e + step, n_e)} for step in range(1, n_e)]
        + [{"hidden": lax.rem(h + step, n_h)} for step in range(1, n_h)]
    )
    w_sends = []
    for at in range(n_e - 1):
        peer = lax.rem(e + 1 + at, n_e)
        copy = remote(
            w_all.at[peer], w_box.at[at], ws_sem.at[at], wr_sem.at[at], {"expert": peer}
        )
        copy.start()
        w_sends.append(copy)
    rows = dh.shape[1] // chunks
    core_sends = {}
    for step in list(range(1, far)) + [0]:
        there = lax.rem(pair + step, far)
        for k in range(chunks):
            part = pl.ds(k * rows, rows)
            copy = remote(
                dh.at[there * 2 + 1 - core, part],
                beside.at[step, part],
                cs_sem.at[step, k],
                cr_sem.at[step, k],
                {"hidden": mate},
            )
            copy.start()
            core_sends[step, k] = copy
    loads = []
    for step in range(far):
        there = lax.rem(pair + step, far)
        load = pltpu.make_async_copy(dh.at[there * 2 + core], mine.at[step], mine_sem.at[step])
        load.start()
        loads.append(load)
    small_sends = []
    for at in range(n_h - 1):
        peer = lax.rem(h + 1 + at, n_h)
        copy = remote(small, small_h.at[at], hs_sem.at[at], hr_sem.at[at], {"hidden": peer})
        copy.start()
        small_sends.append(copy)
    for load in loads:
        load.wait()
    far_sends = []
    for step in range(1, far):
        there = lax.rem(pair + step, far)
        for k in range(chunks):
            part = pl.ds(k * rows, rows)
            core_sends[step, k].wait_recv()
            both = mine[step, part, :].astype(F32) + beside[step, part, :].astype(F32)
            passing[step - 1, part, :] = both.astype(BF)
            copy = remote(
                passing.at[step - 1, part],
                across.at[step - 1, part],
                as_sem.at[step - 1, k],
                ar_sem.at[step - 1, k],
                {"hidden": there * 2 + core},
            )
            copy.start()
            far_sends.append(copy)
    for copy in small_sends:
        copy.wait_recv()
    summed = small[...]
    for at in range(n_h - 1):
        summed = summed + small_h[at]
    small_mid[...] = summed
    small_out = []
    for at in range(n_e - 1):
        peer = lax.rem(e + 1 + at, n_e)
        copy = remote(small_mid, small_e.at[at], es_sem.at[at], er_sem.at[at], {"expert": peer})
        copy.start()
        small_out.append(copy)
    for copy in w_sends:
        copy.wait_recv()
    acc = w_all[e].astype(F32)
    for at in range(n_e - 1):
        acc = acc + w_box[at].astype(F32)
    piece[...] = acc.astype(BF)
    keep = pltpu.make_async_copy(piece, full.at[h, e], keep_sem)
    keep.start()
    started = []

    def slot(eh_of, el_of, pair_of, core_of):
        return full.at[pair_of * 2 + core_of, eh_of * 2 + el_of]

    def back(step, size, place):
        return lax.rem(place + size - step, size)

    def give_z(source):
        for s in range(1, high):
            there = lax.rem(eh + s, high) * 2 + el
            copy = remote(
                source, slot(eh, el, pair, core), zs_sem.at[s], zr_sem.at[s], {"expert": there}
            )
            copy.start()
            started.append(copy)

    def z_arrival(s):
        place = slot(back(s, high, eh), el, pair, core)
        return place, remote(place, place, zs_sem.at[s], zr_sem.at[s], {"expert": e})

    def give_x(source, s):
        target = slot(back(s, high, eh), el, pair, core)
        copy = remote(
            source, target, xs_sem.at[s], xr_sem.at[s], {"expert": eh * 2 + 1 - el}
        )
        copy.start()
        started.append(copy)

    def x_arrival(s):
        place = slot(back(s, high, eh), 1 - el, pair, core)
        return place, remote(place, place, xs_sem.at[s], xr_sem.at[s], {"expert": e})

    def give_y(source, s, flag):
        target = slot(back(s, high, eh), el if flag == 0 else 1 - el, pair, core)
        for t in range(1, far):
            there = lax.rem(pair + t, far) * 2 + core
            at = 2 * s + flag
            copy = remote(
                source, target, ys_sem.at[t, at], yr_sem.at[t, at], {"hidden": there}
            )
            copy.start()
            started.append(copy)

    def y_arrival(t, s, flag):
        other = el if flag == 0 else 1 - el
        place = slot(back(s, high, eh), other, back(t, far, pair), core)
        at = 2 * s + flag
        return place, remote(place, place, ys_sem.at[t, at], yr_sem.at[t, at], {"hidden": h})

    def give_mate(source, t, s, flag):
        other = el if flag == 0 else 1 - el
        target = slot(back(s, high, eh), other, back(t, far, pair), core)
        at = 2 * s + flag
        copy = remote(source, target, ms_sem.at[t, at], mr_sem.at[t, at], {"hidden": mate})
        copy.start()
        started.append(copy)

    def mate_arrival(t, s, flag):
        other = el if flag == 0 else 1 - el
        place = slot(back(s, high, eh), other, back(t, far, pair), 1 - core)
        at = 2 * s + flag
        return place, remote(place, place, ms_sem.at[t, at], mr_sem.at[t, at], {"hidden": h})

    give_z(piece)
    give_x(piece, 0)
    give_y(piece, 0, 0)
    give_mate(piece, 0, 0, 0)
    for s in range(1, high):
        place, arrival = z_arrival(s)
        arrival.wait_recv()
        give_x(place, s)
        give_y(place, s, 0)
        give_mate(place, 0, s, 0)
    for s in range(high):
        place, arrival = x_arrival(s)
        arrival.wait_recv()
        give_y(place, s, 1)
        give_mate(place, 0, s, 1)
    place_of = iota((residual.shape[0], y_back.shape[0]), 1)
    result = residual[...]
    for j in range(2):
        pick = (place_of == pos[:, j : j + 1]).astype(BF)
        result = result + gates[:, j : j + 1] * mm(pick, y_back[...])
    output[...] = result.astype(BF)
    for copy in small_out:
        copy.wait_recv()
    summed = small_mid[...]
    for at in range(n_e - 1):
        summed = summed + small_e[at]
    total[...] = summed
    for k in range(chunks):
        part = pl.ds(k * rows, rows)
        core_sends[0, k].wait_recv()
    for copy in far_sends:
        copy.wait_recv()
    grad = mine[0].astype(F32) + beside[0].astype(F32)
    for step in range(far - 1):
        grad = grad + across[step].astype(F32)
    normed, inverse = norm_parts(tokens[...].astype(F32))
    input_grad[...] = (d_res[...] + norm_back(grad, normed, inverse, gain[...])).astype(BF)
    for t in range(1, far):
        for s in range(high):
            for flag in range(2):
                place, arrival = y_arrival(t, s, flag)
                arrival.wait_recv()
                give_mate(place, t, s, flag)
    for t in range(far):
        for s in range(high):
            for flag in range(2):
                _place, arrival = mate_arrival(t, s, flag)
                arrival.wait_recv()
    keep.wait()
    for copy in started + w_sends + small_sends + small_out + far_sends:
        copy.wait_send()
    for copy in core_sends.values():
        copy.wait_send()


def run_tail(dh, w_all, small, tokens, gain, d_res, residual, gates, pos, y_back, cid):
    n_e, n_h = lax.axis_size("expert"), lax.axis_size("hidden")
    far, high = n_h // 2, n_e // 2
    chunks = 4
    _unused, rows, model = dh.shape
    piece = w_all.shape[1:]
    return pl.pallas_call(
        partial(tail_body, n_e, n_h, chunks),
        name="tail",
        out_shape=[
            shape_of((rows, model), BF),
            shape_of((rows, model), BF),
            shape_of((n_h, n_e, *piece), BF),
            shape_of(small.shape, F32),
        ],
        in_specs=[ANY] + [VMEM] * 9,
        out_specs=[VMEM, VMEM, ANY, VMEM],
        scratch_shapes=[
            pltpu.VMEM((far, rows, model), BF),
            pltpu.VMEM((far, rows, model), BF),
            pltpu.VMEM((far - 1, rows, model), BF),
            pltpu.VMEM((far - 1, rows, model), BF),
            pltpu.VMEM((n_e - 1, *piece), BF),
            pltpu.VMEM(piece, BF),
            pltpu.VMEM(small.shape, F32),
            pltpu.VMEM((n_h - 1, *small.shape), F32),
            pltpu.VMEM((n_e - 1, *small.shape), F32),
            DMA((far,)),
            DMA((far, chunks)),
            DMA((far, chunks)),
            DMA((far - 1, chunks)),
            DMA((far - 1, chunks)),
            DMA((n_e - 1,)),
            DMA((n_e - 1,)),
            DMA((n_h - 1,)),
            DMA((n_h - 1,)),
            DMA((n_e - 1,)),
            DMA((n_e - 1,)),
            DMA,
            DMA((high,)),
            DMA((high,)),
            DMA((high,)),
            DMA((high,)),
            DMA((far, n_e)),
            DMA((far, n_e)),
            DMA((far, n_e)),
            DMA((far, n_e)),
        ],
        compiler_params=pltpu.CompilerParams(
            collective_id=cid, has_side_effects=True, vmem_limit_bytes=56 << 20
        ),
    )(dh, w_all, small, tokens, gain, d_res, residual, gates, pos, y_back)


def turn_body(width, old, full, dw, q_out, k_out, v_out, o_out, up_out, down_out):
    for n, out in enumerate((q_out, k_out, v_out)):
        part = full[:, n * width : (n + 1) * width, :].astype(F32)
        out[...] = part.reshape(-1, part.shape[2]).T
    part = full[:, 3 * width :, :].astype(F32)
    o_out[...] = part.reshape(-1, part.shape[2])
    trained = jnp.where(lax.axis_index("expert") >= old, 1.0, 0.0)
    up_out[...] = dw[0] * trained
    down_out[...] = dw[1].T * trained


def turn_weights(full, dw, width, old):
    n_h, deep, model = full.shape
    cols = 256
    across = pl.BlockSpec((cols, model), lambda i: (i, 0))
    down = pl.BlockSpec((model, cols), lambda i: (0, i))
    square = shape_of((model, model), F32)
    return pl.pallas_call(
        partial(turn_body, width, old),
        name="turn_weights",
        grid=(model // cols,),
        out_shape=[square] * 6,
        in_specs=[
            pl.BlockSpec((n_h, deep, cols), lambda i: (0, 0, i)),
            pl.BlockSpec((2, model, cols), lambda i: (0, 0, i)),
        ],
        out_specs=[across, across, across, down, down, across],
        compiler_params=pltpu.CompilerParams(
            dimension_semantics=("arbitrary",), vmem_limit_bytes=40 << 20
        ),
        cost_estimate=pl.CostEstimate(flops=0, bytes_accessed=24 << 20, transcendentals=0),
    )(full, dw)


def attend_back(heads, ends, blocks, per_device, qkv, d_att, lse, dots, keys, values, accs, d_qkv):
    width = heads * HEAD_DIM
    dq_acc, dk_acc, dv_acc = accs

    def over_keys(j, _):
        part = aligned(j * BLOCK, BLOCK)
        k_pos = j * BLOCK + iota((BLOCK, BLOCK), 0)
        stop = (j + REACH) - (j - (REACH - 2)) * (j // (REACH - 1))
        dk_acc[...] = jnp.zeros_like(dk_acc)
        dv_acc[...] = jnp.zeros_like(dv_acc)

        def over_queries(i, _):
            rows = aligned(i * BLOCK, BLOCK)
            cols = aligned(lax.rem(i, per_device) * BLOCK, BLOCK)
            q_pos = i * BLOCK + iota((1, BLOCK), 1)
            begin = start_of(q_pos, ends)
            allowed = (k_pos <= q_pos) & (k_pos >= begin)
            for n in range(heads):
                here = slice(n * HEAD_DIM, (n + 1) * HEAD_DIM)
                query = qkv[here, rows] * jnp.asarray(SCALE, BF)
                given = d_att[i // per_device, here, cols]
                score = mm(keys[n, part, :], query) - lse[n : n + 1, rows]
                weight = jnp.exp(jnp.where(allowed, score, MASKED))
                d_weight = mm(values[n, part, :], given)
                d_score = (weight * (d_weight - dots[n : n + 1, rows])).astype(BF)
                dv_acc[here, :] += mm_nt(given, weight.astype(BF))
                dk_acc[here, :] += mm_nt(query, d_score)
                lo = width + n * HEAD_DIM
                dq_acc[here, rows] += mm(qkv[lo : lo + HEAD_DIM, part], d_score)
            return 0

        lax.fori_loop(j, stop, over_queries, 0)
        d_qkv[width : 2 * width, part] = dk_acc[...].astype(BF)
        d_qkv[2 * width :, part] = dv_acc[...].astype(BF)
        return 0

    lax.fori_loop(0, blocks, over_keys, 0)


def back_body(
    n_e,
    n_h,
    experts,
    capacity,
    padded,
    heads,
    docs,
    ids,
    slot,
    pos,
    gates,
    count,
    g1,
    s1,
    g2,
    s2,
    w_router,
    lse,
    dg_rows,
    dx_back,
    y_out,
    up_part,
    down_part,
    out_grad,
    residual,
    all_tokens,
    qkv_in,
    att_in,
    att_t_in,
    w_out,
    w_t_in,
    y_back,
    d_hidden,
    d_res,
    w_all,
    small,
    dw_own,
    dxv,
    gv,
    res_v,
    tv,
    qkv,
    att_v,
    att_t,
    wo,
    w_t,
    d_att_v,
    d_att,
    wo_box,
    keys,
    values,
    dots,
    dq_acc,
    dk_acc,
    dv_acc,
    d_qkv,
    w_acc,
    dw_mine,
    dw_beside,
    dw_across,
    load_sem,
    save_sem,
    dw_sem,
    y_own,
    y_s,
    y_r,
    at_s,
    at_r,
    wo_s,
    wo_r,
    dc_s,
    dc_r,
    da_s,
    da_r,
):
    e, h = lax.axis_index("expert"), lax.axis_index("hidden")
    far = n_h // 2
    pair, core = h // 2, lax.rem(h, 2)
    mate = pair * 2 + 1 - core
    rows, model = out_grad.shape
    width = heads * HEAD_DIM
    group = rows * n_h
    per_device = rows // BLOCK
    blocks = group // BLOCK
    ends = doc_bounds(docs)
    sends = []

    loads = [
        pltpu.make_async_copy(source, target, load_sem.at[n])
        for n, (source, target) in enumerate(
            (
                (residual, res_v),
                (dx_back, dxv),
                (out_grad, gv),
                (w_out, wo),
                (att_t_in, att_t),
                (qkv_in, qkv),
                (att_in, att_v),
                (all_tokens, tv),
                (w_t_in, w_t),
            )
        )
    ]
    for load in loads:
        load.start()
    greet(
        [{"hidden": lax.rem(h + step, n_h)} for step in range(1, n_h)]
        + [{"expert": lax.rem(e + step, n_e)} for step in range(1, n_e)]
    )
    mine = []
    for step in list(range(1, far)) + [0]:
        there = lax.rem(pair + step, far)
        for which, part in enumerate((up_part, down_part)):
            copy = remote(
                part.at[there * 2 + 1 - core],
                dw_beside.at[which, step],
                dc_s.at[which, step],
                dc_r.at[which, step],
                {"hidden": mate},
            )
            copy.start()
            sends.append(copy)
            load = pltpu.make_async_copy(
                part.at[there * 2 + core], dw_mine.at[which, step], dw_sem.at[which, step]
            )
            load.start()
            mine.append(load)
    for step in range(1, n_e):
        peer = lax.rem(e + step, n_e)
        copy = remote(y_out.at[peer], y_back.at[e], y_s.at[step], y_r.at[step], {"expert": peer})
        copy.start()
        sends.append(copy)
    own_y = pltpu.make_async_copy(y_out.at[e], y_back.at[e], y_own)
    own_y.start()

    for load in loads[:3]:
        load.wait()
    normed, inverse = norm_parts(res_v[...])
    hidden = (normed * g2[...] + s2[...]).astype(BF)
    gate = [gates[:, j : j + 1] for j in range(2)]
    column = iota((rows, padded), 1)
    dot_of = []
    for j in range(2):
        mix = jnp.zeros((rows, padded), F32)
        for n in range(experts):
            here = jnp.where(ids[:, j : j + 1] == n, slot[:, j : j + 1], -1) == column
            mix = jnp.where(here, dg_rows[n, 0:1, :], mix)
        dot_of.append(jnp.sum(mix, axis=1, keepdims=True))
    mean = gate[0] * dot_of[0] + gate[1] * dot_of[1]
    lane = iota((rows, experts), 1)
    d_logits = jnp.zeros((rows, experts), F32)
    for j in range(2):
        d_logits = jnp.where(lane == ids[:, j : j + 1], gate[j] * (dot_of[j] - mean), d_logits)
    high, low = split_two(d_logits)
    grad = mm_nt(high, w_router[...]) + mm_nt(low, w_router[...])
    small[...] = jnp.zeros_like(small)
    small[5 : 5 + experts, :] = mm_tn(high, hidden) + mm_tn(low, hidden)
    small[4:5, 0:LANES] = count[...]
    place = iota((rows, experts * capacity), 1)
    for j in range(2):
        pick = (place == pos[:, j : j + 1]).astype(BF)
        grad = grad + gate[j] * mm(pick, dxv[...])
    small[2:3, :] = jnp.sum(grad * normed, axis=0, keepdims=True)
    small[3:4, :] = jnp.sum(grad, axis=0, keepdims=True)
    d_resid = gv[...].astype(F32) + norm_back(grad, normed, inverse, g2[...])
    d_res[...] = d_resid
    branch = d_resid.astype(BF)
    loads[3].wait()
    for t in range(n_h):
        owner = lax.rem(h + t, n_h)
        block = mm_nt(wo[owner], branch).astype(BF)
        if t == 0:
            d_att[h] = block
        else:
            d_att_v[owner] = block
            copy = remote(
                d_att_v.at[owner], d_att.at[h], at_s.at[t], at_r.at[t], {"hidden": owner}
            )
            copy.start()
            sends.append(copy)
    loads[4].wait()
    for t in range(n_h):
        owner = lax.rem(h + t, n_h)
        wo[owner] = mm(att_t[owner], branch).astype(BF)
        if t > 0:
            copy = remote(
                wo.at[owner], wo_box.at[t - 1], wo_s.at[t], wo_r.at[t], {"hidden": owner}
            )
            copy.start()
            sends.append(copy)

    for load in mine:
        load.wait()
    lines_w = dw_mine.shape[2]
    bands = lines_w // 96
    for step in range(1, far):
        for which in range(2):
            there = dw_beside.at[which, step]
            remote(
                there, there, dc_s.at[which, step], dc_r.at[which, step], {"hidden": mate}
            ).wait_recv()

            def add(n, _, which=which, step=step):
                band = aligned(n * 96, 96)
                both = dw_mine[which, step, band, :].astype(F32)
                both = both + dw_beside[which, step, band, :].astype(F32)
                dw_mine[which, step, band, :] = both.astype(BF)
                return 0

            lax.fori_loop(0, bands, add, 0)
            copy = remote(
                dw_mine.at[which, step],
                dw_across.at[which, step - 1],
                da_s.at[which, step],
                da_r.at[which, step],
                {"hidden": lax.rem(pair + step, far) * 2 + core},
            )
            copy.start()
            sends.append(copy)

    for load in loads[5:]:
        load.wait()
    dq_acc[...] = jnp.zeros_like(dq_acc)

    def turn(i, _):
        cols = aligned(i * BLOCK, BLOCK)
        for n in range(heads):
            lo = width + n * HEAD_DIM
            keys[n, cols, :] = qkv[lo : lo + HEAD_DIM, cols].astype(F32).T.astype(BF)
            lo = 2 * width + n * HEAD_DIM
            values[n, cols, :] = qkv[lo : lo + HEAD_DIM, cols].astype(F32).T.astype(BF)
        return 0

    lax.fori_loop(0, blocks, turn, 0)
    for t in range(1, n_h):
        there = d_att.at[lax.rem(h + n_h - t, n_h)]
        remote(there, there, at_s.at[t], at_r.at[t], {"hidden": mate}).wait_recv()

    def weigh(i, _):
        cols = aligned(lax.rem(i, per_device) * BLOCK, BLOCK)
        for n in range(heads):
            here = slice(n * HEAD_DIM, (n + 1) * HEAD_DIM)
            product = att_v[i // per_device, here, cols].astype(F32)
            product = product * d_att[i // per_device, here, cols].astype(F32)
            dots[n : n + 1, aligned(i * BLOCK, BLOCK)] = jnp.sum(product, axis=0, keepdims=True)
        return 0

    lax.fori_loop(0, blocks, weigh, 0)
    accs = (dq_acc, dk_acc, dv_acc)
    attend_back(
        heads, ends, blocks, per_device, qkv, d_att, lse, dots, keys, values, accs, d_qkv
    )
    w_acc[...] = jnp.zeros_like(w_acc)

    def finish(i, _):
        cols = aligned(i * BLOCK, BLOCK)
        d_qkv[0:width, cols] = (dq_acc[:, cols] * SCALE).astype(BF)
        block = d_qkv[:, cols]
        grad = mm_tn(block, w_t[...])
        inner = aligned(lax.rem(i, per_device) * BLOCK, BLOCK)
        normed, _unused = norm_parts(tv[i // per_device, inner, :].astype(F32))
        tv[i // per_device, inner, :] = grad.astype(BF)
        small[0:1, :] += jnp.sum(grad * normed, axis=0, keepdims=True)
        small[1:2, :] += jnp.sum(grad, axis=0, keepdims=True)
        hidden = (normed * g1[...] + s1[...]).astype(BF)
        w_acc[...] += mm(block, hidden)
        return 0

    lax.fori_loop(0, blocks, finish, 0)
    save_dh = pltpu.make_async_copy(tv, d_hidden, save_sem)
    save_dh.start()
    w_all[0 : 3 * width, :] = w_acc[...].astype(BF)
    total = wo[h].astype(F32)
    for t in range(1, n_h):
        there = wo_box.at[t - 1]
        remote(there, there, wo_s.at[t], wo_r.at[t], {"hidden": mate}).wait_recv()
        total = total + wo_box[t - 1].astype(F32)
    w_all[3 * width :, :] = total.astype(BF)
    for which in range(2):
        there = dw_beside.at[which, 0]
        remote(there, there, dc_s.at[which, 0], dc_r.at[which, 0], {"hidden": mate}).wait_recv()
        for step in range(1, far):
            there = dw_across.at[which, step - 1]
            remote(
                there, there, da_s.at[which, step], da_r.at[which, step], {"hidden": mate}
            ).wait_recv()

        def add_all(n, _, which=which):
            band = aligned(n * 96, 96)
            both = dw_mine[which, 0, band, :].astype(F32)
            both = both + dw_beside[which, 0, band, :].astype(F32)
            for step in range(1, far):
                both = both + dw_across[which, step - 1, band, :].astype(F32)
            dw_own[which, band, :] = both
            return 0

        lax.fori_loop(0, bands, add_all, 0)
    for step in range(1, n_e):
        there = y_back.at[lax.rem(e + n_e - step, n_e)]
        remote(there, there, y_s.at[step], y_r.at[step], {"expert": e}).wait_recv()
    own_y.wait()
    save_dh.wait()
    for copy in sends:
        copy.wait_send()


def run_back(
    docs,
    ids,
    slot,
    pos,
    gates,
    count,
    g1,
    s1,
    g2,
    s2,
    w_router,
    lse,
    dg_rows,
    dx_back,
    y_out,
    up_part,
    down_part,
    out_grad,
    residual,
    all_tokens,
    qkv,
    att,
    att_t,
    w_out,
    w_t,
    cid,
):
    n_e, n_h = lax.axis_size("expert"), lax.axis_size("hidden")
    experts, capacity, model = y_out.shape
    padded = dg_rows.shape[2]
    rows = out_grad.shape[0]
    width = w_t.shape[0] // 3
    heads = width // HEAD_DIM
    group, far = rows * n_h, n_h // 2
    shard = up_part.shape[1:]
    tall = -(-(5 + experts) // 8) * 8

    def pairs(*shape):
        return [DMA(shape), DMA(shape)]

    return pl.pallas_call(
        partial(back_body, n_e, n_h, experts, capacity, padded, heads),
        name="back",
        out_shape=[
            shape_of(y_out.shape, BF),
            shape_of((n_h, rows, model), BF),
            shape_of((rows, model), F32),
            shape_of((4 * width, model), BF),
            shape_of((tall, model), F32),
            shape_of((2, *shard), F32),
        ],
        in_specs=[SMEM] + [VMEM] * 12 + [ANY] * 12,
        out_specs=[ANY] * 2 + [VMEM] * 4,
        scratch_shapes=[
            pltpu.VMEM((experts * capacity, model), BF),
            pltpu.VMEM((rows, model), BF),
            pltpu.VMEM((rows, model), F32),
            pltpu.VMEM((n_h, rows, model), BF),
            pltpu.VMEM((3 * width, group), BF),
            pltpu.VMEM((n_h, width, rows), BF),
            pltpu.VMEM((n_h, width, rows), BF),
            pltpu.VMEM((n_h, width, model), BF),
            pltpu.VMEM((3 * width, model), BF),
            pltpu.VMEM((n_h, width, rows), BF),
            pltpu.VMEM((n_h, width, rows), BF),
            pltpu.VMEM((n_h - 1, width, model), BF),
            pltpu.VMEM((heads, group, HEAD_DIM), BF),
            pltpu.VMEM((heads, group, HEAD_DIM), BF),
            pltpu.VMEM((8, group), F32),
            pltpu.VMEM((width, group), F32),
            pltpu.VMEM((width, BLOCK), F32),
            pltpu.VMEM((width, BLOCK), F32),
            pltpu.VMEM((3 * width, group), BF),
            pltpu.VMEM((3 * width, model), F32),
            pltpu.VMEM((2, far, *shard), BF),
            pltpu.VMEM((2, far, *shard), BF),
            pltpu.VMEM((2, far - 1, *shard), BF),
            DMA((9,)),
            DMA,
            DMA((2, far)),
            DMA,
            *pairs(n_e),
            *pairs(n_h),
            *pairs(n_h),
            *pairs(2, far),
            *pairs(2, far),
        ],
        compiler_params=pltpu.CompilerParams(
            collective_id=cid, has_side_effects=True, vmem_limit_bytes=60 << 20
        ),
    )(
        docs,
        ids,
        slot,
        pos,
        gates,
        count,
        g1,
        s1,
        g2,
        s2,
        w_router,
        lse,
        dg_rows,
        dx_back.reshape(experts * capacity, model),
        y_out,
        up_part,
        down_part,
        out_grad,
        residual,
        all_tokens,
        qkv,
        att,
        att_t,
        w_out.reshape(n_h, width, model),
        w_t,
    )


def shards(
    tokens,
    doc_lengths,
    expert_ids,
    gain_one,
    shift_one,
    w_query,
    w_key,
    w_value,
    w_out,
    gain_two,
    shift_two,
    w_router,
    w_up,
    w_down,
    out_grad,
):
    rows, model = tokens.shape
    n_expert, n_hidden = lax.axis_size("expert"), lax.axis_size("hidden")
    experts = n_expert * w_up.shape[0]
    capacity = max(2, rows * 2 * 5 // (4 * experts))
    capacity = -(-capacity // 16) * 16
    total = experts * capacity
    heads = HEADS // n_hidden
    width = heads * HEAD_DIM
    g1, s1 = gain_one.reshape(1, model), shift_one.reshape(1, model)
    g2, s2 = gain_two.reshape(1, model), shift_two.reshape(1, model)

    (
        all_tokens,
        qkv,
        att,
        att_t,
        w_t,
        g_in,
        x_slots,
        ups,
        downs,
        pos,
        slot,
        count,
        lse,
        residual,
        gates,
        gate_rows,
    ) = run_front(
        doc_lengths,
        expert_ids,
        g1,
        s1,
        g2,
        s2,
        w_router,
        tokens,
        out_grad,
        (w_query, w_key, w_value, w_out),
        w_up,
        w_down,
        capacity,
        heads,
        1,
    )
    dx_back, dg_back, y_out, up_part, down_part = run_experts(
        x_slots, gate_rows, g_in, ups, downs, 2
    )
    y_back, d_hidden, d_res, w_all, small, dw_own = run_back(
        doc_lengths,
        expert_ids,
        slot,
        pos,
        gates,
        count,
        g1,
        s1,
        g2,
        s2,
        w_router,
        lse,
        dg_back,
        dx_back,
        y_out,
        up_part,
        down_part,
        out_grad,
        residual,
        all_tokens,
        qkv,
        att,
        att_t,
        w_out,
        w_t,
        3,
    )
    input_grad, output, full, small = run_tail(
        d_hidden,
        w_all.reshape(n_expert, 4 * width // n_expert, model),
        small,
        tokens,
        g1,
        d_res,
        residual,
        gates,
        pos,
        y_back.reshape(total, model),
        4,
    )
    *w_grads, up_grad, down_grad = turn_weights(
        full.reshape(n_hidden, 4 * width, model), dw_own, width, experts // 2
    )
    load = small[4, :experts] * experts / (rows * n_expert * n_hidden * 2)
    return (
        output,
        input_grad,
        small[0],
        small[1],
        *w_grads,
        small[2],
        small[3],
        small[5 : 5 + experts].T,
        up_grad[None],
        down_grad[None],
        load,
    )


def solution(mesh):
    in_specs = (
        P(("expert", "hidden"), None),
        P("expert", None),
        P(("expert", "hidden"), None),
        P(),
        P(),
        P(),
        P(),
        P(),
        P(),
        P(),
        P(),
        P(),
        P("expert", None, "hidden"),
        P("expert", "hidden", None),
        P(("expert", "hidden"), None),
    )
    out_specs = (
        P(("expert", "hidden"), None),
        P(("expert", "hidden"), None),
        P(),
        P(),
        P(),
        P(),
        P(),
        P(),
        P(),
        P(),
        P(),
        P("expert", None, "hidden"),
        P("expert", "hidden", None),
        P(),
    )
    return jax.shard_map(shards, mesh=mesh, in_specs=in_specs, out_specs=out_specs, check_vma=False)
```

time: 427 us -> 385 us (0.902)
  starting transfers between devices: 17.7 us -> 0 us
  between operations: 14 us -> 0.7 us
  other arithmetic: 10.2 us -> 1.19 us
  waiting for transfers between devices: 7.78 us -> 0 us
    all_to_all x2 -> x0, starting transfers between devices: 17.6 us -> none  [the longest x1 11.9 us: shards(): lax.all_to_all(y_out, 'expert', split_axis=0, concat_axis=0, tiled=True)]
    all_gather x2 -> x0, waiting for transfers between devices: 6.52 us -> none  [the longest x1 6.5 us: shards(): downs = lax.all_gather(down_src, 'hidden', axis=0, tiled=True)]
    pallas_call x1, Pallas kernels: 79.5 us -> 85.8 us  [run_tail(): pl.pallas_call(partial(tail_body, n_e, n_h, chunks), name='tail', out_sha...]
    mul x2 -> x0, other arithmetic: 4.41 us -> none  [the longest x1 2.98 us: shards(): up_grad = up_grad.astype(F32) * trainable]
    unnamed x44 -> x14, local copies, waits for them, and re-layouts: 9.53 us -> 7.17 us
    pallas_call x10 -> x3, Pallas kernels: 192 us -> 190 us  [the longest x1 97.3 us: run_front(): pl.pallas_call(partial(front_body, n_e, n_h, experts, capacity, padded, h...]
  transfers between devices with their start and end apart: 6 -> 0, of which waited for: 1 -> 0; matrix products, arithmetic and copies ran while one was open for 4% -> 0% of each run, Pallas kernels for 57% -> 0%
where the time goes in v3:
time: 385 us; the launch traced here: 383 us
  Pallas kernels  366 us (95%)
  local copies, waits for them, and re-layouts  15.2 us (4%)
    pallas_call x1, Pallas kernels, run_front(): pl.pallas_call(partial(front_body, n_e, n_h, experts, capacity, padded, h...  97.3 us
    pallas_call x1, Pallas kernels, run_experts(): pl.pallas_call(partial(moe_body, size, capacity, padded, per), name='expe...  89.7 us
    pallas_call x1, Pallas kernels, run_back(): pl.pallas_call(partial(back_body, n_e, n_h, experts, capacity, padded, he...  87 us
    pallas_call x1, Pallas kernels, run_tail(): pl.pallas_call(partial(tail_body, n_e, n_h, chunks), name='tail', out_sha...  85.8 us

profile of v3, /device:TPU:17, one launch (start us, length us, event | category | flops | bytes accessed | tf_op | source)
XLA Modules:
  0.0 382.8 jit_solution(17577229683776096441)
XLA Ops:
  0.6 1.3 reshape.57.g1.gain
  1.9 1.3 reshape.58.s1
  3.2 1.3 reshape.59.g2
  4.4 1.3 reshape.60.s2
  5.7 1.5 copy.30.w_router
  7.2 1.5 copy.31.ids
  8.8 97.3 %front.1 = (bf16[4,512,768]{2,1,0:T(8,128)(2,1)}, bf16[576,2048]{1,0:T(8,128)(2,1)}, bf16[4,192,512]{2,1,0:T(8,128)(2,1)}, bf16[4,192,512]{2,1,0:T(8,128)(2,1)},...) custom-call(s32[1,3]{1,0:T(1,128)} %docs.3, ...), custom_call_target="tpu_custom_call" | custom-call | tf_op jit(solution)/shard_map/front/pallas_call | solution.py:513
  106.1 89.7 %experts.1 = (bf16[8,160,768]{2,1,0:T(8,128)(2,1)}, f32[8,8,256]{2,1,0:T(8,128)}, bf16[8,160,768]{2,1,0:T(8,128)(2,1)}, bf16[4,768,768]{2,1,0:T(8,128)(2,1)}, bf16[4,768,768]{2,1,0:T(8,128)(2,1)}) custom-call(bf16[8,160,768]{2,1,0:T(8,128)(2,1)} %get-tuple-element.56.x_slots, f32[8,8,256]{2,1,0:T(8,128)} %get-tuple-element.57.gate_rows, ...), custom_call_target="tpu_custom_call" | custom-call | flops 36238786560 | bytes 41943040 | tf_op jit(solution)/shard_map/experts/pallas_call | solution.py:785
  195.9 87.0 %back.1 = (bf16[8,160,768]{2,1,0:T(8,128)(2,1)}, bf16[4,512,768]{2,1,0:T(8,128)(2,1)}, f32[512,768]{1,0:T(8,128)}, bf16[768,768]{1,0:T(8,128)(2,1)}, f32[16,768]{1,0:T(8,128)}, /*index=5*/f32[2,768,768]{2,1,0:T(8,128)}) custom-call(s32[1,3]{1,0:T(1,128)} %docs.3, s32[512,2]{1,0:T(8,128)} %copy.31.ids, s32[512,2]{1,0:T(8,128)} %get-tuple-element.51.slot, ...), custom_call_target="tpu_custom_call" | custom-call | tf_op jit(solution)/shard_map/back/pallas_call | solution.py:1553
  282.8 0.0 slice-start
  282.9 0.0 slice-start.1
  282.9 85.8 %tail.1 = (bf16[512,768]{1,0:T(8,128)(2,1)}, bf16[512,768]{1,0:T(8,128)(2,1)}, bf16[4,8,96,768]{3,2,1,0:T(8,128)(2,1)}, f32[16,768]{1,0:T(8,128)}) custom-call(bf16[4,512,768]{2,1,0:T(8,128)(2,1)} %get-tuple-element.72.dh, bf16[8,96,768]{2,1,0:T(8,128)(2,1)} %bitcast.18, f32[16,768]{1,0:T(8,128)} %get-tuple-element.74.small, bf16[512,768]{1,0:T(8,128)(2,1)} %tokens.3, ...), custom_call_target="tpu_custom_call" | custom-call | tf_op jit(solution)/shard_map/tail/pallas_call | solution.py:1084
  368.7 1.2 multiply_bitcast_fusion
  369.9 1.5 slice_reduce_fusion
  371.4 1.4 slice_bitcast_fusion
  372.8 0.0 slice-done
  372.8 0.0 slice-done.1
  372.8 0.0 copy-start
  372.8 2.3 copy-done
  375.1 0.0 copy-start.2
  375.1 0.0 copy-start.1
  375.1 5.9 %turn_weights.1 = (f32[768,768]{1,0:T(8,128)}, f32[768,768]{1,0:T(8,128)}, f32[768,768]{1,0:T(8,128)}, f32[768,768]{1,0:T(8,128)}, f32[768,768]{1,0:T(8,128)}, /*index=5*/f32[768,768]{1,0:T(8,128)}) custom-call(bf16[4,768,768]{2,1,0:T(8,128)(2,1)S(1)} %bitcast.14, f32[2,768,768]{2,1,0:T(8,128)S(1)} %bitcast.13), custom_call_target="tpu_custom_call" | custom-call | bytes 25165824 | tf_op jit(solution)/shard_map/turn_weights/pallas_call | solution.py:1149
  381.0 0.0 copy-done.2
  381.0 0.9 copy.35
  381.9 0.0 copy-done.1
  381.9 0.9 copy.36
  (1 shorter events, 0.0 us)
Async XLA Ops:
  282.8 89.9 %slice-start = ((s8[4718592]{0:T(1024)(128)(4,1)}), s8[4194304]{0:T(1024)(128)(4,1)S(1)}, s32[]{:S(2)}) async-start(s8[4718592]{0:T(1024)(128)(4,1)} %bitcast.12), calls=%async_computation | async-start | bytes 8388608
  282.9 89.9 %slice-start.1 = ((s8[4718592]{0:T(1024)(128)(4,1)}), s8[524288]{0:T(1024)(128)(4,1)S(1)}, s32[]{:S(2)}) async-start(s8[4718592]{0:T(1024)(128)(4,1)} %bitcast.12), calls=%async_computation.1 | async-start | bytes 1048576
  372.8 2.3 copy-start
  375.1 5.9 %copy-start.2 = (bf16[512,768]{1,0:T(8,128)(2,1)S(1)}, bf16[512,768]{1,0:T(8,128)(2,1)}, u32[]{:S(2)}) copy-start(bf16[512,768]{1,0:T(8,128)(2,1)} %get-tuple-element.106) | copy-start | bytes 2359300
  375.1 6.7 %copy-start.1 = (bf16[512,768]{1,0:T(8,128)(2,1)S(1)}, bf16[512,768]{1,0:T(8,128)(2,1)}, u32[]{:S(2)}) copy-start(bf16[512,768]{1,0:T(8,128)(2,1)} %get-tuple-element.107) | copy-start | bytes 2359300
